TPU v7x, 32 devices: a whole 2x2x4 slice. The times are simulated.
32 devices in a mesh: row: 8 (over z, x), col: 4 (over y, core).
Axes of the slice: x: 2, y: 2, z: 4, core: 2. Of those that a mesh axis runs over, the one named last changes fastest.
Arguments:
- positions: float32 [3, 32, 16, 256], P(None, 'row', 'col'), may hold values from 0 to 1
- masses: float32 [32, 16, 256], P('row', 'col'), may hold values from 0.002 to 0.02
- counts: int32 [32, 16, 4], P('row', 'col'), may hold values from 1 to 64, as said below
- multipoles: float32 [32, 16, 224], P('row', 'col'), may hold values from -6 to 6
- parent_local: float32 [16, 8, 112], P('row', 'col'), may hold values from -6 to 6
- m2l_ops: float32 [343, 3136], replicated, may hold values from -0.0625 to 0.0625
- l2l_ops: float32 [8, 56, 56], replicated, may hold values from -0.75 to 0.75
- check_to_equiv: float32 [56, 56], replicated, may hold values from -0.1875 to 0.1875
Outputs:
- potential: float32 [32, 16, 256], P('row', 'col')
- local_densities: float32 [32, 16, 224], P('row', 'col')
Inputs may be any that keep to these rules, and one draw needn't show every extreme that they name: Occupancy is clustered: leaves' counts vary strongly between regions of the box.
All inputs are finite; a program needn't handle non-finite values.
Results may differ from a plain program's by a relative error of at most 0.0003.
Values sent between devices are 32-bit elements; how exact they have to be, the bound alone decides.
No kernel may reach another device: no remote copies, remote signals or barrier semaphores. Data moves between devices by JAX's collectives and lax.ppermute only.
A program may use at most 128 MiB of HBM per device.

v0:
```python
import jax
import jax.numpy as jnp
import numpy as np
from jax import lax
from jax.sharding import PartitionSpec as P

CAP = 64
P_SIZE = 4
Q = 56


SOFTEN = 0.05


def padded_2(block, sides, width):
    for axis, dim in sides:
        count = lax.axis_size(axis)
        forward = [(i, i + 1) for i in range(count - 1)]
        backward = [(target, source) for source, target in forward]
        low = lax.ppermute(
            lax.slice_in_dim(block, block.shape[dim] - width, None, axis=dim), axis, forward
        )
        high = lax.ppermute(lax.slice_in_dim(block, 0, width, axis=dim), axis, backward)
        block = jnp.concatenate([low, block, high], axis=dim)
    return block


def surface_points():
    steps_grid = np.stack(
        np.meshgrid(np.arange(P_SIZE), np.arange(P_SIZE), np.arange(P_SIZE), indexing="ij"), -1
    ).reshape(-1, 3)
    on_face = np.any((steps_grid == 0) | (steps_grid == P_SIZE - 1), axis=1)
    chosen = steps_grid[on_face] / (P_SIZE - 1)
    return jnp.asarray(0.5 + 1.4 * (chosen - 0.5), jnp.float32)


def admits(shift, parity):
    return (shift >= -2 - parity) & (shift <= 3 - parity)


def admitted(shift_x, shift_y, shift_z, parity_x, parity_y, parity_z):
    distant = jnp.maximum(jnp.maximum(jnp.abs(shift_x), jnp.abs(shift_y)), jnp.abs(shift_z)) >= 2
    return (
        admits(shift_x, parity_x) & admits(shift_y, parity_y) & admits(shift_z, parity_z) & distant
    )


def downward(m2l_check, parent_local, l2l_ops, check_to_equiv):
    parent_x, parent_y, parent_width = parent_local.shape
    parent_z = parent_width // Q
    parents = parent_local.reshape(parent_x, parent_y, parent_z, Q)
    spread = jnp.einsum("xyzq,oqr->xyzor", parents, l2l_ops, precision=lax.Precision.HIGHEST)
    spread = spread.reshape(parent_x, parent_y, parent_z, 2, 2, 2, Q).transpose(0, 3, 1, 4, 2, 5, 6)
    spread = spread.reshape(2 * parent_x, 2 * parent_y, 2 * parent_z, Q)
    check_field = m2l_check + spread
    return jnp.einsum("xyzq,qr->xyzr", check_field, check_to_equiv, precision=lax.Precision.HIGHEST)


def near_field(targets, padded):
    size_x, size_y, size_z, slot_count = targets.shape[1:]
    summed = jnp.zeros((size_x, size_y, size_z, slot_count), jnp.float32)
    for shift_x in (-1, 0, 1):
        for shift_y in (-1, 0, 1):
            for shift_z in (-1, 0, 1):
                sources = padded[
                    :,
                    1 + shift_x : 1 + shift_x + size_x,
                    1 + shift_y : 1 + shift_y + size_y,
                    1 + shift_z : 1 + shift_z + size_z,
                    :,
                ]
                distance = (
                    jnp.zeros((size_x, size_y, size_z, slot_count, slot_count), jnp.float32)
                    + SOFTEN * SOFTEN
                )
                for comp, shift in enumerate((shift_x, shift_y, shift_z)):
                    gap = targets[comp][..., :, None] - (sources[comp][..., None, :] + float(shift))
                    distance = distance + gap * gap
                summed = summed + jnp.sum(sources[3][..., None, :] * lax.rsqrt(distance), axis=-1)
    return summed


def far_field(targets, local_field, points):
    distance = jnp.zeros(targets.shape[1:] + (points.shape[0],), jnp.float32)
    for comp in range(3):
        gap = targets[comp][..., None] - points[:, comp]
        distance = distance + gap * gap
    return jnp.einsum(
        "xyzcq,xyzq->xyzc", lax.rsqrt(distance), local_field, precision=lax.Precision.HIGHEST
    )


def m2l_block(rimmed_poles, m2l_ops, size_x, size_y, size_z):
    grid_cells = rimmed_poles.reshape(size_x + 6, size_y + 6, size_z, Q)
    padded = jnp.pad(grid_cells, ((0, 0), (0, 0), (3, 3), (0, 0)))
    parity_x = (jnp.arange(size_x, dtype=jnp.int32) % 2)[:, None, None]
    parity_y = (jnp.arange(size_y, dtype=jnp.int32) % 2)[None, :, None]
    parity_z = (jnp.arange(size_z, dtype=jnp.int32) % 2)[None, None, :]
    pieces = []
    for shift_x in range(-3, 4):
        for shift_y in range(-3, 4):
            for shift_z in range(-3, 4):
                sources = padded[
                    3 + shift_x : 3 + shift_x + size_x,
                    3 + shift_y : 3 + shift_y + size_y,
                    3 + shift_z : 3 + shift_z + size_z,
                    :,
                ]
                weights = admitted(
                    jnp.int32(shift_x),
                    jnp.int32(shift_y),
                    jnp.int32(shift_z),
                    parity_x,
                    parity_y,
                    parity_z,
                )
                pieces.append(sources * weights.astype(jnp.float32)[..., None])
    stacked = jnp.concatenate(pieces, axis=-1).reshape(size_x * size_y * size_z, 343 * Q)
    check_field = jnp.dot(
        stacked,
        m2l_ops.reshape(343 * Q, Q),
        precision=lax.Precision.HIGHEST,
        preferred_element_type=jnp.float32,
    )
    return check_field.reshape(size_x, size_y, size_z, Q)


def body(positions, masses, counts, multipoles, parent_local, m2l_ops, l2l_ops, check_to_equiv):
    size_x, size_y, slot_width = masses.shape
    size_z = slot_width // CAP
    slot_index = jnp.arange(CAP, dtype=jnp.int32)
    alive_mask = (slot_index < counts[..., None]).astype(jnp.float32)
    targets = positions.reshape(3, size_x, size_y, size_z, CAP)
    weighed = masses.reshape(size_x, size_y, size_z, CAP) * alive_mask
    packed = jnp.concatenate([positions, weighed.reshape(1, size_x, size_y, slot_width)], 0)
    rimmed_poles = padded_2(multipoles, (("row", 0), ("col", 1)), 3)
    rimmed = padded_2(packed, (("row", 1), ("col", 2)), 1)
    m2l_check = m2l_block(rimmed_poles, m2l_ops, size_x, size_y, size_z)
    local_field = downward(m2l_check, parent_local, l2l_ops, check_to_equiv)
    padded = rimmed.reshape(4, size_x + 2, size_y + 2, size_z, CAP)
    padded = jnp.pad(padded, ((0, 0), (0, 0), (0, 0), (1, 1), (0, 0)))
    points = surface_points()
    potential = (near_field(targets, padded) + far_field(targets, local_field, points)) * alive_mask
    return (
        potential.reshape(size_x, size_y, slot_width),
        local_field.reshape(size_x, size_y, size_z * Q),
    )


def solution(mesh):
    return jax.shard_map(
        body,
        mesh=mesh,
        in_specs=(
            P(None, "row", "col", None),
            P("row", "col", None),
            P("row", "col", None),
            P("row", "col", None),
            P("row", "col", None),
            P(),
            P(),
            P(),
        ),
        out_specs=(P("row", "col", None), P("row", "col", None)),
        check_vma=False,
    )
```

profile of v0, /device:TPU:19, one launch (start us, length us, event | category | flops | bytes accessed | tf_op | source)
XLA Modules:
  0.0 172.6 jit_solution(9666406061611697917)
XLA Ops:
  1.4 3.2 %collective-permute-start.4 = (f32[3,4,224]{2,1,0:T(4,128)S(1)}, f32[3,4,224]{2,1,0:T(4,128)S(1)}, u32[]{:S(2)}, u32[]{:S(2)}) collective-permute-start(f32[3,4,224]{2,1,0:T(4,128)S(1)} %get-tuple-element.490), channel_id=1, source_target_pairs={{0,4},{4,8},{8,12},{12,16},{16,20},{20,24},{24,28},{1,5},{5,9},{9,... | collective-permute-start | bytes 32264 | tf_op jit(solution)/shard_map/ppermute | solution.py:20
  4.6 2.1 %collective-permute-start.5 = (f32[3,4,224]{2,1,0:T(4,128)S(1)}, f32[3,4,224]{2,1,0:T(4,128)S(1)}, u32[]{:S(2)}, u32[]{:S(2)}) collective-permute-start(f32[3,4,224]{2,1,0:T(4,128)S(1)} %get-tuple-element.489), channel_id=1, source_target_pairs={{4,0},{8,4},{12,8},{16,12},{20,16},{24,20},{28,24},{5,1},{9,5},{13... | collective-permute-start | bytes 32264 | tf_op jit(solution)/shard_map/ppermute | solution.py:23
  9.1 4.1 %collective-permute-start = (f32[4,1,4,256]{3,2,1,0:T(4,128)S(1)}, f32[4,1,4,256]{3,2,1,0:T(4,128)S(1)}, u32[]{:S(2)}, u32[]{:S(2)}) collective-permute-start(f32[4,1,4,256]{3,2,1,0:T(4,128)S(1)} %get-tuple-element.482), channel_id=1, source_target_pairs={{0,4},{4,8},{8,12},{12,16},{16,20},{20,24},{24,28},{1,5},{5,9},{9,... | collective-permute-start | bytes 49160 | tf_op jit(solution)/shard_map/ppermute | solution.py:20
  13.2 1.9 %collective-permute-start.1 = (f32[4,1,4,256]{3,2,1,0:T(4,128)S(1)}, f32[4,1,4,256]{3,2,1,0:T(4,128)S(1)}, u32[]{:S(2)}, u32[]{:S(2)}) collective-permute-start(f32[4,1,4,256]{3,2,1,0:T(4,128)S(1)} %get-tuple-element.483), channel_id=1, source_target_pairs={{4,0},{8,4},{12,8},{16,12},{20,16},{24,20},{28,24},{5,1},{9,5},{13... | collective-permute-start | bytes 49160 | tf_op jit(solution)/shard_map/ppermute | solution.py:23
  17.1 1.1 and_convert_fusion.87
  18.3 1.1 and_convert_fusion.112
  19.4 1.2 and_convert_fusion.192
  20.6 1.2 and_convert_fusion.138
  22.6 8.8 %reshape.2830 = f32[19208,56]{1,0:T(8,128)} reshape(f32[343,3136]{1,0:T(8,128)} %param.14) | data formatting | bytes 8605184 | tf_op jit(solution)/shard_map/reshape | solution.py:121
  34.1 4.5 %collective-permute-start.6 = (f32[10,3,224]{2,1,0:T(4,128)S(1)}, f32[10,3,224]{2,1,0:T(4,128)S(1)}, u32[]{:S(2)}, u32[]{:S(2)}) collective-permute-start(f32[10,3,224]{2,1,0:T(4,128)S(1)} %get-tuple-element.487), channel_id=1, source_target_pairs={{0,1},{1,2},{2,3},{4,5},{5,6},{6,7},{8,9},{9,10},{10,11},{12,13},{... | collective-permute-start | bytes 80648 | tf_op jit(solution)/shard_map/ppermute | solution.py:20
  38.7 1.9 %collective-permute-start.7 = (f32[10,3,224]{2,1,0:T(4,128)S(1)}, f32[10,3,224]{2,1,0:T(4,128)S(1)}, u32[]{:S(2)}, u32[]{:S(2)}) collective-permute-start(f32[10,3,224]{2,1,0:T(4,128)S(1)} %get-tuple-element.488), channel_id=1, source_target_pairs={{1,0},{2,1},{3,2},{5,4},{6,5},{7,6},{9,8},{10,9},{11,10},{13,12},{... | collective-permute-start | bytes 80648 | tf_op jit(solution)/shard_map/ppermute | solution.py:23
  41.3 3.6 %collective-permute-start.2 = (f32[4,6,1,256]{3,2,1,0:T(1,128)}, f32[4,6,1,256]{3,2,1,0:T(1,128)}, u32[]{:S(2)}, u32[]{:S(2)}) collective-permute-start(f32[4,6,1,256]{3,2,1,0:T(1,128)} %get-tuple-element.480), channel_id=1, source_target_pairs={{0,1},{1,2},{2,3},{4,5},{5,6},{6,7},{8,9},{9,10},{10,11},{12,13},{... | collective-permute-start | bytes 73736 | tf_op jit(solution)/shard_map/ppermute | solution.py:20
  45.0 2.1 %collective-permute-start.3 = (f32[4,6,1,256]{3,2,1,0:T(1,128)}, f32[4,6,1,256]{3,2,1,0:T(1,128)}, u32[]{:S(2)}, u32[]{:S(2)}) collective-permute-start(f32[4,6,1,256]{3,2,1,0:T(1,128)} %get-tuple-element.481), channel_id=1, source_target_pairs={{1,0},{2,1},{3,2},{5,4},{6,5},{7,6},{9,8},{10,9},{11,10},{13,12},{... | collective-permute-start | bytes 73736 | tf_op jit(solution)/shard_map/ppermute | solution.py:23
  48.8 1.7 fusion.221
  53.4 1.8 %slice_multiply_fusion.39 = (f32[4,4,4,56]{3,2,1,0:T(4,128)}, f32[4,4,4,56]{3,2,1,0:T(4,128)}, f32[4,4,4,56]{3,2,1,0:T(4,128)}, f32[4,4,4,56]{3,2,1,0:T(4,128)},...) fusion(f32[10,10,4,56]{3,2,1,0:T(4,128)S(1)} %reshape.2829, ...), kind=kLoop, calls=%fused_computation.862 | loop fusion | flops 32256 | bytes 260352 | tf_op jit(solution)/shard_map/mul | solution.py:117
  55.2 1.6 slice_multiply_fusion.14
  58.8 1.6 slice_multiply_fusion.12
  72.2 1.7 fusion.343
  73.9 1.8 %fusion.348 = (f32[4,4,4,56]{3,2,1,0:T(4,128)}, f32[4,4,4,56]{3,2,1,0:T(4,128)}, f32[4,4,4,56]{3,2,1,0:T(4,128)}, f32[4,4,4,56]{3,2,1,0:T(4,128)}, f32[4,4,4,56]...) fusion(f32[10,10,4,56]{3,2,1,0:T(4,128)S(1)} %reshape.2829, ...), kind=kLoop, calls=%fused_computation.741 | loop fusion | flops 35840 | bytes 235264 | tf_op jit(solution)/shard_map/mul | solution.py:117
  75.7 1.7 fusion.347
  77.4 1.7 fusion.346
  84.0 4.7 %concatenate.25 = f32[4,4,4,4872]{3,2,1,0:T(4,128)S(1)} concatenate(f32[4,4,4,56]{3,2,1,0:T(4,128)} %get-tuple-element.141, f32[4,4,4,56]{3,2,1,0:T(4,128)} %get-tuple-element.142, f32[4,4,4,56]{3,2,1,0:T(4,128)} %get-tuple-element.143, f32[4,4,4,56]{3,2,1,0:T(4,128)} %get-tuple-element.144, f32[4,4,4,56]{3,2,1,0:T(4,128)} %get-tuple-element.145, ...), dimensions={3} | concatenate | bytes 2494464
  88.7 17.2 %concatenate.24 = f32[4,4,4,14336]{3,2,1,0:T(4,128)} concatenate(f32[4,4,4,56]{3,2,1,0:T(4,128)S(1)} %get-tuple-element.896, f32[4,4,4,56]{3,2,1,0:T(4,128)} %get-tuple-element.383, f32[4,4,4,56]{3,2,1,0:T(4,128)} %get-tuple-element.384, f32[4,4,4,56]{3,2,1,0:T(4,128)S(1)} %get-tuple-element.897, f32[4,4,4,56]{3,2,1,0:T(4,128)} %get-tuple-element.385, ...), dimensions={3} | concatenate | bytes 7340032
  106.0 14.0 %fusion.11 = f32[4,4,4,56]{3,2,1,0:T(4,128)S(1)} fusion(f32[4,4,4,56]{3,2,1,0:T(4,128)} %bitcast.250, f32[19208,56]{1,0:T(8,128)} %reshape.2830, f32[4,4,4,4872]{3,2,1,0:T(4,128)S(1)} %concatenate.25, f32[4,4,4,14336]{3,2,1,0:T(4,128)} %concatenate.24), kind=kOutput, calls=%fused_computation.406 | convolution fusion | flops 827330560 | bytes 9248512 | tf_op jit(solution)/shard_map/dot_general | solution.py:119
  120.2 5.1 %fusion.7 = f32[4,4,4,1,64]{4,3,2,1,0:T(1,128)S(1)} fusion(f32[4,4,4,56,1]{3,4,2,1,0:T(1,128)S(1)} %bitcast.251, f32[56]{0:T(128)S(1)} %copy-done.108, f32[56]{0:T(128)S(1)} %copy-done.107, f32[56]{0:T(128)S(1)} %copy-done.106, f32[4,4,4,64]{3,2,1,0:T(4,128)S(1)} %copy-done.100, f32[4,4,4,64]{3,2,1,0:T(4,128)S(1)} %copy-done.99, ...), kind=kOutput, calls=%fused_computation.374 | convolution fusion | flops 4587520 | bytes 80544 | tf_op jit(solution)/shard_map/xyzcq,xyzq->xyzc/dot_general | solution.py:88
  128.0 4.9 %multiply_reduce_fusion.2 = (f32[4,4,4,64]{3,2,1,0:T(4,128)S(1)}, f32[4,4,4,64]{3,2,1,0:T(4,128)S(1)}, f32[4,4,4,64]{3,2,1,0:T(4,128)S(1)}) fusion(f32[4,4,4,64]{3,2,1,0:T(4,128)S(1)} %get-tuple-element.99, f32[4,4,4,64]{3,2,1,0:T(4,128)S(1)} %get-tuple-element.98, f32[4,4,4,64]{3,2,1,0:T(4,128)S(1)} %get-tuple-element.97, ...), kind=kLoop, calls=%fused_computation.380 | loop fusion | flops 8638464 | bytes 294912 | tf_op jit(solution)/shard_map/reduce_sum | solution.py:79
  132.9 6.4 %multiply_reduce_fusion.10 = (f32[4,4,4,64]{3,2,1,0:T(4,128)S(1)}, f32[4,4,4,64]{3,2,1,0:T(4,128)S(1)}, f32[4,4,4,64]{3,2,1,0:T(4,128)S(1)}, f32[4,4,4,64]{3,2,1,0:T(4,128)S(1)}) fusion(f32[4,4,4,64]{3,2,1,0:T(4,128)S(1)} %get-tuple-element.117, f32[4,4,4,64]{3,2,1,0:T(4,128)S(1)} %get-tuple-element.118, f32[4,4,4,64]{3,2,1,0:T(4,128)S(1)} %get-tuple-element.119, ...), kind=kLoop, calls=%fused_computation.388 | loop fusion | flops 11517952 | bytes 376832 | tf_op jit(solution)/shard_map/reduce_sum | solution.py:79
  139.4 6.4 %multiply_reduce_fusion.6 = (f32[4,4,4,64]{3,2,1,0:T(4,128)S(1)}, f32[4,4,4,64]{3,2,1,0:T(4,128)S(1)}, f32[4,4,4,64]{3,2,1,0:T(4,128)S(1)}, f32[4,4,4,64]{3,2,1,0:T(4,128)S(1)}) fusion(f32[4,4,4,64]{3,2,1,0:T(4,128)S(1)} %get-tuple-element.87, f32[4,4,4,64]{3,2,1,0:T(4,128)S(1)} %get-tuple-element.85, f32[4,4,4,64]{3,2,1,0:T(4,128)S(1)} %get-tuple-element.84, ...), kind=kLoop, calls=%fused_computation.384 | loop fusion | flops 11517952 | bytes 376832 | tf_op jit(solution)/shard_map/reduce_sum | solution.py:79
  145.8 6.7 %multiply_reduce_fusion.14 = (f32[4,4,4,64]{3,2,1,0:T(4,128)S(1)}, f32[4,4,4,64]{3,2,1,0:T(4,128)S(1)}, f32[4,4,4,64]{3,2,1,0:T(4,128)S(1)}, f32[4,4,4,64]{3,2,1,0:T(4,128)S(1)}) fusion(f32[4,4,4,64]{3,2,1,0:T(4,128)S(1)} %get-tuple-element.65, f32[4,4,4,64]{3,2,1,0:T(4,128)S(1)} %get-tuple-element.64, f32[4,4,4,64]{3,2,1,0:T(4,128)S(1)} %get-tuple-element.63, ...), kind=kLoop, calls=%fused_computation.392 | loop fusion | flops 11517952 | bytes 376832 | tf_op jit(solution)/shard_map/reduce_sum | solution.py:79
  152.5 6.4 %multiply_reduce_fusion.25 = (f32[4,4,4,64]{3,2,1,0:T(4,128)S(1)}, f32[4,4,4,64]{3,2,1,0:T(4,128)S(1)}, f32[4,4,4,64]{3,2,1,0:T(4,128)S(1)}, f32[4,4,4,64]{3,2,1,0:T(4,128)S(1)}) fusion(f32[4,4,4,64]{3,2,1,0:T(4,128)S(1)} %get-tuple-element.134, f32[4,4,4,64]{3,2,1,0:T(4,128)S(1)} %get-tuple-element.135, f32[4,4,4,64]{3,2,1,0:T(4,128)S(1)} %get-tuple-element.124, ...), kind=kLoop, calls=%fused_computation.403 | loop fusion | flops 11517952 | bytes 376832 | tf_op jit(solution)/shard_map/reduce_sum | solution.py:79
  158.9 6.4 %multiply_reduce_fusion.18 = (f32[4,4,4,64]{3,2,1,0:T(4,128)S(1)}, f32[4,4,4,64]{3,2,1,0:T(4,128)S(1)}, f32[4,4,4,64]{3,2,1,0:T(4,128)S(1)}, f32[4,4,4,64]{3,2,1,0:T(4,128)S(1)}) fusion(f32[4,4,4,64]{3,2,1,0:T(4,128)S(1)} %get-tuple-element.53, f32[4,4,4,64]{3,2,1,0:T(4,128)S(1)} %get-tuple-element.52, f32[4,4,4,64]{3,2,1,0:T(4,128)S(1)} %get-tuple-element.51, ...), kind=kLoop, calls=%fused_computation.396 | loop fusion | flops 11517952 | bytes 376832 | tf_op jit(solution)/shard_map/reduce_sum | solution.py:79
  165.4 6.4 %multiply_reduce_fusion.26 = (f32[4,4,4,64]{3,2,1,0:T(4,128)S(1)}, f32[4,4,4,64]{3,2,1,0:T(4,128)S(1)}, f32[4,4,4,64]{3,2,1,0:T(4,128)S(1)}, f32[4,4,4,64]{3,2,1,0:T(4,128)S(1)}) fusion(f32[4,4,4,64]{3,2,1,0:T(4,128)S(1)} %get-tuple-element.32, f32[4,4,4,64]{3,2,1,0:T(4,128)S(1)} %copy-done.100, f32[4,4,4,64]{3,2,1,0:T(4,128)S(1)} %get-tuple-element.31, ...), kind=kLoop, calls=%fused_computation.404 | loop fusion | flops 11517952 | bytes 376832 | tf_op jit(solution)/shard_map/reduce_sum | solution.py:79
  (297 shorter events, 35.0 us)
Async XLA Ops:
  0.6 16.1 %copy-start = (f32[8,56,56]{2,1,0:T(8,128)S(1)}, f32[8,56,56]{2,1,0:T(8,128)}, u32[]{:S(2)}) copy-start(f32[8,56,56]{2,1,0:T(8,128)} %param.15) | copy-start | bytes 301060
  1.4 32.6 %collective-permute-start.4 = (f32[3,4,224]{2,1,0:T(4,128)S(1)}, f32[3,4,224]{2,1,0:T(4,128)S(1)}, u32[]{:S(2)}, u32[]{:S(2)}) collective-permute-start(f32[3,4,224]{2,1,0:T(4,128)S(1)} %get-tuple-element.490), channel_id=1, source_target_pairs={{0,4},{4,8},{8,12},{12,16},{16,20},{20,24},{24,28},{1,5},{5,9},{9,... | collective-permute-start | bytes 32264 | tf_op jit(solution)/shard_map/ppermute | solution.py:20
  4.6 29.5 %collective-permute-start.5 = (f32[3,4,224]{2,1,0:T(4,128)S(1)}, f32[3,4,224]{2,1,0:T(4,128)S(1)}, u32[]{:S(2)}, u32[]{:S(2)}) collective-permute-start(f32[3,4,224]{2,1,0:T(4,128)S(1)} %get-tuple-element.489), channel_id=1, source_target_pairs={{4,0},{8,4},{12,8},{16,12},{20,16},{24,20},{28,24},{5,1},{9,5},{13... | collective-permute-start | bytes 32264 | tf_op jit(solution)/shard_map/ppermute | solution.py:23
  9.1 31.5 %collective-permute-start = (f32[4,1,4,256]{3,2,1,0:T(4,128)S(1)}, f32[4,1,4,256]{3,2,1,0:T(4,128)S(1)}, u32[]{:S(2)}, u32[]{:S(2)}) collective-permute-start(f32[4,1,4,256]{3,2,1,0:T(4,128)S(1)} %get-tuple-element.482), channel_id=1, source_target_pairs={{0,4},{4,8},{8,12},{12,16},{16,20},{20,24},{24,28},{1,5},{5,9},{9,... | collective-permute-start | bytes 49160 | tf_op jit(solution)/shard_map/ppermute | solution.py:20
  13.2 27.4 %collective-permute-start.1 = (f32[4,1,4,256]{3,2,1,0:T(4,128)S(1)}, f32[4,1,4,256]{3,2,1,0:T(4,128)S(1)}, u32[]{:S(2)}, u32[]{:S(2)}) collective-permute-start(f32[4,1,4,256]{3,2,1,0:T(4,128)S(1)} %get-tuple-element.483), channel_id=1, source_target_pairs={{4,0},{8,4},{12,8},{16,12},{20,16},{24,20},{28,24},{5,1},{9,5},{13... | collective-permute-start | bytes 49160 | tf_op jit(solution)/shard_map/ppermute | solution.py:23
  22.6 11.5 %copy-start.2 = (f32[4,4,224]{2,1,0:T(4,128)S(1)}, f32[4,4,224]{2,1,0:T(4,128)}, u32[]{:S(2)}) copy-start(f32[4,4,224]{2,1,0:T(4,128)} %param.12) | copy-start | bytes 43012
  22.6 18.1 %copy-start.1 = (f32[3,4,4,256]{3,2,1,0:T(4,128)S(1)}, f32[3,4,4,256]{3,2,1,0:T(4,128)}, u32[]{:S(2)}) copy-start(f32[3,4,4,256]{3,2,1,0:T(4,128)} %param.9) | copy-start | bytes 147460
  34.1 12.9 %collective-permute-start.6 = (f32[10,3,224]{2,1,0:T(4,128)S(1)}, f32[10,3,224]{2,1,0:T(4,128)S(1)}, u32[]{:S(2)}, u32[]{:S(2)}) collective-permute-start(f32[10,3,224]{2,1,0:T(4,128)S(1)} %get-tuple-element.487), channel_id=1, source_target_pairs={{0,1},{1,2},{2,3},{4,5},{5,6},{6,7},{8,9},{9,10},{10,11},{12,13},{... | collective-permute-start | bytes 80648 | tf_op jit(solution)/shard_map/ppermute | solution.py:20
  38.7 8.4 %collective-permute-start.7 = (f32[10,3,224]{2,1,0:T(4,128)S(1)}, f32[10,3,224]{2,1,0:T(4,128)S(1)}, u32[]{:S(2)}, u32[]{:S(2)}) collective-permute-start(f32[10,3,224]{2,1,0:T(4,128)S(1)} %get-tuple-element.488), channel_id=1, source_target_pairs={{1,0},{2,1},{3,2},{5,4},{6,5},{7,6},{9,8},{10,9},{11,10},{13,12},{... | collective-permute-start | bytes 80648 | tf_op jit(solution)/shard_map/ppermute | solution.py:23
  41.3 84.7 %collective-permute-start.2 = (f32[4,6,1,256]{3,2,1,0:T(1,128)}, f32[4,6,1,256]{3,2,1,0:T(1,128)}, u32[]{:S(2)}, u32[]{:S(2)}) collective-permute-start(f32[4,6,1,256]{3,2,1,0:T(1,128)} %get-tuple-element.480), channel_id=1, source_target_pairs={{0,1},{1,2},{2,3},{4,5},{5,6},{6,7},{8,9},{9,10},{10,11},{12,13},{... | collective-permute-start | bytes 73736 | tf_op jit(solution)/shard_map/ppermute | solution.py:20
  45.0 81.1 %collective-permute-start.3 = (f32[4,6,1,256]{3,2,1,0:T(1,128)}, f32[4,6,1,256]{3,2,1,0:T(1,128)}, u32[]{:S(2)}, u32[]{:S(2)}) collective-permute-start(f32[4,6,1,256]{3,2,1,0:T(1,128)} %get-tuple-element.481), channel_id=1, source_target_pairs={{1,0},{2,1},{3,2},{5,4},{6,5},{7,6},{9,8},{10,9},{11,10},{13,12},{... | collective-permute-start | bytes 73736 | tf_op jit(solution)/shard_map/ppermute | solution.py:23
  69.1 10.0 %copy-start.75 = (f32[4,4,4]{2,1,0:T(4,128)S(1)}, f32[4,4,4]{2,1,0:T(4,128)}, u32[]{:S(2)}) copy-start(f32[4,4,4]{2,1,0:T(4,128)} %get-tuple-element.755) | copy-start | bytes 772
  69.1 10.0 %copy-start.76 = (f32[4,4,4]{2,1,0:T(4,128)S(1)}, f32[4,4,4]{2,1,0:T(4,128)}, u32[]{:S(2)}) copy-start(f32[4,4,4]{2,1,0:T(4,128)} %get-tuple-element.757) | copy-start | bytes 772
  69.1 10.0 %copy-start.77 = (f32[4,4,4]{2,1,0:T(4,128)S(1)}, f32[4,4,4]{2,1,0:T(4,128)}, u32[]{:S(2)}) copy-start(f32[4,4,4]{2,1,0:T(4,128)} %get-tuple-element.759) | copy-start | bytes 772
  69.1 10.0 %copy-start.78 = (f32[4,4,4]{2,1,0:T(4,128)S(1)}, f32[4,4,4]{2,1,0:T(4,128)}, u32[]{:S(2)}) copy-start(f32[4,4,4]{2,1,0:T(4,128)} %get-tuple-element.760) | copy-start | bytes 772
  69.1 10.0 %copy-start.79 = (f32[4,4,4]{2,1,0:T(4,128)S(1)}, f32[4,4,4]{2,1,0:T(4,128)}, u32[]{:S(2)}) copy-start(f32[4,4,4]{2,1,0:T(4,128)} %get-tuple-element.761) | copy-start | bytes 772
  69.1 10.0 %copy-start.80 = (f32[4,4,4]{2,1,0:T(4,128)S(1)}, f32[4,4,4]{2,1,0:T(4,128)}, u32[]{:S(2)}) copy-start(f32[4,4,4]{2,1,0:T(4,128)} %get-tuple-element.762) | copy-start | bytes 772
  69.1 10.0 %copy-start.81 = (f32[4,4,4]{2,1,0:T(4,128)S(1)}, f32[4,4,4]{2,1,0:T(4,128)}, u32[]{:S(2)}) copy-start(f32[4,4,4]{2,1,0:T(4,128)} %get-tuple-element.764) | copy-start | bytes 772
  69.2 10.0 %copy-start.82 = (f32[4,4,4]{2,1,0:T(4,128)S(1)}, f32[4,4,4]{2,1,0:T(4,128)}, u32[]{:S(2)}) copy-start(f32[4,4,4]{2,1,0:T(4,128)} %get-tuple-element.766) | copy-start | bytes 772
  70.1 10.0 %copy-start.70 = (f32[4,4,4]{2,1,0:T(4,128)S(1)}, f32[4,4,4]{2,1,0:T(4,128)}, u32[]{:S(2)}) copy-start(f32[4,4,4]{2,1,0:T(4,128)} %get-tuple-element.752) | copy-start | bytes 772
  70.1 10.0 %copy-start.71 = (f32[4,4,4]{2,1,0:T(4,128)S(1)}, f32[4,4,4]{2,1,0:T(4,128)}, u32[]{:S(2)}) copy-start(f32[4,4,4]{2,1,0:T(4,128)} %get-tuple-element.756) | copy-start | bytes 772
  70.1 10.0 %copy-start.72 = (f32[4,4,4]{2,1,0:T(4,128)S(1)}, f32[4,4,4]{2,1,0:T(4,128)}, u32[]{:S(2)}) copy-start(f32[4,4,4]{2,1,0:T(4,128)} %get-tuple-element.758) | copy-start | bytes 772
  70.1 10.0 %copy-start.73 = (f32[4,4,4]{2,1,0:T(4,128)S(1)}, f32[4,4,4]{2,1,0:T(4,128)}, u32[]{:S(2)}) copy-start(f32[4,4,4]{2,1,0:T(4,128)} %get-tuple-element.772) | copy-start | bytes 772
  70.2 10.0 %copy-start.74 = (f32[4,4,4]{2,1,0:T(4,128)S(1)}, f32[4,4,4]{2,1,0:T(4,128)}, u32[]{:S(2)}) copy-start(f32[4,4,4]{2,1,0:T(4,128)} %get-tuple-element.781) | copy-start | bytes 772
  105.9 14.0 %copy-start.105 = (f32[56,56]{1,0:T(8,128)S(1)}, f32[56,56]{1,0:T(8,128)}, u32[]{:S(2)}) copy-start(f32[56,56]{1,0:T(8,128)} %param.16) | copy-start | bytes 37636
  105.9 14.2 %copy-start.98 = (f32[4,4,4,64]{3,2,1,0:T(4,128)S(1)}, f32[4,4,4,64]{3,2,1,0:T(4,128)}, u32[]{:S(2)}) copy-start(f32[4,4,4,64]{3,2,1,0:T(4,128)} %sub.1816) | copy-start | bytes 49156
  105.9 14.2 %copy-start.99 = (f32[4,4,4,64]{3,2,1,0:T(4,128)S(1)}, f32[4,4,4,64]{3,2,1,0:T(4,128)}, u32[]{:S(2)}) copy-start(f32[4,4,4,64]{3,2,1,0:T(4,128)} %sub.1820) | copy-start | bytes 49156
  105.9 14.2 %copy-start.100 = (f32[4,4,4,64]{3,2,1,0:T(4,128)S(1)}, f32[4,4,4,64]{3,2,1,0:T(4,128)}, u32[]{:S(2)}) copy-start(f32[4,4,4,64]{3,2,1,0:T(4,128)} %sub.1824) | copy-start | bytes 49156
  105.9 14.2 %copy-start.106 = (f32[56]{0:T(128)S(1)}, f32[56]{0:T(128)}, u32[]{:S(2)}) copy-start(f32[56]{0:T(128)} %constant.84) | copy-start | bytes 676
  106.0 14.2 %copy-start.107 = (f32[56]{0:T(128)S(1)}, f32[56]{0:T(128)}, u32[]{:S(2)}) copy-start(f32[56]{0:T(128)} %constant.85) | copy-start | bytes 676
  106.0 14.2 %copy-start.108 = (f32[56]{0:T(128)S(1)}, f32[56]{0:T(128)}, u32[]{:S(2)}) copy-start(f32[56]{0:T(128)} %constant.86) | copy-start | bytes 676
  158.9 12.9 %copy-start.45 = (s32[4,4,4]{2,1,0:T(4,128)S(1)}, s32[4,4,4]{2,1,0:T(4,128)}, u32[]{:S(2)}) copy-start(s32[4,4,4]{2,1,0:T(4,128)} %param.11) | copy-start | bytes 772
  (85 other events, 668.0 us)
where the time goes:
time: 176 us; the launch traced here: 173 us
  other arithmetic  88.3 us (50%)
  local copies, waits for them, and re-layouts  39 us (22%)
  starting transfers between devices  23.5 us (13%)
  matrix products  19.5 us (11%)
  between operations  2.43 us (1%)
    reduce_sum x7, other arithmetic, near_field(): jnp.sum(sources[3][..., None, :] * lax.rsqrt(distance), axis=-1)  43.7 us
    mul x36, other arithmetic, m2l_block(): pieces.append(sources * weights.astype(jnp.float32)[..., None])  35 us
    unnamed x222, local copies, waits for them, and re-layouts  22.4 us
    ppermute x4, starting transfers between devices, padded_2(): lax.ppermute(lax.slice_in_dim(block, block.shape[dim] - width, None, axis...  15.4 us
    dot_general x1, matrix products, m2l_block(): jnp.dot(stacked, m2l_ops.reshape(343 * Q, Q), precision=lax.Precision.HIG...  14 us
    reshape x1, local copies, waits for them, and re-layouts, m2l_block(): m2l_ops.reshape(343 * Q, Q)  8.8 us
    ppermute x4, starting transfers between devices, padded_2(): lax.ppermute(lax.slice_in_dim(block, 0, width, axis=dim), axis, backward)  8.05 us
    convert_element_type x5, other arithmetic, m2l_block(): pieces.append(sources * weights.astype(jnp.float32)[..., None])  5.42 us
  transfers between devices with their start and end apart: 8, of which 0 were waited for; matrix products, arithmetic and copies ran while one was open for 57% of the time, Pallas kernels for 0%

commit v1 on v0

v1 whole, which is shorter than its diff:
```python
import functools

import jax
import jax.numpy as jnp
import numpy as np
from jax import lax
from jax.experimental import pallas as pl
from jax.experimental.pallas import tpu as pltpu
from jax.sharding import PartitionSpec as P

CAP = 64
P_SIZE = 4
Q = 56
SOFTEN = 0.05
LANES = 128
BIG = 2.0**100
DEAD = 2.0**120
F32, BF16 = jnp.float32, jnp.bfloat16
REACH = 3
SPAN = 2 * REACH + 1
KROWS = 136


def surface_points():
    steps = np.stack(
        np.meshgrid(np.arange(P_SIZE), np.arange(P_SIZE), np.arange(P_SIZE), indexing="ij"), -1
    ).reshape(-1, 3)
    on_face = np.any((steps == 0) | (steps == P_SIZE - 1), axis=1)
    return (0.5 + 1.4 * (steps[on_face] / (P_SIZE - 1) - 0.5)).astype(np.float32)


def admits(shift, parity):
    return -2 - parity <= shift <= 3 - parity


def split2(x):
    hi = x.astype(BF16)
    return hi, (x - hi.astype(F32)).astype(BF16)


def split3(x):
    hi = x.astype(BF16).astype(F32)
    rest = x - hi
    mid = rest.astype(BF16).astype(F32)
    return hi, mid, rest - mid


def dot(a, b):
    return jnp.dot(a, b, preferred_element_type=F32)


def dot_exact(a, b):
    return jnp.dot(a, b, preferred_element_type=F32, precision=lax.Precision.HIGHEST)


def column_weights(masses, counts, x, y, sz):
    lane = lax.broadcasted_iota(jnp.int32, (1, sz * CAP), 1)
    limit = jnp.zeros((1, sz * CAP), jnp.int32)
    for z in range(sz):
        limit = jnp.where(lane // CAP == z, counts[x, y, z], limit)
    return jnp.where(lane % CAP < limit, masses, 0.0)


def pack_row_kernel(dims, pos, mass, counts, poles, first, last):
    sx, sy, sz = dims
    width = sz * Q
    for out, x0, xp in ((first, 0, 0), (last, sx - REACH, sx - 1)):
        out[...] = jnp.zeros_like(out)
        for x in range(REACH):
            out[x * sy : (x + 1) * sy, 0:width] = poles[x0 + x]
        base = REACH * sy
        for c in range(3):
            out[base + c * sy : base + (c + 1) * sy, :] = pos[c, xp] - 0.5
        for y in range(sy):
            row = base + 3 * sy + y
            out[row : row + 1, :] = column_weights(mass[xp, y : y + 1, :], counts, xp, y, sz)


def pack_col_kernel(dims, pos, mass, counts, poles, low, high, first, last):
    sx, sy, sz = dims
    width = sz * Q
    base_in = REACH * sy
    base = REACH * (sx + 2 * REACH)
    px = sx + 2
    for out, y0, yp in ((first, 0, 0), (last, sy - REACH, sy - 1)):
        out[...] = jnp.zeros_like(out)
        for x in range(sx + 2 * REACH):
            if x < REACH:
                rows = low[x * sy + y0 : x * sy + y0 + REACH, :]
                out[x * REACH : (x + 1) * REACH, :] = rows
            elif x < REACH + sx:
                rows = poles[x - REACH, y0 : y0 + REACH, :]
                out[x * REACH : (x + 1) * REACH, 0:width] = rows
            else:
                at = (x - REACH - sx) * sy + y0
                out[x * REACH : (x + 1) * REACH, :] = high[at : at + REACH, :]
        for c in range(4):
            for x in range(px):
                if x == 0:
                    row = low[base_in + c * sy + yp : base_in + c * sy + yp + 1, :]
                elif x == px - 1:
                    row = high[base_in + c * sy + yp : base_in + c * sy + yp + 1, :]
                elif c < 3:
                    row = pos[c, x - 1, yp : yp + 1, :] - 0.5
                else:
                    row = column_weights(mass[x - 1, yp : yp + 1, :], counts, x - 1, yp, sz)
                out[base + c * px + x : base + c * px + x + 1, :] = row


def gather_constant(dims):
    sx, sy, _ = dims
    cells = [(x + REACH, y + REACH) for x in range(sx) for y in range(sy)]
    cells += [(x, y + REACH) for x in range(REACH) for y in range(sy)]
    cells += [(x + REACH + sx, y + REACH) for x in range(REACH) for y in range(sy)]
    cells += [(x, y) for x in range(sx + 2 * REACH) for y in range(REACH)]
    cells += [(x, y + REACH + sy) for x in range(sx + 2 * REACH) for y in range(REACH)]
    at = {cell: i for i, cell in enumerate(cells)}
    pick = np.zeros((2 * LANES, sx * sy * LANES), np.float32)
    for x in range(sx):
        for y in range(sy):
            for a in range(SPAN):
                for b in range(SPAN):
                    if admits(a - REACH, x % 2) and admits(b - REACH, y % 2):
                        for half in range(2):
                            col = (x * sy + y) * LANES + half * 64 + a * SPAN + b
                            pick[half * LANES + at[(x + a, y + b)], col] = 1.0
    return pick


def spread_constant(dims):
    sx, sy, sz = dims
    parents = (sx // 2) * (sy // 2) * (sz // 2)
    pick = np.zeros((sx * sy * sz, 8 * parents), np.float32)
    for z in range(sz):
        for x in range(sx):
            for y in range(sy):
                octant = 4 * (x % 2) + 2 * (y % 2) + z % 2
                parent = ((z // 2) * (sx // 2) + x // 2) * (sy // 2) + y // 2
                pick[(z * sx + x) * sy + y, octant * parents + parent] = 1.0
    return pick


def main_kernel(
    dims,
    pos, mass, counts, poles, low1, high1, low2, high2, parents, ops, tail, l2l, c2e, pick, spread,
    points,
    potential, local_out,
    su, feats, lhs, rfeats, near, sm, picked, lm, raw, table, dens, sems,
):
    sx, sy, sz = dims
    hx, hy = sx + 2, sy + 2
    cols = sx * sy
    tiles = raw.shape[0]
    width = ops.shape[1]

    whole = width // LANES

    def fetch(j):
        return pltpu.make_async_copy(ops.at[:, pl.ds(j * LANES, LANES)], raw.at[j], sems.at[j])

    for j in range(whole):
        fetch(j).start()
    if whole < tiles:
        raw[whole] = tail[...]

    su[...] = jnp.zeros_like(su)
    base1 = REACH * sy
    base2 = REACH * (sx + 2 * REACH)
    for c in range(4):
        for x in range(sx):
            at = (x + 1) * hy + 1
            if c < 3:
                su[c, at : at + sy, :] = pos[c, x] - 0.5
            else:
                for y in range(sy):
                    su[c, at + y : at + y + 1, :] = column_weights(
                        mass[x, y : y + 1, :], counts, x, y, sz
                    )
        su[c, 1 : 1 + sy, :] = low1[base1 + c * sy : base1 + (c + 1) * sy, :]
        at = (hx - 1) * hy + 1
        su[c, at : at + sy, :] = high1[base1 + c * sy : base1 + (c + 1) * sy, :]
        for x in range(hx):
            row = base2 + c * hx + x
            su[c, x * hy : x * hy + 1, :] = low2[row : row + 1, :]
            su[c, x * hy + hy - 1 : x * hy + hy, :] = high2[row : row + 1, :]

    groups = su.shape[1] // 8
    for half in range(2):
        lanes = slice(half * LANES, (half + 1) * LANES)
        shape = (8, LANES)

        def of_group(i, carry, half=half, lanes=lanes):
            at = pl.multiple_of(i * 8, 8)
            rows = lax.broadcasted_iota(jnp.int32, shape, 0) + at
            lane = lax.broadcasted_iota(jnp.int32, shape, 1) + half * LANES
            arrays = [su[c, pl.ds(at, 8), lanes] for c in range(4)]
            for k, value in source_features_at(sz, hy, arrays, rows, lane):
                feats[half, pl.ds(at * KROWS + k, 8, stride=KROWS), :] = value
            return carry

        lax.fori_loop(0, groups, of_group, 0)

    def turn(i, carry):
        at = pl.multiple_of(i * KROWS, 8)
        for half in range(2):
            block = feats[half, pl.ds(at, LANES), :]
            to = pl.multiple_of(i * (2 * LANES) + half * LANES, LANES)
            lhs[pl.ds(to, LANES), :] = block.T.astype(BF16)
        return carry

    lax.fori_loop(0, hx * hy, turn, 0)

    for half in range(2):
        lanes = slice(half * LANES, (half + 1) * LANES)
        for i in range(cols // 8):
            at = i * 8
            rows = lax.broadcasted_iota(jnp.int32, (8, LANES), 0) + at
            lane = lax.broadcasted_iota(jnp.int32, (8, LANES), 1) + half * LANES
            arrays = [
                jnp.concatenate(
                    [pos[c, (at + r) // sy] for r in range(0, 8, sy)], axis=0
                )[:, lanes]
                - 0.5
                for c in range(3)
            ]
            for k, value in target_features_at(dims, arrays, rows, lane):
                rfeats[half, pl.ds(at * KROWS + k, 8, stride=KROWS), :] = value

    def near_row(x, carry):
        for y in range(sy):
            at = pl.multiple_of((x * sy + y) * KROWS, 8)
            rhs = jnp.concatenate(
                [rfeats[0, pl.ds(at, LANES), :], rfeats[1, pl.ds(at, LANES), :]], axis=1
            ).astype(BF16)
            total = [jnp.zeros((8, LANES), F32) for _ in range(2)]
            for dx in range(3):
                for dy in range(3):
                    src = ((x + dx) * hy + y + dy) * (sz * CAP)
                    for z in range(sz):
                        rows = pl.multiple_of(src + z * CAP, CAP)
                        d2 = dot(lhs[pl.ds(rows, CAP), :], rhs)
                        for half in range(2):
                            if any(abs(z - t) <= 1 for t in (2 * half, 2 * half + 1)):
                                part = lax.rsqrt(d2[:, half * LANES : (half + 1) * LANES])
                                total[half] = total[half] + jnp.sum(
                                    part.reshape(CAP // 8, 8, LANES), axis=0
                                )
            near[pl.ds(x * sy + y, 1), :] = jnp.concatenate(
                [jnp.sum(part, axis=0, keepdims=True) for part in total], axis=1
            )
        return carry

    lax.fori_loop(0, sx, near_row, 0)

    sm[...] = jnp.zeros_like(sm)
    for x in range(sx):
        sm[x * sy : (x + 1) * sy, 0 : sz * Q] = poles[x]
    at = cols
    for ref, count in (
        (low1, REACH * sy),
        (high1, REACH * sy),
        (low2, REACH * (sx + 2 * REACH)),
        (high2, REACH * (sx + 2 * REACH)),
    ):
        sm[at : at + count, :] = ref[0:count, :]
        at += count
    for pair in range(sz // 2):
        his, los = [], []
        for zi in range(2):
            z = 2 * pair + zi
            rolled = pltpu.roll(sm[...], (2 * LANES - z * Q) % (2 * LANES), 1)[:, 0:LANES]
            hi, lo = split2(rolled.T[0:64, :])
            his.append(hi)
            los.append(lo)
        keep = lax.broadcasted_iota(jnp.int32, (64, 2 * LANES), 0) < Q
        his = jnp.where(keep, jnp.concatenate(his, axis=1).astype(F32), 0.0)
        los = jnp.where(keep, jnp.concatenate(los, axis=1).astype(F32), 0.0)
        picked[...] = jnp.concatenate([his, los], axis=0).astype(BF16)
        for xy in range(0, cols, 2):
            block = dot(picked[...], pick[:, xy * LANES : (xy + 2) * LANES])
            for i in range(2):
                lm[pair, pl.ds(xy + i, 2 * 64, stride=cols), :] = block[
                    :, i * LANES : (i + 1) * LANES
                ]

    ab = lax.broadcasted_iota(jnp.int32, (64, LANES), 0)
    closeby = (jnp.abs(ab // SPAN - REACH) <= 1) & (jnp.abs(ab % SPAN - REACH) <= 1)
    for j in range(tiles):
        if j < whole:
            fetch(j).wait()
        for c in range(SPAN):
            block = raw[j, pl.ds(c, SPAN * SPAN, stride=SPAN), :]
            block = jnp.concatenate(
                [block, jnp.zeros((64 - SPAN * SPAN, LANES), F32)], axis=0
            )
            if abs(c - REACH) <= 1:
                block = jnp.where(closeby, 0.0, block)
            if (j + 1) * LANES > width:
                lane = lax.broadcasted_iota(jnp.int32, (64, LANES), 1)
                block = jnp.where(lane < width - j * LANES, block, 0.0)
            hi, lo = split2(block)
            table[c * 64 : (c + 1) * 64, 2 * j * LANES : (2 * j + 1) * LANES] = hi
            table[c * 64 : (c + 1) * 64, (2 * j + 1) * LANES : (2 * j + 2) * LANES] = lo

    period = 16
    lane16 = lax.broadcasted_iota(jnp.int32, (cols, LANES), 1)
    check = [jnp.zeros((cols, LANES), F32) for _ in range(sz)]
    for t in range(period * Q // LANES):
        members = [s for s in range(period) if s * Q < (t + 1) * LANES and (s + 1) * Q > t * LANES]
        rows = len(members) * cols
        left = []
        for j in range(-(-Q // period)):
            if j * (period * Q // LANES) + t >= tiles:
                continue
            start = (j * period + members[0]) * cols
            left.append(
                jnp.concatenate(
                    [
                        jnp.concatenate(
                            [
                                lm[p, h * 64 * cols + start : h * 64 * cols + start + rows, :]
                                for p in range(sz // 2)
                            ],
                            axis=1,
                        )
                        for h in range(2)
                    ],
                    axis=0,
                ).astype(BF16)
            )
        for z in range(sz):
            total = None
            for j, block in enumerate(left):
                tile = j * (period * Q // LANES) + t
                first = (REACH - z) * 64
                part = dot(
                    block,
                    table[first : first + sz * 64, 2 * tile * LANES : (2 * tile + 2) * LANES],
                )
                total = part if total is None else total + part
            both = total[0:rows, 0:LANES] + (
                total[0:rows, LANES : 2 * LANES] + total[rows : 2 * rows, 0:LANES]
            )
            for i, s in enumerate(members):
                offset = s * Q - t * LANES
                part = both[i * cols : (i + 1) * cols, :]
                part = jnp.where((lane16 >= offset) & (lane16 < offset + Q), part, 0.0)
                check[z] = check[z] + pltpu.roll(part, (-offset) % LANES, 1)

    rows = []
    for pz in range(sz // 2):
        for x in range(sx // 2):
            rows.append(parents[x, :, pz * Q : (pz + 1) * Q])
    above = jnp.concatenate(rows, axis=0)
    below = jnp.concatenate([dot_exact(above, l2l[o]) for o in range(8)], axis=0)
    field = jnp.concatenate([part[:, 0:Q] for part in check], axis=0)
    field = field + dot_exact(spread[...], below)
    local = dot_exact(field, c2e[...])
    dens[...] = jnp.zeros_like(dens)
    dens[0 : sz * cols, 0:Q] = local
    flat = None
    for z in range(sz):
        part = jnp.concatenate(
            [dens[z * cols : (z + 1) * cols, :], jnp.zeros((cols, LANES), F32)], axis=1
        )
        part = pltpu.roll(part, z * Q, 1) if z else part
        flat = part if flat is None else flat + part
    for x in range(sx):
        local_out[x] = flat[x * sy : (x + 1) * sy, 0 : sz * Q]

    turned = dens[...].T[0:64, :]
    hi, lo = split2(turned[:, 0 : sz * cols])
    weights = jnp.concatenate([hi.astype(F32), lo.astype(F32)], axis=1).astype(BF16)
    row = lax.broadcasted_iota(jnp.int32, (2 * sz * cols, sz * CAP), 0) % (sz * cols)
    lane = lax.broadcasted_iota(jnp.int32, (2 * sz * cols, sz * CAP), 1)
    owner = row - (lane // CAP) * cols
    for x in range(sx):
        for y in range(sy):
            one_hot = jnp.where(owner == x * sy + y, 1.0, 0.0).astype(BF16)
            spread_out = dot(weights, one_hot)
            sums = []
            for half in range(2):
                lanes = slice(half * LANES, (half + 1) * LANES)
                d2 = jnp.zeros((64, LANES), F32)
                for c in range(3):
                    gap = pos[c, x, y : y + 1, lanes] - points[c]
                    d2 = d2 + gap * gap
                part = spread_out[:, lanes] * lax.rsqrt(d2)
                sums.append(jnp.sum(part, axis=0, keepdims=True))
            i = x * sy + y
            value = near[i : i + 1, :] + jnp.concatenate(sums, axis=1)
            potential[x, y : y + 1, :] = column_weights(value, counts, x, y, sz)


def source_features_at(sz, hy, arrays, rows, lane):
    ux, uy, uz, w = arrays
    shape = w.shape
    live = w > 0
    g = jnp.where(live, 1.0 / jnp.where(live, w * w, 1.0), 0.0)
    n = (ux * ux + uy * uy + uz * uz + SOFTEN * SOFTEN) * g
    n = jnp.where(live, n, DEAD)
    v = [split3(-2.0 * u * g) for u in (ux, uy, uz)]
    ones = [
        [(rows // hy) % 3 == m for m in range(3)],
        [(rows % hy) % 3 == m for m in range(3)],
        [lane // CAP == m for m in range(sz)],
    ]
    k = 0
    for c in range(3):
        for piece in (0, 0, 0, 1, 1, 2):
            yield k, v[c][piece]
            k += 1
    for c in range(3):
        for mask in ones[c]:
            for piece in range(3):
                yield k, jnp.where(mask, v[c][piece], 0.0)
                k += 1
    for piece in split3(n):
        yield k, piece
        k += 1
    gs = split3(g)
    for c in range(3):
        for mask in ones[c]:
            for piece in (0, 0, 0, 1, 1, 2):
                yield k, jnp.where(mask, gs[piece], 0.0)
                k += 1
    while k < LANES:
        yield k, jnp.zeros(shape, F32)
        k += 1


def target_features_at(dims, arrays, rows, lane):
    sx, sy, sz = dims
    shape = lane.shape
    place = (rows // sy, rows % sy, lane // CAP)
    t = [split3(u) for u in arrays]

    def shift(c, m):
        if c == 2:
            return (place[2] - m).astype(F32)
        return 1.0 - ((m - place[c] + 6) % 3).astype(F32)

    k = 0
    for c in range(3):
        for piece in (0, 1, 2, 0, 1, 0):
            yield k, t[c][piece]
            k += 1
    for c in range(3):
        for m in range(sz if c == 2 else 3):
            for _ in range(3):
                yield k, shift(c, m)
                k += 1
    for _ in range(3):
        yield k, jnp.ones(shape, F32)
        k += 1
    for c in range(3):
        for m in range(sz if c == 2 else 3):
            moved = arrays[c] + shift(c, m)
            parts = list(split3(moved * moved))
            if c == 2:
                reach = jnp.abs(place[2] - m) <= 1
                parts = [jnp.where(reach, p, BIG if i == 0 else 0.0) for i, p in enumerate(parts)]
            for piece in (0, 1, 2, 0, 1, 0):
                yield k, parts[piece]
                k += 1
    while k < LANES:
        yield k, jnp.zeros(shape, F32)
        k += 1


VMEM = pl.BlockSpec(memory_space=pltpu.VMEM)
SMEM = pl.BlockSpec(memory_space=pltpu.SMEM)
ANY = pl.BlockSpec(memory_space=pl.ANY)


def round_up(n, m):
    return -(-n // m) * m


def pack_row(dims, pos, mass, counts, poles):
    sx, sy, sz = dims
    rows = round_up((REACH + 4) * sy, 8)
    shape = jax.ShapeDtypeStruct((rows, sz * CAP), F32)
    return pl.pallas_call(
        functools.partial(pack_row_kernel, dims),
        out_shape=(shape, shape),
        in_specs=[VMEM, VMEM, SMEM, VMEM],
        out_specs=(VMEM, VMEM),
        name="pack_row",
    )(pos, mass, counts, poles)


def pack_col(dims, pos, mass, counts, poles, low, high):
    sx, sy, sz = dims
    rows = round_up(REACH * (sx + 2 * REACH) + 4 * (sx + 2), 8)
    shape = jax.ShapeDtypeStruct((rows, sz * CAP), F32)
    return pl.pallas_call(
        functools.partial(pack_col_kernel, dims),
        out_shape=(shape, shape),
        in_specs=[VMEM, VMEM, SMEM, VMEM, VMEM, VMEM],
        out_specs=(VMEM, VMEM),
        name="pack_col",
    )(pos, mass, counts, poles, low, high)


def main_call(dims, pos, mass, counts, poles, low1, high1, low2, high2, parents, ops, l2l, c2e):
    sx, sy, sz = dims
    cols = sx * sy
    halo = round_up((sx + 2) * (sy + 2), 8)
    pick = jnp.asarray(gather_constant(dims), BF16)
    spread = jnp.asarray(spread_constant(dims))
    points = np.full((3, 64, LANES), 10.0, np.float32)
    points[:, :Q, :] = surface_points().T[:, :, None]
    tiles = -(-ops.shape[1] // LANES)
    last = pl.BlockSpec((ops.shape[0], LANES), lambda _: (0, tiles - 1))
    return pl.pallas_call(
        functools.partial(main_kernel, dims),
        grid=(1,),
        out_shape=(
            jax.ShapeDtypeStruct((sx, sy, sz * CAP), F32),
            jax.ShapeDtypeStruct((sx, sy, sz * Q), F32),
        ),
        in_specs=[VMEM, VMEM, SMEM] + [VMEM] * 6 + [ANY, last] + [VMEM] * 5,
        out_specs=(VMEM, VMEM),
        scratch_shapes=[
            pltpu.VMEM((4, halo, sz * CAP), F32),
            pltpu.VMEM((2, halo * KROWS, LANES), F32),
            pltpu.VMEM(((sx + 2) * (sy + 2) * sz * CAP, LANES), BF16),
            pltpu.VMEM((2, cols * KROWS, LANES), F32),
            pltpu.VMEM((cols, sz * CAP), F32),
            pltpu.VMEM((LANES, 2 * LANES), F32),
            pltpu.VMEM((LANES, 2 * LANES), BF16),
            pltpu.VMEM((sz // 2, 2 * 64 * cols, LANES), F32),
            pltpu.VMEM((tiles, ops.shape[0], LANES), F32),
            pltpu.VMEM((SPAN * 64, 2 * tiles * LANES), BF16),
            pltpu.VMEM((LANES, LANES), F32),
            pltpu.SemaphoreType.DMA((tiles,)),
        ],
        compiler_params=pltpu.CompilerParams(vmem_limit_bytes=60 << 20),
        name="fields",
    )(pos, mass, counts, poles, low1, high1, low2, high2, parents, ops, ops, l2l, c2e, pick, spread,
      jnp.asarray(points))


def body(positions, masses, counts, multipoles, parent_local, m2l_ops, l2l_ops, check_to_equiv):
    sx, sy, slots = masses.shape
    dims = (sx, sy, slots // CAP)

    def exchange(first, last, axis):
        count = lax.axis_size(axis)
        up = [(i, i + 1) for i in range(count - 1)]
        down = [(b, a) for a, b in up]
        return lax.ppermute(last, axis, up), lax.ppermute(first, axis, down)

    first, last = pack_row(dims, positions, masses, counts, multipoles)
    low1, high1 = exchange(first, last, "row")
    first, last = pack_col(dims, positions, masses, counts, multipoles, low1, high1)
    low2, high2 = exchange(first, last, "col")
    return main_call(
        dims, positions, masses, counts, multipoles, low1, high1, low2, high2,
        parent_local, m2l_ops, l2l_ops, check_to_equiv,
    )


def solution(mesh):
    return jax.shard_map(
        body,
        mesh=mesh,
        in_specs=(
            P(None, "row", "col", None),
            P("row", "col", None),
            P("row", "col", None),
            P("row", "col", None),
            P("row", "col", None),
            P(),
            P(),
            P(),
        ),
        out_specs=(P("row", "col", None), P("row", "col", None)),
        check_vma=False,
    )
```

time: 176 us -> 43.5 us (0.25); the launches traced: 173 us -> 43.2 us
  other arithmetic: 88.3 us -> 0 us
  local copies, waits for them, and re-layouts: 39 us -> 1.24 us
  Pallas kernels: 0 us -> 21.5 us
  matrix products: 19.5 us -> 0 us
  starting transfers between devices: 23.5 us -> 12.3 us
  waiting for transfers between devices: 0.02 us -> 7.4 us
    reduce_sum x7 -> x0, other arithmetic: 43.7 us -> none  [near_field(): jnp.sum(sources[3][..., None, :] * lax.rsqrt(distance), axis=-1)]
    mul x40 -> x0, other arithmetic: 36.1 us -> none  [the longest x36 35 us: m2l_block(): pieces.append(sources * weights.astype(jnp.float32)[..., None])]
    pallas_call x0 -> x3, Pallas kernels: none -> 21.5 us  [the longest x1 18.4 us: main_call(): pl.pallas_call(functools.partial(main_kernel, dims), grid=(1,), out_shape...]
    unnamed x222 -> x8, local copies, waits for them, and re-layouts: 22.4 us -> 1.24 us
    dot_general x4 -> x0, matrix products: 19.5 us -> none  [the longest x1 14 us: m2l_block(): jnp.dot(stacked, m2l_ops.reshape(343 * Q, Q), precision=lax.Precision.HIG...]
    reshape x6 -> x0, local copies, waits for them, and re-layouts: 11.3 us -> none  [the longest x1 8.8 us: m2l_block(): m2l_ops.reshape(343 * Q, Q)]
    ppermute x8 -> x4, starting transfers between devices: 23.5 us -> 12.3 us  [exchange(): return (lax.ppermute(last, axis, up), lax.ppermute(first, axis, down))]
    ppermute x8 -> x4, waiting for transfers between devices: 0.02 us -> 7.4 us  [exchange(): return (lax.ppermute(last, axis, up), lax.ppermute(first, axis, down))]
  transfers between devices with their start and end apart: 8 -> 4, of which waited for: 0 -> 2; matrix products, arithmetic and copies ran while one was open for 57% -> 0% of each run, Pallas kernels for 0% -> 0%
where the time goes in v1:
time: 43.5 us; the launch traced here: 43.2 us
  Pallas kernels  21.5 us (49%)
  starting transfers between devices  12.3 us (28%)
  waiting for transfers between devices  7.4 us (17%)
  local copies, waits for them, and re-layouts  1.24 us (3%)
  between operations  0.7 us (2%)
    pallas_call x1, Pallas kernels, main_call(): pl.pallas_call(functools.partial(main_kernel, dims), grid=(1,), out_shape...  18.4 us
    ppermute x4, starting transfers between devices, exchange(): return (lax.ppermute(last, axis, up), lax.ppermute(first, axis, down))  12.3 us
    ppermute x4, waiting for transfers between devices, exchange(): return (lax.ppermute(last, axis, up), lax.ppermute(first, axis, down))  7.4 us
    pallas_call x1, Pallas kernels, pack_col(): pl.pallas_call(functools.partial(pack_col_kernel, dims), out_shape=(shape...  1.63 us
    pallas_call x1, Pallas kernels, pack_row(): pl.pallas_call(functools.partial(pack_row_kernel, dims), out_shape=(shape...  1.57 us
    unnamed x8, local copies, waits for them, and re-layouts  1.24 us
  transfers between devices with their start and end apart: 4, of which 2 were waited for; matrix products, arithmetic and copies ran while one was open for 0% of the time, Pallas kernels for 0%

profile of v1, /device:TPU:19, one launch (start us, length us, event | category | flops | bytes accessed | tf_op | source)
XLA Modules:
  0.0 43.2 jit_solution(13028198964614694013)
XLA Ops:
  0.6 1.6 %pack_row.1 = (f32[32,256]{1,0:T(8,128)}, f32[32,256]{1,0:T(8,128)}) custom-call(f32[3,4,4,256]{3,2,1,0:T(4,128)} %pos.5, f32[4,4,256]{2,1,0:T(4,128)} %mass.5, s32[4,4,4]{2,1,0:T(4,128)} %counts.5, f32[4,4,224]{2,1,0:T(4,128)} %poles.5), custom_call_target="tpu_custom_call" | custom-call | tf_op jit(solution)/shard_map/pack_row/pallas_call | solution.py:484
  2.2 3.2 %collective-permute-start = (f32[32,256]{1,0:T(8,128)}, f32[32,256]{1,0:T(8,128)S(1)}, u32[]{:S(2)}, u32[]{:S(2)}) collective-permute-start(f32[32,256]{1,0:T(8,128)} %get-tuple-element.6), channel_id=1, source_target_pairs={{0,4},{4,8},{8,12},{12,16},{16,20},{20,24},{24,28},{1,5},{5,9},{9,... | collective-permute-start | bytes 98312 | tf_op jit(solution)/shard_map/ppermute | solution.py:553
  5.4 2.1 %collective-permute-start.1 = (f32[32,256]{1,0:T(8,128)}, f32[32,256]{1,0:T(8,128)S(1)}, u32[]{:S(2)}, u32[]{:S(2)}) collective-permute-start(f32[32,256]{1,0:T(8,128)} %get-tuple-element.7), channel_id=1, source_target_pairs={{4,0},{8,4},{12,8},{16,12},{20,16},{24,20},{28,24},{5,1},{9,5},{13... | collective-permute-start | bytes 98312 | tf_op jit(solution)/shard_map/ppermute | solution.py:553
  7.5 0.0 collective-permute-done.low.low1
  7.5 0.0 copy-start
  7.5 3.6 %collective-permute-done.1.high.high1 = f32[32,256]{1,0:T(8,128)S(1)} collective-permute-done((f32[32,256]{1,0:T(8,128)}, f32[32,256]{1,0:T(8,128)S(1)}, u32[]{:S(2)}, u32[]{:S(2)}) %collective-permute-start.1) | collective-permute-done | bytes 32800 | tf_op jit(solution)/shard_map/ppermute | solution.py:553
  11.1 0.0 copy-done
  11.1 0.0 copy-start.1
  11.1 0.6 %copy-done.1 = f32[32,256]{1,0:T(8,128)} copy-done((f32[32,256]{1,0:T(8,128)}, f32[32,256]{1,0:T(8,128)S(1)}, u32[]{:S(2)}) %copy-start.1) | copy-done | bytes 32792
  11.7 1.6 %pack_col.1 = (f32[56,256]{1,0:T(8,128)}, f32[56,256]{1,0:T(8,128)}) custom-call(f32[3,4,4,256]{3,2,1,0:T(4,128)} %pos.5, f32[4,4,256]{2,1,0:T(4,128)} %mass.5, s32[4,4,4]{2,1,0:T(4,128)} %counts.5, f32[4,4,224]{2,1,0:T(4,128)} %poles.5, f32[32,256]{1,0:T(8,128)} %copy-done, f32[32,256]{1,0:T(8,128)} %copy-done.1), custom_call_target="tpu_custom_call" | custom-call | tf_op jit(solution)/shard_map/pack_col/pallas_call | solution.py:497
  13.4 5.1 %collective-permute-start.2 = (f32[56,256]{1,0:T(8,128)}, f32[56,256]{1,0:T(8,128)S(1)}, u32[]{:S(2)}, u32[]{:S(2)}) collective-permute-start(f32[56,256]{1,0:T(8,128)} %get-tuple-element.8), channel_id=1, source_target_pairs={{0,1},{1,2},{2,3},{4,5},{5,6},{6,7},{8,9},{9,10},{10,11},{12,13},{... | collective-permute-start | bytes 172040 | tf_op jit(solution)/shard_map/ppermute | solution.py:553
  18.5 1.9 %collective-permute-start.3 = (f32[56,256]{1,0:T(8,128)}, f32[56,256]{1,0:T(8,128)S(1)}, u32[]{:S(2)}, u32[]{:S(2)}) collective-permute-start(f32[56,256]{1,0:T(8,128)} %get-tuple-element.9), channel_id=1, source_target_pairs={{1,0},{2,1},{3,2},{5,4},{6,5},{7,6},{9,8},{10,9},{11,10},{13,12},{... | collective-permute-start | bytes 172040 | tf_op jit(solution)/shard_map/ppermute | solution.py:553
  20.4 0.0 collective-permute-done.2.low2
  20.4 0.0 copy-start.2
  20.4 3.8 %collective-permute-done.3.high2 = f32[56,256]{1,0:T(8,128)S(1)} collective-permute-done((f32[56,256]{1,0:T(8,128)}, f32[56,256]{1,0:T(8,128)S(1)}, u32[]{:S(2)}, u32[]{:S(2)}) %collective-permute-start.3) | collective-permute-done | bytes 57376 | tf_op jit(solution)/shard_map/ppermute | solution.py:553
  24.2 0.0 copy-done.2
  24.2 0.0 copy-start.3
  24.2 0.6 %copy-done.3 = f32[56,256]{1,0:T(8,128)} copy-done((f32[56,256]{1,0:T(8,128)}, f32[56,256]{1,0:T(8,128)S(1)}, u32[]{:S(2)}) %copy-start.3) | copy-done | bytes 57368
  24.8 18.4 %fields.1 = (f32[4,4,256]{2,1,0:T(4,128)}, f32[4,4,224]{2,1,0:T(4,128)}) custom-call(f32[3,4,4,256]{3,2,1,0:T(4,128)} %pos.5, f32[4,4,256]{2,1,0:T(4,128)} %mass.5, s32[4,4,4]{2,1,0:T(4,128)} %counts.5, f32[4,4,224]{2,1,0:T(4,128)} %poles.5, f32[32,256]{1,0:T(8,128)} %copy-done, f32[32,256]{1,0:T(8,128)} %copy-done.1, f32[56,256]{1,0:T(8,128)} %copy-done.2, ...), custom_call_target="tpu_custom_call" | custom-call | tf_op jit(solution)/shard_map/fields/pallas_call | solution.py:516
Async XLA Ops:
  2.2 5.3 %collective-permute-start = (f32[32,256]{1,0:T(8,128)}, f32[32,256]{1,0:T(8,128)S(1)}, u32[]{:S(2)}, u32[]{:S(2)}) collective-permute-start(f32[32,256]{1,0:T(8,128)} %get-tuple-element.6), channel_id=1, source_target_pairs={{0,4},{4,8},{8,12},{12,16},{16,20},{20,24},{24,28},{1,5},{5,9},{9,... | collective-permute-start | bytes 98312 | tf_op jit(solution)/shard_map/ppermute | solution.py:553
  5.4 5.8 %collective-permute-start.1 = (f32[32,256]{1,0:T(8,128)}, f32[32,256]{1,0:T(8,128)S(1)}, u32[]{:S(2)}, u32[]{:S(2)}) collective-permute-start(f32[32,256]{1,0:T(8,128)} %get-tuple-element.7), channel_id=1, source_target_pairs={{4,0},{8,4},{12,8},{16,12},{20,16},{24,20},{28,24},{5,1},{9,5},{13... | collective-permute-start | bytes 98312 | tf_op jit(solution)/shard_map/ppermute | solution.py:553
  7.5 3.6 %copy-start = (f32[32,256]{1,0:T(8,128)}, f32[32,256]{1,0:T(8,128)S(1)}, u32[]{:S(2)}) copy-start(f32[32,256]{1,0:T(8,128)S(1)} %collective-permute-done.low.low1) | copy-start | bytes 98308
  11.1 0.6 %copy-start.1 = (f32[32,256]{1,0:T(8,128)}, f32[32,256]{1,0:T(8,128)S(1)}, u32[]{:S(2)}) copy-start(f32[32,256]{1,0:T(8,128)S(1)} %collective-permute-done.1.high.high1) | copy-start | bytes 98308
  13.4 7.1 %collective-permute-start.2 = (f32[56,256]{1,0:T(8,128)}, f32[56,256]{1,0:T(8,128)S(1)}, u32[]{:S(2)}, u32[]{:S(2)}) collective-permute-start(f32[56,256]{1,0:T(8,128)} %get-tuple-element.8), channel_id=1, source_target_pairs={{0,1},{1,2},{2,3},{4,5},{5,6},{6,7},{8,9},{9,10},{10,11},{12,13},{... | collective-permute-start | bytes 172040 | tf_op jit(solution)/shard_map/ppermute | solution.py:553
  18.5 5.7 %collective-permute-start.3 = (f32[56,256]{1,0:T(8,128)}, f32[56,256]{1,0:T(8,128)S(1)}, u32[]{:S(2)}, u32[]{:S(2)}) collective-permute-start(f32[56,256]{1,0:T(8,128)} %get-tuple-element.9), channel_id=1, source_target_pairs={{1,0},{2,1},{3,2},{5,4},{6,5},{7,6},{9,8},{10,9},{11,10},{13,12},{... | collective-permute-start | bytes 172040 | tf_op jit(solution)/shard_map/ppermute | solution.py:553
  20.4 3.8 %copy-start.2 = (f32[56,256]{1,0:T(8,128)}, f32[56,256]{1,0:T(8,128)S(1)}, u32[]{:S(2)}) copy-start(f32[56,256]{1,0:T(8,128)S(1)} %collective-permute-done.2.low2) | copy-start | bytes 172036
  24.2 0.6 %copy-start.3 = (f32[56,256]{1,0:T(8,128)}, f32[56,256]{1,0:T(8,128)S(1)}, u32[]{:S(2)}) copy-start(f32[56,256]{1,0:T(8,128)S(1)} %collective-permute-done.3.high2) | copy-start | bytes 172036

commit v2 on v1

--- a/solution.py
+++ b/solution.py
@@ -61,50 +61,74 @@
     return jnp.where(lane % CAP < limit, masses, 0.0)
 
 
-def pack_row_kernel(dims, pos, mass, counts, poles, first, last):
-    sx, sy, sz = dims
-    width = sz * Q
-    for out, x0, xp in ((first, 0, 0), (last, sx - REACH, sx - 1)):
-        out[...] = jnp.zeros_like(out)
-        for x in range(REACH):
-            out[x * sy : (x + 1) * sy, 0:width] = poles[x0 + x]
-        base = REACH * sy
-        for c in range(3):
-            out[base + c * sy : base + (c + 1) * sy, :] = pos[c, xp] - 0.5
-        for y in range(sy):
-            row = base + 3 * sy + y
-            out[row : row + 1, :] = column_weights(mass[xp, y : y + 1, :], counts, xp, y, sz)
-
-
-def pack_col_kernel(dims, pos, mass, counts, poles, low, high, first, last):
-    sx, sy, sz = dims
-    width = sz * Q
+def is_odd(axis):
+    return lax.axis_index(axis) % 2 == 1
+
+
+def store_pair(odd, to_first_pair, to_second_pair, rows, lanes, low_edge, high_edge):
+    to_first_pair[rows, lanes] = jnp.where(odd, low_edge, high_edge)
+    to_second_pair[rows, lanes] = jnp.where(odd, high_edge, low_edge)
+
+
+def pack_row_kernel(dims, pos, mass, counts, poles, send_a, send_b):
+    sx, sy, sz = dims
+    odd = is_odd("row")
+    store = functools.partial(store_pair, odd, send_a, send_b)
+    every = slice(0, sz * CAP)
+    send_a[...] = jnp.zeros_like(send_a)
+    send_b[...] = jnp.zeros_like(send_b)
+    for x in range(REACH):
+        store(slice(x * sy, (x + 1) * sy), slice(0, sz * Q), poles[x], poles[sx - REACH + x])
+    base = REACH * sy
+    for c in range(3):
+        rows = slice(base + c * sy, base + (c + 1) * sy)
+        store(rows, every, pos[c, 0] - 0.5, pos[c, sx - 1] - 0.5)
+    for y in range(sy):
+        row = base + 3 * sy + y
+        store(
+            slice(row, row + 1),
+            every,
+            column_weights(mass[0, y : y + 1, :], counts, 0, y, sz),
+            column_weights(mass[sx - 1, y : y + 1, :], counts, sx - 1, y, sz),
+        )
+
+
+def pack_col_kernel(dims, pos, mass, counts, poles, got_a, got_b, send_a, send_b, low, high):
+    sx, sy, sz = dims
+    odd_row = is_odd("row")
+    low[...] = jnp.where(odd_row, got_a[...], got_b[...])
+    high[...] = jnp.where(odd_row, got_b[...], got_a[...])
+    store = functools.partial(store_pair, is_odd("col"), send_a, send_b)
+    every = slice(0, sz * CAP)
     base_in = REACH * sy
     base = REACH * (sx + 2 * REACH)
     px = sx + 2
-    for out, y0, yp in ((first, 0, 0), (last, sy - REACH, sy - 1)):
-        out[...] = jnp.zeros_like(out)
-        for x in range(sx + 2 * REACH):
-            if x < REACH:
-                rows = low[x * sy + y0 : x * sy + y0 + REACH, :]
-                out[x * REACH : (x + 1) * REACH, :] = rows
-            elif x < REACH + sx:
-                rows = poles[x - REACH, y0 : y0 + REACH, :]
-                out[x * REACH : (x + 1) * REACH, 0:width] = rows
-            else:
-                at = (x - REACH - sx) * sy + y0
-                out[x * REACH : (x + 1) * REACH, :] = high[at : at + REACH, :]
-        for c in range(4):
-            for x in range(px):
+    send_a[...] = jnp.zeros_like(send_a)
+    send_b[...] = jnp.zeros_like(send_b)
+    for x in range(sx + 2 * REACH):
+        rows = slice(x * REACH, (x + 1) * REACH)
+        if REACH <= x < REACH + sx:
+            own = poles.at[x - REACH]
+            store(rows, slice(0, sz * Q), own[0:REACH, :], own[sy - REACH : sy, :])
+        else:
+            ref, at = (low, x * sy) if x < REACH else (high, (x - REACH - sx) * sy)
+            store(rows, every, ref[at : at + REACH, :], ref[at + sy - REACH : at + sy, :])
+    for c in range(4):
+        for x in range(px):
+            edges = []
+            for y in (0, sy - 1):
+                at = base_in + c * sy + y
                 if x == 0:
-                    row = low[base_in + c * sy + yp : base_in + c * sy + yp + 1, :]
+                    row = low[at : at + 1, :]
                 elif x == px - 1:
-                    row = high[base_in + c * sy + yp : base_in + c * sy + yp + 1, :]
+                    row = high[at : at + 1, :]
                 elif c < 3:
-                    row = pos[c, x - 1, yp : yp + 1, :] - 0.5
+                    row = pos[c, x - 1, y : y + 1, :] - 0.5
                 else:
-                    row = column_weights(mass[x - 1, yp : yp + 1, :], counts, x - 1, yp, sz)
-                out[base + c * px + x : base + c * px + x + 1, :] = row
+                    row = column_weights(mass[x - 1, y : y + 1, :], counts, x - 1, y, sz)
+                edges.append(row)
+            at = base + c * px + x
+            store(slice(at, at + 1), every, *edges)
 
 
 def gather_constant(dims):
@@ -140,130 +164,181 @@
     return pick
 
 
-def main_kernel(
-    dims,
-    pos, mass, counts, poles, low1, high1, low2, high2, parents, ops, tail, l2l, c2e, pick, spread,
-    points,
-    potential, local_out,
-    su, feats, lhs, rfeats, near, sm, picked, lm, raw, table, dens, sems,
-):
-    sx, sy, sz = dims
-    hx, hy = sx + 2, sy + 2
-    cols = sx * sy
+def prepare_kernel(ops, tail, table, raw, made, sems, out_sems):
+    width = ops.shape[1]
     tiles = raw.shape[0]
-    width = ops.shape[1]
-
     whole = width // LANES
 
     def fetch(j):
         return pltpu.make_async_copy(ops.at[:, pl.ds(j * LANES, LANES)], raw.at[j], sems.at[j])
+
+    def put(j):
+        lanes = pl.ds(2 * j * LANES, 2 * LANES)
+        return pltpu.make_async_copy(made.at[:, lanes], table.at[:, lanes], out_sems.at[j])
 
     for j in range(whole):
         fetch(j).start()
     if whole < tiles:
         raw[whole] = tail[...]
-
-    su[...] = jnp.zeros_like(su)
+    ab = lax.broadcasted_iota(jnp.int32, (64, LANES), 0)
+    closeby = (jnp.abs(ab // SPAN - REACH) <= 1) & (jnp.abs(ab % SPAN - REACH) <= 1)
+    for j in range(tiles):
+        if j < whole:
+            fetch(j).wait()
+        for c in range(SPAN):
+            block = raw[j, pl.ds(c, SPAN * SPAN, stride=SPAN), :]
+            block = jnp.concatenate(
+                [block, jnp.zeros((64 - SPAN * SPAN, LANES), F32)], axis=0
+            )
+            if abs(c - REACH) <= 1:
+                block = jnp.where(closeby, 0.0, block)
+            if (j + 1) * LANES > width:
+                lane = lax.broadcasted_iota(jnp.int32, (64, LANES), 1)
+                block = jnp.where(lane < width - j * LANES, block, 0.0)
+            hi, lo = split2(block)
+            made[c * 64 : (c + 1) * 64, 2 * j * LANES : (2 * j + 1) * LANES] = hi
+            made[c * 64 : (c + 1) * 64, (2 * j + 1) * LANES : (2 * j + 2) * LANES] = lo
+        put(j).start()
+    for j in range(tiles):
+        put(j).wait()
+
+
+def build_sources(sz, place, su, feats, lhs, columns):
+    for i in range(su.shape[1] // 8):
+        at = i * 8
+        for half in range(2):
+            rows = lax.broadcasted_iota(jnp.int32, (8, LANES), 0) + at
+            lane = lax.broadcasted_iota(jnp.int32, (8, LANES), 1) + half * LANES
+            lanes = slice(half * LANES, (half + 1) * LANES)
+            arrays = [su[c, at : at + 8, lanes] for c in range(4)]
+            for k, value in source_features_at(sz, place(rows), arrays, lane):
+                feats[half, pl.ds(at * KROWS + k, 8, stride=KROWS), :] = value
+    for i in range(columns):
+        for half in range(2):
+            block = feats[half, i * KROWS : i * KROWS + LANES, :]
+            at = (2 * i + half) * LANES
+            lhs[at : at + LANES, :] = block.T.astype(BF16)
+
+
+def near_sums(sz, lhs, rhs, sources):
+    total = [jnp.zeros((8, LANES), F32) for _ in range(2)]
+    for src in sources:
+        for z in range(sz):
+            rows = src * sz * CAP + z * CAP
+            d2 = dot(lhs[rows : rows + CAP, :], rhs)
+            for half in range(2):
+                if any(abs(z - t) <= 1 for t in (2 * half, 2 * half + 1)):
+                    part = lax.rsqrt(d2[:, half * LANES : (half + 1) * LANES])
+                    total[half] = total[half] + jnp.sum(
+                        part.reshape(CAP // 8, 8, LANES), axis=0
+                    )
+    return jnp.concatenate([jnp.sum(part, axis=0, keepdims=True) for part in total], axis=1)
+
+
+def near_own_kernel(dims, pos, mass, counts, after, near, rhs, su, feats, lhs, rfeats):
+    sx, sy, sz = dims
+    cols = sx * sy
+    for x in range(sx):
+        for c in range(3):
+            su[c, x * sy : (x + 1) * sy, :] = pos[c, x] - 0.5
+        for y in range(sy):
+            row = x * sy + y
+            su[3, row : row + 1, :] = column_weights(mass[x, y : y + 1, :], counts, x, y, sz)
+
+    build_sources(sz, lambda rows: (rows // sy + 1, rows % sy + 1), su, feats, lhs, cols)
+    for half in range(2):
+        lanes = slice(half * LANES, (half + 1) * LANES)
+        for at in range(0, cols, 8):
+            rows = lax.broadcasted_iota(jnp.int32, (8, LANES), 0) + at
+            lane = lax.broadcasted_iota(jnp.int32, (8, LANES), 1) + half * LANES
+            arrays = [su[c, at : at + 8, lanes] for c in range(3)]
+            for k, value in target_features_at(dims, arrays, rows, lane):
+                rfeats[half, pl.ds(at * KROWS + k, 8, stride=KROWS), :] = value
+    for i in range(cols):
+        for half in range(2):
+            rhs[i * LANES : (i + 1) * LANES, half * LANES : (half + 1) * LANES] = rfeats[
+                half, i * KROWS : i * KROWS + LANES, :
+            ].astype(BF16)
+    for x in range(sx):
+        for y in range(sy):
+            i = x * sy + y
+            sources = [
+                a * sy + b
+                for a in range(max(x - 1, 0), min(x + 2, sx))
+                for b in range(max(y - 1, 0), min(y + 2, sy))
+            ]
+            near[i : i + 1, :] = near_sums(
+                sz, lhs, rhs[i * LANES : (i + 1) * LANES, :], sources
+            )
+
+
+def fields_kernel(
+    dims,
+    pos, counts, poles, a1, b1, a2, b2, near_own, rhs_far, table_far, parents, l2l, c2e, pick,
+    spread, points,
+    potential, local_out,
+    su, feats, lhs, rhs, near, sm, picked, lm, table, dens, sems,
+):
+    sx, sy, sz = dims
+    hx, hy = sx + 2, sy + 2
+    cols = sx * sy
+    tiles = table.shape[1] // (2 * LANES)
+    width = Q * Q
+
+    get_rhs = pltpu.make_async_copy(rhs_far, rhs, sems.at[0])
+    get_table = pltpu.make_async_copy(table_far, table, sems.at[1])
+    get_rhs.start()
+    get_table.start()
+
+    odd_row, odd_col = is_odd("row"), is_odd("col")
     base1 = REACH * sy
     base2 = REACH * (sx + 2 * REACH)
-    for c in range(4):
-        for x in range(sx):
-            at = (x + 1) * hy + 1
-            if c < 3:
-                su[c, at : at + sy, :] = pos[c, x] - 0.5
-            else:
-                for y in range(sy):
-                    su[c, at + y : at + y + 1, :] = column_weights(
-                        mass[x, y : y + 1, :], counts, x, y, sz
-                    )
-        su[c, 1 : 1 + sy, :] = low1[base1 + c * sy : base1 + (c + 1) * sy, :]
-        at = (hx - 1) * hy + 1
-        su[c, at : at + sy, :] = high1[base1 + c * sy : base1 + (c + 1) * sy, :]
-        for x in range(hx):
-            row = base2 + c * hx + x
-            su[c, x * hy : x * hy + 1, :] = low2[row : row + 1, :]
-            su[c, x * hy + hy - 1 : x * hy + hy, :] = high2[row : row + 1, :]
-
-    groups = su.shape[1] // 8
-    for half in range(2):
-        lanes = slice(half * LANES, (half + 1) * LANES)
-        shape = (8, LANES)
-
-        def of_group(i, carry, half=half, lanes=lanes):
-            at = pl.multiple_of(i * 8, 8)
-            rows = lax.broadcasted_iota(jnp.int32, shape, 0) + at
-            lane = lax.broadcasted_iota(jnp.int32, shape, 1) + half * LANES
-            arrays = [su[c, pl.ds(at, 8), lanes] for c in range(4)]
-            for k, value in source_features_at(sz, hy, arrays, rows, lane):
-                feats[half, pl.ds(at * KROWS + k, 8, stride=KROWS), :] = value
-            return carry
-
-        lax.fori_loop(0, groups, of_group, 0)
-
-    def turn(i, carry):
-        at = pl.multiple_of(i * KROWS, 8)
-        for half in range(2):
-            block = feats[half, pl.ds(at, LANES), :]
-            to = pl.multiple_of(i * (2 * LANES) + half * LANES, LANES)
-            lhs[pl.ds(to, LANES), :] = block.T.astype(BF16)
-        return carry
-
-    lax.fori_loop(0, hx * hy, turn, 0)
-
-    for half in range(2):
-        lanes = slice(half * LANES, (half + 1) * LANES)
-        for i in range(cols // 8):
-            at = i * 8
-            rows = lax.broadcasted_iota(jnp.int32, (8, LANES), 0) + at
-            lane = lax.broadcasted_iota(jnp.int32, (8, LANES), 1) + half * LANES
-            arrays = [
-                jnp.concatenate(
-                    [pos[c, (at + r) // sy] for r in range(0, 8, sy)], axis=0
-                )[:, lanes]
-                - 0.5
-                for c in range(3)
-            ]
-            for k, value in target_features_at(dims, arrays, rows, lane):
-                rfeats[half, pl.ds(at * KROWS + k, 8, stride=KROWS), :] = value
-
-    def near_row(x, carry):
-        for y in range(sy):
-            at = pl.multiple_of((x * sy + y) * KROWS, 8)
-            rhs = jnp.concatenate(
-                [rfeats[0, pl.ds(at, LANES), :], rfeats[1, pl.ds(at, LANES), :]], axis=1
-            ).astype(BF16)
-            total = [jnp.zeros((8, LANES), F32) for _ in range(2)]
-            for dx in range(3):
-                for dy in range(3):
-                    src = ((x + dx) * hy + y + dy) * (sz * CAP)
-                    for z in range(sz):
-                        rows = pl.multiple_of(src + z * CAP, CAP)
-                        d2 = dot(lhs[pl.ds(rows, CAP), :], rhs)
-                        for half in range(2):
-                            if any(abs(z - t) <= 1 for t in (2 * half, 2 * half + 1)):
-                                part = lax.rsqrt(d2[:, half * LANES : (half + 1) * LANES])
-                                total[half] = total[half] + jnp.sum(
-                                    part.reshape(CAP // 8, 8, LANES), axis=0
-                                )
-            near[pl.ds(x * sy + y, 1), :] = jnp.concatenate(
-                [jnp.sum(part, axis=0, keepdims=True) for part in total], axis=1
-            )
-        return carry
-
-    lax.fori_loop(0, sx, near_row, 0)
-
+    sides = []
+    for odd, got_a, got_b, base, line in (
+        (odd_row, a1, b1, base1, sy), (odd_col, a2, b2, base2, hx)
+    ):
+        for first, second in ((got_a, got_b), (got_b, got_a)):
+            sides.append((odd, first, second, base, line))
+
+    su[...] = jnp.zeros_like(su)
     sm[...] = jnp.zeros_like(sm)
     for x in range(sx):
         sm[x * sy : (x + 1) * sy, 0 : sz * Q] = poles[x]
-    at = cols
-    for ref, count in (
-        (low1, REACH * sy),
-        (high1, REACH * sy),
-        (low2, REACH * (sx + 2 * REACH)),
-        (high2, REACH * (sx + 2 * REACH)),
-    ):
-        sm[at : at + count, :] = ref[0:count, :]
-        at += count
+    to, to_poles = 0, cols
+    for odd, first, second, base, line in sides:
+        value = jnp.where(odd, first[...], second[...])
+        sm[to_poles : to_poles + base, :] = value[0:base, :]
+        to_poles += base
+        for c in range(4):
+            su[c, to : to + line, :] = value[base + c * line : base + (c + 1) * line, :]
+        to += line
+
+    def place(rows):
+        x, y = rows - 2 * sy - hx, jnp.full_like(rows, hy - 1)
+        x = jnp.where(rows < 2 * sy + hx, rows - 2 * sy, x)
+        y = jnp.where(rows < 2 * sy + hx, 0, y)
+        x = jnp.where(rows < 2 * sy, hx - 1, x)
+        y = jnp.where(rows < 2 * sy, rows - sy + 1, y)
+        x = jnp.where(rows < sy, 0, x)
+        y = jnp.where(rows < sy, rows + 1, y)
+        return x, y
+
+    halo = {(0, y + 1): y for y in range(sy)}
+    halo.update({(hx - 1, y + 1): sy + y for y in range(sy)})
+    halo.update({(x, 0): 2 * sy + x for x in range(hx)})
+    halo.update({(x, hy - 1): 2 * sy + hx + x for x in range(hx)})
+    build_sources(sz, place, su, feats, lhs, len(halo))
+    get_rhs.wait()
+    for x in range(sx):
+        for y in range(sy):
+            i = x * sy + y
+            cells = [(x + dx, y + dy) for dx in range(3) for dy in range(3)]
+            sources = [halo[cell] for cell in cells if cell in halo]
+            value = near_own[i : i + 1, :]
+            if sources:
+                value = value + near_sums(sz, lhs, rhs[i * LANES : (i + 1) * LANES, :], sources)
+            near[i : i + 1, :] = value
+
     for pair in range(sz // 2):
         his, los = [], []
         for zi in range(2):
@@ -283,25 +358,7 @@
                     :, i * LANES : (i + 1) * LANES
                 ]
 
-    ab = lax.broadcasted_iota(jnp.int32, (64, LANES), 0)
-    closeby = (jnp.abs(ab // SPAN - REACH) <= 1) & (jnp.abs(ab % SPAN - REACH) <= 1)
-    for j in range(tiles):
-        if j < whole:
-            fetch(j).wait()
-        for c in range(SPAN):
-            block = raw[j, pl.ds(c, SPAN * SPAN, stride=SPAN), :]
-            block = jnp.concatenate(
-                [block, jnp.zeros((64 - SPAN * SPAN, LANES), F32)], axis=0
-            )
-            if abs(c - REACH) <= 1:
-                block = jnp.where(closeby, 0.0, block)
-            if (j + 1) * LANES > width:
-                lane = lax.broadcasted_iota(jnp.int32, (64, LANES), 1)
-                block = jnp.where(lane < width - j * LANES, block, 0.0)
-            hi, lo = split2(block)
-            table[c * 64 : (c + 1) * 64, 2 * j * LANES : (2 * j + 1) * LANES] = hi
-            table[c * 64 : (c + 1) * 64, (2 * j + 1) * LANES : (2 * j + 2) * LANES] = lo
-
+    get_table.wait()
     period = 16
     lane16 = lax.broadcasted_iota(jnp.int32, (cols, LANES), 1)
     check = [jnp.zeros((cols, LANES), F32) for _ in range(sz)]
@@ -392,7 +449,7 @@
             potential[x, y : y + 1, :] = column_weights(value, counts, x, y, sz)
 
 
-def source_features_at(sz, hy, arrays, rows, lane):
+def source_features_at(sz, place, arrays, lane):
     ux, uy, uz, w = arrays
     shape = w.shape
     live = w > 0
@@ -401,8 +458,8 @@
     n = jnp.where(live, n, DEAD)
     v = [split3(-2.0 * u * g) for u in (ux, uy, uz)]
     ones = [
-        [(rows // hy) % 3 == m for m in range(3)],
-        [(rows % hy) % 3 == m for m in range(3)],
+        [place[0] % 3 == m for m in range(3)],
+        [place[1] % 3 == m for m in range(3)],
         [lane // CAP == m for m in range(sz)],
     ]
     k = 0
@@ -490,7 +547,28 @@
     )(pos, mass, counts, poles)
 
 
-def pack_col(dims, pos, mass, counts, poles, low, high):
+def prepare(ops):
+    rows, width = ops.shape
+    tiles = -(-width // LANES)
+    return pl.pallas_call(
+        prepare_kernel,
+        grid=(1,),
+        out_shape=jax.ShapeDtypeStruct((SPAN * 64, 2 * tiles * LANES), BF16),
+        in_specs=[ANY, pl.BlockSpec((rows, LANES), lambda _: (0, tiles - 1))],
+        out_specs=ANY,
+        scratch_shapes=[
+            pltpu.VMEM((tiles, rows, LANES), F32),
+            pltpu.VMEM((SPAN * 64, 2 * tiles * LANES), BF16),
+            pltpu.SemaphoreType.DMA((tiles,)),
+            pltpu.SemaphoreType.DMA((tiles,)),
+        ],
+        compiler_params=pltpu.CompilerParams(vmem_limit_bytes=20 << 20),
+        cost_estimate=pl.CostEstimate(flops=1 << 24, bytes_accessed=10 << 20, transcendentals=0),
+        name="prepare",
+    )(ops, ops)
+
+
+def pack_col(dims, pos, mass, counts, poles, got_a, got_b):
     sx, sy, sz = dims
     rows = round_up(REACH * (sx + 2 * REACH) + 4 * (sx + 2), 8)
     shape = jax.ShapeDtypeStruct((rows, sz * CAP), F32)
@@ -499,66 +577,89 @@
         out_shape=(shape, shape),
         in_specs=[VMEM, VMEM, SMEM, VMEM, VMEM, VMEM],
         out_specs=(VMEM, VMEM),
+        scratch_shapes=[pltpu.VMEM(got_a.shape, F32), pltpu.VMEM(got_a.shape, F32)],
         name="pack_col",
-    )(pos, mass, counts, poles, low, high)
-
-
-def main_call(dims, pos, mass, counts, poles, low1, high1, low2, high2, parents, ops, l2l, c2e):
+    )(pos, mass, counts, poles, got_a, got_b)
+
+
+def near_own(dims, pos, mass, counts, after):
     sx, sy, sz = dims
     cols = sx * sy
-    halo = round_up((sx + 2) * (sy + 2), 8)
+    return pl.pallas_call(
+        functools.partial(near_own_kernel, dims),
+        out_shape=(
+            jax.ShapeDtypeStruct((cols, sz * CAP), F32),
+            jax.ShapeDtypeStruct((cols * LANES, sz * CAP), BF16),
+        ),
+        in_specs=[VMEM, VMEM, SMEM, ANY],
+        out_specs=(VMEM, VMEM),
+        scratch_shapes=[
+            pltpu.VMEM((4, cols, sz * CAP), F32),
+            pltpu.VMEM((2, cols * KROWS, LANES), F32),
+            pltpu.VMEM((cols * sz * CAP, LANES), BF16),
+            pltpu.VMEM((2, cols * KROWS, LANES), F32),
+        ],
+        compiler_params=pltpu.CompilerParams(vmem_limit_bytes=20 << 20),
+        cost_estimate=pl.CostEstimate(flops=1 << 32, bytes_accessed=1 << 20, transcendentals=1 << 22),
+        name="near_own",
+    )(pos, mass, counts, after)
+
+
+def fields(dims, pos, counts, poles, a1, b1, a2, b2, near, rhs, table, parents, l2l, c2e):
+    sx, sy, sz = dims
+    cols = sx * sy
+    ring = 2 * sy + 2 * (sx + 2)
     pick = jnp.asarray(gather_constant(dims), BF16)
     spread = jnp.asarray(spread_constant(dims))
     points = np.full((3, 64, LANES), 10.0, np.float32)
     points[:, :Q, :] = surface_points().T[:, :, None]
-    tiles = -(-ops.shape[1] // LANES)
-    last = pl.BlockSpec((ops.shape[0], LANES), lambda _: (0, tiles - 1))
     return pl.pallas_call(
-        functools.partial(main_kernel, dims),
-        grid=(1,),
+        functools.partial(fields_kernel, dims),
         out_shape=(
             jax.ShapeDtypeStruct((sx, sy, sz * CAP), F32),
             jax.ShapeDtypeStruct((sx, sy, sz * Q), F32),
         ),
-        in_specs=[VMEM, VMEM, SMEM] + [VMEM] * 6 + [ANY, last] + [VMEM] * 5,
+        in_specs=[VMEM, SMEM] + [VMEM] * 6 + [ANY, ANY] + [VMEM] * 6,
         out_specs=(VMEM, VMEM),
         scratch_shapes=[
-            pltpu.VMEM((4, halo, sz * CAP), F32),
-            pltpu.VMEM((2, halo * KROWS, LANES), F32),
-            pltpu.VMEM(((sx + 2) * (sy + 2) * sz * CAP, LANES), BF16),
-            pltpu.VMEM((2, cols * KROWS, LANES), F32),
+            pltpu.VMEM((4, round_up(ring, 8), sz * CAP), F32),
+            pltpu.VMEM((2, round_up(ring, 8) * KROWS, LANES), F32),
+            pltpu.VMEM((ring * sz * CAP, LANES), BF16),
+            pltpu.VMEM(rhs.shape, BF16),
             pltpu.VMEM((cols, sz * CAP), F32),
             pltpu.VMEM((LANES, 2 * LANES), F32),
             pltpu.VMEM((LANES, 2 * LANES), BF16),
             pltpu.VMEM((sz // 2, 2 * 64 * cols, LANES), F32),
-            pltpu.VMEM((tiles, ops.shape[0], LANES), F32),
-            pltpu.VMEM((SPAN * 64, 2 * tiles * LANES), BF16),
+            pltpu.VMEM(table.shape, BF16),
             pltpu.VMEM((LANES, LANES), F32),
-            pltpu.SemaphoreType.DMA((tiles,)),
+            pltpu.SemaphoreType.DMA((2,)),
         ],
-        compiler_params=pltpu.CompilerParams(vmem_limit_bytes=60 << 20),
+        compiler_params=pltpu.CompilerParams(vmem_limit_bytes=30 << 20),
         name="fields",
-    )(pos, mass, counts, poles, low1, high1, low2, high2, parents, ops, ops, l2l, c2e, pick, spread,
+    )(pos, counts, poles, a1, b1, a2, b2, near, rhs, table, parents, l2l, c2e, pick, spread,
       jnp.asarray(points))
+
+
+def exchange(send_a, send_b, axis):
+    count = lax.axis_size(axis)
+    got = []
+    for value, first in ((send_a, 0), (send_b, 1)):
+        pairs = [(i, i + 1) for i in range(first, count - 1, 2)]
+        got.append(lax.ppermute(value, axis, pairs + [(b, a) for a, b in pairs]))
+    return got
 
 
 def body(positions, masses, counts, multipoles, parent_local, m2l_ops, l2l_ops, check_to_equiv):
     sx, sy, slots = masses.shape
     dims = (sx, sy, slots // CAP)
-
-    def exchange(first, last, axis):
-        count = lax.axis_size(axis)
-        up = [(i, i + 1) for i in range(count - 1)]
-        down = [(b, a) for a, b in up]
-        return lax.ppermute(last, axis, up), lax.ppermute(first, axis, down)
-
-    first, last = pack_row(dims, positions, masses, counts, multipoles)
-    low1, high1 = exchange(first, last, "row")
-    first, last = pack_col(dims, positions, masses, counts, multipoles, low1, high1)
-    low2, high2 = exchange(first, last, "col")
-    return main_call(
-        dims, positions, masses, counts, multipoles, low1, high1, low2, high2,
-        parent_local, m2l_ops, l2l_ops, check_to_equiv,
+    table = prepare(m2l_ops)
+    a1, b1 = exchange(*pack_row(dims, positions, masses, counts, multipoles), "row")
+    send = pack_col(dims, positions, masses, counts, multipoles, a1, b1)
+    a2, b2 = exchange(*send, "col")
+    near, rhs = near_own(dims, positions, masses, counts, send[0])
+    return fields(
+        dims, positions, counts, multipoles, a1, b1, a2, b2, near, rhs, table,
+        parent_local, l2l_ops, check_to_equiv,
     )
 
 

time: 43.5 us -> 36.5 us (0.84)
  waiting for transfers between devices: 7.4 us -> 0.01 us
  local copies, waits for them, and re-layouts: 1.24 us -> 6.94 us
  starting transfers between devices: 12.3 us -> 8.88 us
  Pallas kernels: 21.5 us -> 19.2 us
    ppermute x4, waiting for transfers between devices: 7.4 us -> 0.01 us  [exchange(): got.append(lax.ppermute(value, axis, pairs + [(b, a) for a, b in pairs]))]
    unnamed x8 -> x38, local copies, waits for them, and re-layouts: 1.24 us -> 6.94 us
    ppermute x4, starting transfers between devices: 12.3 us -> 8.88 us  [exchange(): got.append(lax.ppermute(value, axis, pairs + [(b, a) for a, b in pairs]))]
    pallas_call x1 -> x3, Pallas kernels: 18.4 us -> 16 us  [the longest x1 8.47 us: fields(): pl.pallas_call(functools.partial(fields_kernel, dims), out_shape=(jax.Sha...]
  transfers between devices with their start and end apart: 4 -> 4, of which waited for: 2 -> 0; matrix products, arithmetic and copies ran while one was open for 0% -> 0% of each run, Pallas kernels for 0% -> 21%
where the time goes in v2:
time: 36.5 us; the launch traced here: 36.1 us
  Pallas kernels  19.2 us (53%)
  starting transfers between devices  8.88 us (24%)
  local copies, waits for them, and re-layouts  6.94 us (19%)
  between operations  1.08 us (3%)
    ppermute x4, starting transfers between devices, exchange(): got.append(lax.ppermute(value, axis, pairs + [(b, a) for a, b in pairs]))  8.88 us
    pallas_call x1, Pallas kernels, fields(): pl.pallas_call(functools.partial(fields_kernel, dims), out_shape=(jax.Sha...  8.47 us
    unnamed x38, local copies, waits for them, and re-layouts  6.94 us
    pallas_call x1, Pallas kernels, near_own(): pl.pallas_call(functools.partial(near_own_kernel, dims), out_shape=(jax.S...  5.16 us
    pallas_call x1, Pallas kernels, prepare(): pl.pallas_call(prepare_kernel, grid=(1,), out_shape=jax.ShapeDtypeStruct(...  2.33 us
    pallas_call x1, Pallas kernels, pack_col(): pl.pallas_call(functools.partial(pack_col_kernel, dims), out_shape=(shape...  1.65 us
    pallas_call x1, Pallas kernels, pack_row(): pl.pallas_call(functools.partial(pack_row_kernel, dims), out_shape=(shape...  1.58 us
  transfers between devices with their start and end apart: 4, of which 0 were waited for; matrix products, arithmetic and copies ran while one was open for 0% of the time, Pallas kernels for 21%

profile of v2, /device:TPU:19, one launch (start us, length us, event | category | flops | bytes accessed | tf_op | source)
XLA Modules:
  0.0 36.1 jit_solution(14109453890301124422)
XLA Ops:
  0.6 1.6 %pack_row.1 = (f32[32,256]{1,0:T(8,128)}, f32[32,256]{1,0:T(8,128)}) custom-call(f32[3,4,4,256]{3,2,1,0:T(4,128)} %pos.7, f32[4,4,256]{2,1,0:T(4,128)} %mass.5, s32[4,4,4]{2,1,0:T(4,128)} %counts.7, f32[4,4,224]{2,1,0:T(4,128)} %poles.5), custom_call_target="tpu_custom_call" | custom-call | tf_op jit(solution)/shard_map/pack_row/pallas_call | solution.py:541
  2.2 0.3 collective-permute-start
  2.5 4.1 %collective-permute-start.1 = (f32[32,256]{1,0:T(8,128)}, f32[32,256]{1,0:T(8,128)S(1)}, u32[]{:S(2)}, u32[]{:S(2)}) collective-permute-start(f32[32,256]{1,0:T(8,128)} %get-tuple-element.9), channel_id=1, source_target_pairs={{4,8},{12,16},{20,24},{8,4},{16,12},{24,20},{5,9},{13,17},{21,25},... | collective-permute-start | bytes 98312 | tf_op jit(solution)/shard_map/ppermute | solution.py:648
  6.6 0.0 copy-start.1
  6.6 2.2 %copy-done.1 = f32[343,3136]{1,0:T(8,128)S(1)} copy-done((f32[343,3136]{1,0:T(8,128)S(1)}, f32[343,3136]{1,0:T(8,128)}, u32[]{:S(2)}) %copy-start.1) | copy-done | bytes 4302616
  8.9 2.3 %prepare.1.table_far = bf16[448,6400]{1,0:T(8,128)(2,1)S(1)} custom-call(f32[343,3136]{1,0:T(8,128)S(1)} %copy-done.1, f32[343,3136]{1,0:T(8,128)S(1)} %copy-done.1), custom_call_target="tpu_custom_call" | custom-call | flops 16777216 | bytes 10485760 | tf_op jit(solution)/shard_map/prepare/pallas_call | solution.py:553
  11.2 2.5 %copy-done = bf16[448,6400]{1,0:T(8,128)(2,1)} copy-done((bf16[448,6400]{1,0:T(8,128)(2,1)}, bf16[448,6400]{1,0:T(8,128)(2,1)S(1)}, u32[]{:S(2)}) %copy-start) | copy-done | bytes 5734424
  13.7 0.0 collective-permute-done.got_a.a1
  13.7 0.0 collective-permute-done.1.got_b.b1
  13.7 0.6 %copy-done.6 = f32[32,256]{1,0:T(8,128)} copy-done((f32[32,256]{1,0:T(8,128)}, f32[32,256]{1,0:T(8,128)S(1)}, u32[]{:S(2)}) %copy-start.6) | copy-done | bytes 32792
  14.3 0.6 %copy-done.8 = f32[32,256]{1,0:T(8,128)} copy-done((f32[32,256]{1,0:T(8,128)}, f32[32,256]{1,0:T(8,128)S(1)}, u32[]{:S(2)}) %copy-start.8) | copy-done | bytes 32792
  14.9 1.6 %pack_col.1 = (f32[56,256]{1,0:T(8,128)}, f32[56,256]{1,0:T(8,128)}) custom-call(f32[3,4,4,256]{3,2,1,0:T(4,128)} %pos.7, f32[4,4,256]{2,1,0:T(4,128)} %mass.5, s32[4,4,4]{2,1,0:T(4,128)} %counts.7, f32[4,4,224]{2,1,0:T(4,128)} %poles.5, f32[32,256]{1,0:T(8,128)} %copy-done.6, f32[32,256]{1,0:T(8,128)} %copy-done.8), custom_call_target="tpu_custom_call" | custom-call | tf_op jit(solution)/shard_map/pack_col/pallas_call | solution.py:575
  16.5 4.4 %collective-permute-start.3 = (f32[56,256]{1,0:T(8,128)}, f32[56,256]{1,0:T(8,128)S(1)}, u32[]{:S(2)}, u32[]{:S(2)}) collective-permute-start(f32[56,256]{1,0:T(8,128)} %get-tuple-element.11), channel_id=1, source_target_pairs={{1,2},{2,1},{5,6},{6,5},{9,10},{10,9},{13,14},{14,13},{17,18},{18,... | collective-permute-start | bytes 172040 | tf_op jit(solution)/shard_map/ppermute | solution.py:648
  21.0 0.0 slice-start
  21.0 0.0 slice-start.1
  21.0 0.0 copy-start.2
  21.0 0.0 copy-start.4
  21.0 0.0 copy-start.5
  21.0 0.0 copy-start.7
  21.0 0.0 copy-start.9
  21.0 0.0 copy-start.10
  21.1 0.0 copy-start.13
  21.1 0.0 copy-start.14
  21.1 0.0 copy-start.15
  21.1 0.1 collective-permute-start.2
  21.2 1.0 %copy-done.16 = f32[56,256]{1,0:T(8,128)S(1)} copy-done((f32[56,256]{1,0:T(8,128)S(1)}, f32[56,256]{1,0:T(8,128)}, u32[]{:S(2)}) %copy-start.16) | copy-done | bytes 57368
  22.2 5.2 %near_own.1 = (f32[16,256]{1,0:T(8,128)S(1)}, bf16[2048,256]{1,0:T(8,128)(2,1)S(1)}) custom-call(f32[3,4,4,256]{3,2,1,0:T(4,128)S(1)} %copy-done.3, f32[4,4,256]{2,1,0:T(4,128)S(1)} %copy-done.12, s32[4,4,4]{2,1,0:T(4,128)S(1)} %copy-done.11, f32[56,256]{1,0:T(8,128)S(1)} %copy-done.16), custom_call_target="tpu_custom_call" | custom-call | flops 4294967296 | bytes 1048576 | tf_op jit(solution)/shard_map/near_own/pallas_call | solution.py:588
  27.3 0.0 collective-permute-done.3.b2
  27.3 0.0 collective-permute-done.2.a2
  27.4 0.0 slice-done
  27.4 0.0 slice-done.1
  27.5 8.5 %fields.1 = (f32[4,4,256]{2,1,0:T(4,128)}, f32[4,4,224]{2,1,0:T(4,128)}) custom-call(f32[3,4,4,256]{3,2,1,0:T(4,128)S(1)} %copy-done.3, s32[4,4,4]{2,1,0:T(4,128)S(1)} %copy-done.11, f32[4,4,224]{2,1,0:T(4,128)S(1)} %copy-done.5, f32[32,256]{1,0:T(8,128)S(1)} %copy-done.7, f32[32,256]{1,0:T(8,128)S(1)} %copy-done.9, ...), custom_call_target="tpu_custom_call" | custom-call | tf_op jit(solution)/shard_map/fields/pallas_call | solution.py:616
  (20 shorter events, 0.0 us)
Async XLA Ops:
  2.2 11.5 %collective-permute-start = (f32[32,256]{1,0:T(8,128)}, f32[32,256]{1,0:T(8,128)S(1)}, u32[]{:S(2)}, u32[]{:S(2)}) collective-permute-start(f32[32,256]{1,0:T(8,128)} %get-tuple-element.8), channel_id=1, source_target_pairs={{0,4},{8,12},{16,20},{24,28},{4,0},{12,8},{20,16},{28,24},{1,5},{9... | collective-permute-start | bytes 98312 | tf_op jit(solution)/shard_map/ppermute | solution.py:648
  2.5 11.2 %collective-permute-start.1 = (f32[32,256]{1,0:T(8,128)}, f32[32,256]{1,0:T(8,128)S(1)}, u32[]{:S(2)}, u32[]{:S(2)}) collective-permute-start(f32[32,256]{1,0:T(8,128)} %get-tuple-element.9), channel_id=1, source_target_pairs={{4,8},{12,16},{20,24},{8,4},{16,12},{24,20},{5,9},{13,17},{21,25},... | collective-permute-start | bytes 98312 | tf_op jit(solution)/shard_map/ppermute | solution.py:648
  6.6 2.3 %copy-start.1 = (f32[343,3136]{1,0:T(8,128)S(1)}, f32[343,3136]{1,0:T(8,128)}, u32[]{:S(2)}) copy-start(f32[343,3136]{1,0:T(8,128)} %tail.1) | copy-start | bytes 12907780
  8.8 12.3 %copy-start.3 = (f32[3,4,4,256]{3,2,1,0:T(4,128)S(1)}, f32[3,4,4,256]{3,2,1,0:T(4,128)}, u32[]{:S(2)}) copy-start(f32[3,4,4,256]{3,2,1,0:T(4,128)} %pos.7) | copy-start | bytes 147460
  8.8 12.3 %copy-start.11 = (s32[4,4,4]{2,1,0:T(4,128)S(1)}, s32[4,4,4]{2,1,0:T(4,128)}, u32[]{:S(2)}) copy-start(s32[4,4,4]{2,1,0:T(4,128)} %counts.7) | copy-start | bytes 772
  8.9 12.3 %copy-start.12 = (f32[4,4,256]{2,1,0:T(4,128)S(1)}, f32[4,4,256]{2,1,0:T(4,128)}, u32[]{:S(2)}) copy-start(f32[4,4,256]{2,1,0:T(4,128)} %mass.5) | copy-start | bytes 49156
  11.2 2.5 %copy-start = (bf16[448,6400]{1,0:T(8,128)(2,1)}, bf16[448,6400]{1,0:T(8,128)(2,1)S(1)}, u32[]{:S(2)}) copy-start(bf16[448,6400]{1,0:T(8,128)(2,1)S(1)} %prepare.1.table_far) | copy-start | bytes 17203204
  13.7 0.6 %copy-start.6 = (f32[32,256]{1,0:T(8,128)}, f32[32,256]{1,0:T(8,128)S(1)}, u32[]{:S(2)}) copy-start(f32[32,256]{1,0:T(8,128)S(1)} %collective-permute-done.got_a.a1) | copy-start | bytes 98308
  14.3 0.6 %copy-start.8 = (f32[32,256]{1,0:T(8,128)}, f32[32,256]{1,0:T(8,128)S(1)}, u32[]{:S(2)}) copy-start(f32[32,256]{1,0:T(8,128)S(1)} %collective-permute-done.1.got_b.b1) | copy-start | bytes 98308
  16.5 10.8 %collective-permute-start.3 = (f32[56,256]{1,0:T(8,128)}, f32[56,256]{1,0:T(8,128)S(1)}, u32[]{:S(2)}, u32[]{:S(2)}) collective-permute-start(f32[56,256]{1,0:T(8,128)} %get-tuple-element.11), channel_id=1, source_target_pairs={{1,2},{2,1},{5,6},{6,5},{9,10},{10,9},{13,14},{14,13},{17,18},{18,... | collective-permute-start | bytes 172040 | tf_op jit(solution)/shard_map/ppermute | solution.py:648
  21.0 6.4 %slice-start = ((s8[5734400]{0:T(1024)(128)(4,1)}), s8[4194304]{0:T(1024)(128)(4,1)S(1)}, s32[]{:S(2)}) async-start(s8[5734400]{0:T(1024)(128)(4,1)} %bitcast), calls=%async_computation | async-start | bytes 8388608
  21.0 6.4 %slice-start.1 = ((s8[5734400]{0:T(1024)(128)(4,1)}), s8[1540096]{0:T(1024)(128)(4,1)S(1)}, s32[]{:S(2)}) async-start(s8[5734400]{0:T(1024)(128)(4,1)} %bitcast), calls=%async_computation.1 | async-start | bytes 3080192
  21.0 6.4 %copy-start.2 = (bf16[256,2048]{1,0:T(8,128)(2,1)S(1)}, bf16[256,2048]{1,0:T(8,128)(2,1)}, u32[]{:S(2)}) copy-start(bf16[256,2048]{1,0:T(8,128)(2,1)} %constant.6.clone.pick) | copy-start | bytes 3145732
  21.0 6.4 %copy-start.4 = (f32[8,56,56]{2,1,0:T(8,128)S(1)}, f32[8,56,56]{2,1,0:T(8,128)}, u32[]{:S(2)}) copy-start(f32[8,56,56]{2,1,0:T(8,128)} %l2l.1) | copy-start | bytes 301060
  21.0 6.4 %copy-start.5 = (f32[4,4,224]{2,1,0:T(4,128)S(1)}, f32[4,4,224]{2,1,0:T(4,128)}, u32[]{:S(2)}) copy-start(f32[4,4,224]{2,1,0:T(4,128)} %poles.5) | copy-start | bytes 43012
  21.0 6.4 %copy-start.7 = (f32[32,256]{1,0:T(8,128)S(1)}, f32[32,256]{1,0:T(8,128)}, u32[]{:S(2)}) copy-start(f32[32,256]{1,0:T(8,128)} %copy-done.6) | copy-start | bytes 98308
  21.0 6.4 %copy-start.9 = (f32[32,256]{1,0:T(8,128)S(1)}, f32[32,256]{1,0:T(8,128)}, u32[]{:S(2)}) copy-start(f32[32,256]{1,0:T(8,128)} %copy-done.8) | copy-start | bytes 98308
  21.0 6.4 %copy-start.10 = (f32[3,64,128]{2,1,0:T(8,128)S(1)}, f32[3,64,128]{2,1,0:T(8,128)}, u32[]{:S(2)}) copy-start(f32[3,64,128]{2,1,0:T(8,128)} %constant.8.clone.points) | copy-start | bytes 294916
  21.1 6.4 %copy-start.13 = (f32[64,64]{1,0:T(8,128)S(1)}, f32[64,64]{1,0:T(8,128)}, u32[]{:S(2)}) copy-start(f32[64,64]{1,0:T(8,128)} %constant.7.clone.spread) | copy-start | bytes 49156
  21.1 6.4 %copy-start.14 = (f32[56,56]{1,0:T(8,128)S(1)}, f32[56,56]{1,0:T(8,128)}, u32[]{:S(2)}) copy-start(f32[56,56]{1,0:T(8,128)} %c2e.1) | copy-start | bytes 37636
  21.1 6.4 %copy-start.15 = (f32[2,2,112]{2,1,0:T(2,128)S(1)}, f32[2,2,112]{2,1,0:T(2,128)}, u32[]{:S(2)}) copy-start(f32[2,2,112]{2,1,0:T(2,128)} %parents.1) | copy-start | bytes 5380
  21.1 6.3 %collective-permute-start.2 = (f32[56,256]{1,0:T(8,128)}, f32[56,256]{1,0:T(8,128)S(1)}, u32[]{:S(2)}, u32[]{:S(2)}) collective-permute-start(f32[56,256]{1,0:T(8,128)} %get-tuple-element.10.after), channel_id=1, source_target_pairs={{0,1},{2,3},{1,0},{3,2},{4,5},{6,7},{5,4},{7,6},{8,9},{10,11},{9,8... | collective-permute-start | bytes 172040 | tf_op jit(solution)/shard_map/ppermute | solution.py:648
  21.2 1.0 %copy-start.16 = (f32[56,256]{1,0:T(8,128)S(1)}, f32[56,256]{1,0:T(8,128)}, u32[]{:S(2)}) copy-start(f32[56,256]{1,0:T(8,128)} %get-tuple-element.10.after) | copy-start | bytes 172036

commit v3 on v2

--- a/solution.py
+++ b/solution.py
@@ -65,70 +65,79 @@
     return lax.axis_index(axis) % 2 == 1
 
 
-def store_pair(odd, to_first_pair, to_second_pair, rows, lanes, low_edge, high_edge):
-    to_first_pair[rows, lanes] = jnp.where(odd, low_edge, high_edge)
-    to_second_pair[rows, lanes] = jnp.where(odd, high_edge, low_edge)
-
-
-def pack_row_kernel(dims, pos, mass, counts, poles, send_a, send_b):
-    sx, sy, sz = dims
-    odd = is_odd("row")
-    store = functools.partial(store_pair, odd, send_a, send_b)
-    every = slice(0, sz * CAP)
+def pack_row_kernel(
+    dims, pos_far, mass_far, counts_far, poles_far, send_a, send_b, own,
+    pos, mass, counts, poles, sems,
+):
+    sx, sy, sz = dims
+    cols = sx * sy
+    copies = [
+        pltpu.make_async_copy(far, near, sems.at[i])
+        for i, (far, near) in enumerate(
+            ((counts_far, counts), (pos_far, pos), (mass_far, mass), (poles_far, poles))
+        )
+    ]
+    for copy in copies:
+        copy.start()
+    own[...] = jnp.zeros_like(own)
     send_a[...] = jnp.zeros_like(send_a)
     send_b[...] = jnp.zeros_like(send_b)
-    for x in range(REACH):
-        store(slice(x * sy, (x + 1) * sy), slice(0, sz * Q), poles[x], poles[sx - REACH + x])
+    for copy in copies:
+        copy.wait()
+    for x in range(sx):
+        at = x * sy
+        for c in range(3):
+            own[c * cols + at : c * cols + at + sy, :] = pos[c, x] - 0.5
+        for y in range(sy):
+            row = 3 * cols + at + y
+            own[row : row + 1, :] = column_weights(mass[x, y : y + 1, :], counts, x, y, sz)
+        own[4 * cols + at : 4 * cols + at + sy, 0 : sz * Q] = poles[x]
+    odd = is_odd("row")
+    pieces = [(4 * cols, 4 * cols + (sx - REACH) * sy, REACH * sy, 0)]
     base = REACH * sy
-    for c in range(3):
-        rows = slice(base + c * sy, base + (c + 1) * sy)
-        store(rows, every, pos[c, 0] - 0.5, pos[c, sx - 1] - 0.5)
-    for y in range(sy):
-        row = base + 3 * sy + y
-        store(
-            slice(row, row + 1),
-            every,
-            column_weights(mass[0, y : y + 1, :], counts, 0, y, sz),
-            column_weights(mass[sx - 1, y : y + 1, :], counts, sx - 1, y, sz),
-        )
-
-
-def pack_col_kernel(dims, pos, mass, counts, poles, got_a, got_b, send_a, send_b, low, high):
-    sx, sy, sz = dims
-    odd_row = is_odd("row")
+    for c in range(4):
+        pieces.append((c * cols, c * cols + (sx - 1) * sy, sy, base + c * sy))
+    for low, high, rows, at in pieces:
+        low_edge, high_edge = own[low : low + rows, :], own[high : high + rows, :]
+        send_a[at : at + rows, :] = jnp.where(odd, low_edge, high_edge)
+        send_b[at : at + rows, :] = jnp.where(odd, high_edge, low_edge)
+
+
+def pack_col_kernel(dims, own, got_a, got_b, token, send_a, send_b, next_token, low, high):
+    sx, sy, sz = dims
+    cols = sx * sy
+    odd_row, odd_col = is_odd("row"), is_odd("col")
+    next_token[...] = token[...]
     low[...] = jnp.where(odd_row, got_a[...], got_b[...])
     high[...] = jnp.where(odd_row, got_b[...], got_a[...])
-    store = functools.partial(store_pair, is_odd("col"), send_a, send_b)
-    every = slice(0, sz * CAP)
     base_in = REACH * sy
     base = REACH * (sx + 2 * REACH)
     px = sx + 2
     send_a[...] = jnp.zeros_like(send_a)
     send_b[...] = jnp.zeros_like(send_b)
+
+    def store(at, rows, ref, start):
+        low_edge = ref[start : start + rows, :]
+        high_edge = ref[start + sy - rows : start + sy, :]
+        send_a[at : at + rows, :] = jnp.where(odd_col, low_edge, high_edge)
+        send_b[at : at + rows, :] = jnp.where(odd_col, high_edge, low_edge)
+
     for x in range(sx + 2 * REACH):
-        rows = slice(x * REACH, (x + 1) * REACH)
         if REACH <= x < REACH + sx:
-            own = poles.at[x - REACH]
-            store(rows, slice(0, sz * Q), own[0:REACH, :], own[sy - REACH : sy, :])
+            store(x * REACH, REACH, own, 4 * cols + (x - REACH) * sy)
+        elif x < REACH:
+            store(x * REACH, REACH, low, x * sy)
         else:
-            ref, at = (low, x * sy) if x < REACH else (high, (x - REACH - sx) * sy)
-            store(rows, every, ref[at : at + REACH, :], ref[at + sy - REACH : at + sy, :])
+            store(x * REACH, REACH, high, (x - REACH - sx) * sy)
     for c in range(4):
         for x in range(px):
-            edges = []
-            for y in (0, sy - 1):
-                at = base_in + c * sy + y
-                if x == 0:
-                    row = low[at : at + 1, :]
-                elif x == px - 1:
-                    row = high[at : at + 1, :]
-                elif c < 3:
-                    row = pos[c, x - 1, y : y + 1, :] - 0.5
-                else:
-                    row = column_weights(mass[x - 1, y : y + 1, :], counts, x - 1, y, sz)
-                edges.append(row)
             at = base + c * px + x
-            store(slice(at, at + 1), every, *edges)
+            if x == 0:
+                store(at, 1, low, base_in + c * sy)
+            elif x == px - 1:
+                store(at, 1, high, base_in + c * sy)
+            else:
+                store(at, 1, own, c * cols + (x - 1) * sy)
 
 
 def gather_constant(dims):
@@ -164,22 +173,17 @@
     return pick
 
 
-def prepare_kernel(ops, tail, table, raw, made, sems, out_sems):
+def prepare_kernel(ops, tail, token, table, raw, sems):
     width = ops.shape[1]
     tiles = raw.shape[0]
-    whole = width // LANES
+    whole = tiles - 1
 
     def fetch(j):
         return pltpu.make_async_copy(ops.at[:, pl.ds(j * LANES, LANES)], raw.at[j], sems.at[j])
 
-    def put(j):
-        lanes = pl.ds(2 * j * LANES, 2 * LANES)
-        return pltpu.make_async_copy(made.at[:, lanes], table.at[:, lanes], out_sems.at[j])
-
     for j in range(whole):
         fetch(j).start()
-    if whole < tiles:
-        raw[whole] = tail[...]
+    raw[tiles - 1] = tail[...]
     ab = lax.broadcasted_iota(jnp.int32, (64, LANES), 0)
     closeby = (jnp.abs(ab // SPAN - REACH) <= 1) & (jnp.abs(ab % SPAN - REACH) <= 1)
     for j in range(tiles):
@@ -196,62 +200,74 @@
                 lane = lax.broadcasted_iota(jnp.int32, (64, LANES), 1)
                 block = jnp.where(lane < width - j * LANES, block, 0.0)
             hi, lo = split2(block)
-            made[c * 64 : (c + 1) * 64, 2 * j * LANES : (2 * j + 1) * LANES] = hi
-            made[c * 64 : (c + 1) * 64, (2 * j + 1) * LANES : (2 * j + 2) * LANES] = lo
-        put(j).start()
-    for j in range(tiles):
-        put(j).wait()
-
-
-def build_sources(sz, place, su, feats, lhs, columns):
-    for i in range(su.shape[1] // 8):
-        at = i * 8
+            table[c * 64 : (c + 1) * 64, 2 * j * LANES : (2 * j + 1) * LANES] = hi
+            table[c * 64 : (c + 1) * 64, (2 * j + 1) * LANES : (2 * j + 2) * LANES] = lo
+
+
+def fill_features(sz, place, su, feats, at):
+    for half in range(2):
+        rows = lax.broadcasted_iota(jnp.int32, (8, LANES), 0) + at
+        lane = lax.broadcasted_iota(jnp.int32, (8, LANES), 1) + half * LANES
+        lanes = slice(half * LANES, (half + 1) * LANES)
+        arrays = [su[c][at : at + 8, lanes] for c in range(4)]
+        for k, value in source_features_at(sz, place(rows), arrays, lane):
+            feats[half, pl.ds(at * KROWS + k, 8, stride=KROWS), :] = value
+
+
+def turn_features(feats, lhs, i):
+    for half in range(2):
+        block = feats[half, i * KROWS : i * KROWS + LANES, :]
+        at = (2 * i + half) * LANES
+        lhs[at : at + LANES, :] = block.T.astype(BF16)
+
+
+def near_sums(sz, lhs, rhs, total, src, targets):
+    halves = [[h for h in range(2) if any(abs(z - t) <= 1 for t in (2 * h, 2 * h + 1))] for z in range(sz)]
+
+    def add(target, half, d2):
+        part = jnp.sum(lax.rsqrt(d2).reshape(d2.shape[0] // 8, 8, LANES), axis=0)
+        at, lanes = slice(target * 8, (target + 1) * 8), slice(half * LANES, (half + 1) * LANES)
+        total[at, lanes] = total[at, lanes] + part
+
+    def operand(target, half):
+        return rhs[target * LANES : (target + 1) * LANES, half * LANES : (half + 1) * LANES]
+
+    base = src * sz * CAP
+    middle = [z for z in range(sz) if len(halves[z]) == 2]
+    rows = slice(base + middle[0] * CAP, base + (middle[-1] + 1) * CAP)
+    for target in targets:
+        d2 = dot(lhs[rows, :], rhs[target * LANES : (target + 1) * LANES, :])
         for half in range(2):
-            rows = lax.broadcasted_iota(jnp.int32, (8, LANES), 0) + at
-            lane = lax.broadcasted_iota(jnp.int32, (8, LANES), 1) + half * LANES
-            lanes = slice(half * LANES, (half + 1) * LANES)
-            arrays = [su[c, at : at + 8, lanes] for c in range(4)]
-            for k, value in source_features_at(sz, place(rows), arrays, lane):
-                feats[half, pl.ds(at * KROWS + k, 8, stride=KROWS), :] = value
-    for i in range(columns):
-        for half in range(2):
-            block = feats[half, i * KROWS : i * KROWS + LANES, :]
-            at = (2 * i + half) * LANES
-            lhs[at : at + LANES, :] = block.T.astype(BF16)
-
-
-def near_sums(sz, lhs, rhs, sources):
-    total = [jnp.zeros((8, LANES), F32) for _ in range(2)]
-    for src in sources:
-        for z in range(sz):
-            rows = src * sz * CAP + z * CAP
-            d2 = dot(lhs[rows : rows + CAP, :], rhs)
-            for half in range(2):
-                if any(abs(z - t) <= 1 for t in (2 * half, 2 * half + 1)):
-                    part = lax.rsqrt(d2[:, half * LANES : (half + 1) * LANES])
-                    total[half] = total[half] + jnp.sum(
-                        part.reshape(CAP // 8, 8, LANES), axis=0
-                    )
-    return jnp.concatenate([jnp.sum(part, axis=0, keepdims=True) for part in total], axis=1)
-
-
-def near_own_kernel(dims, pos, mass, counts, after, near, rhs, su, feats, lhs, rfeats):
+            add(target, half, d2[:, half * LANES : (half + 1) * LANES])
+    for z in range(sz):
+        if len(halves[z]) == 2:
+            continue
+        half = halves[z][0]
+        rows = slice(base + z * CAP, base + (z + 1) * CAP)
+        for i in range(0, len(targets), 2):
+            both = targets[i : i + 2]
+            wide = jnp.concatenate([operand(t, half) for t in both], axis=1)
+            d2 = dot(lhs[rows, :], wide)
+            for n, target in enumerate(both):
+                add(target, half, d2[:, n * LANES : (n + 1) * LANES])
+
+
+def near_own_kernel(dims, own, near, rhs, token, feats, lhs, rfeats):
     sx, sy, sz = dims
     cols = sx * sy
-    for x in range(sx):
-        for c in range(3):
-            su[c, x * sy : (x + 1) * sy, :] = pos[c, x] - 0.5
-        for y in range(sy):
-            row = x * sy + y
-            su[3, row : row + 1, :] = column_weights(mass[x, y : y + 1, :], counts, x, y, sz)
-
-    build_sources(sz, lambda rows: (rows // sy + 1, rows % sy + 1), su, feats, lhs, cols)
+    token[...] = own[0:8, 0:LANES]
+    su = [own.at[c * cols : (c + 1) * cols] for c in range(4)]
+
+    for at in range(0, cols, 8):
+        fill_features(sz, lambda rows: (rows // sy + 1, rows % sy + 1), su, feats, at)
+    for i in range(cols):
+        turn_features(feats, lhs, i)
     for half in range(2):
         lanes = slice(half * LANES, (half + 1) * LANES)
         for at in range(0, cols, 8):
             rows = lax.broadcasted_iota(jnp.int32, (8, LANES), 0) + at
             lane = lax.broadcasted_iota(jnp.int32, (8, LANES), 1) + half * LANES
-            arrays = [su[c, at : at + 8, lanes] for c in range(3)]
+            arrays = [su[c][at : at + 8, lanes] for c in range(3)]
             for k, value in target_features_at(dims, arrays, rows, lane):
                 rfeats[half, pl.ds(at * KROWS + k, 8, stride=KROWS), :] = value
     for i in range(cols):
@@ -259,37 +275,28 @@
             rhs[i * LANES : (i + 1) * LANES, half * LANES : (half + 1) * LANES] = rfeats[
                 half, i * KROWS : i * KROWS + LANES, :
             ].astype(BF16)
+    near[...] = jnp.zeros_like(near)
     for x in range(sx):
         for y in range(sy):
-            i = x * sy + y
-            sources = [
+            targets = [
                 a * sy + b
                 for a in range(max(x - 1, 0), min(x + 2, sx))
                 for b in range(max(y - 1, 0), min(y + 2, sy))
             ]
-            near[i : i + 1, :] = near_sums(
-                sz, lhs, rhs[i * LANES : (i + 1) * LANES, :], sources
-            )
+            near_sums(sz, lhs, rhs, near, x * sy + y, targets)
 
 
 def fields_kernel(
     dims,
-    pos, counts, poles, a1, b1, a2, b2, near_own, rhs_far, table_far, parents, l2l, c2e, pick,
+    own, a1, b1, a2, b2, near_own, rhs, table, parents, l2l, c2e, pick,
     spread, points,
     potential, local_out,
-    su, feats, lhs, rhs, near, sm, picked, lm, table, dens, sems,
+    halo_slots, feats, lhs, near, sm, picked, lm, dens,
 ):
     sx, sy, sz = dims
     hx, hy = sx + 2, sy + 2
     cols = sx * sy
     tiles = table.shape[1] // (2 * LANES)
-    width = Q * Q
-
-    get_rhs = pltpu.make_async_copy(rhs_far, rhs, sems.at[0])
-    get_table = pltpu.make_async_copy(table_far, table, sems.at[1])
-    get_rhs.start()
-    get_table.start()
-
     odd_row, odd_col = is_odd("row"), is_odd("col")
     base1 = REACH * sy
     base2 = REACH * (sx + 2 * REACH)
@@ -300,17 +307,17 @@
         for first, second in ((got_a, got_b), (got_b, got_a)):
             sides.append((odd, first, second, base, line))
 
-    su[...] = jnp.zeros_like(su)
+    su = [halo_slots.at[c] for c in range(4)]
+    halo_slots[...] = jnp.zeros_like(halo_slots)
     sm[...] = jnp.zeros_like(sm)
-    for x in range(sx):
-        sm[x * sy : (x + 1) * sy, 0 : sz * Q] = poles[x]
+    sm[0:cols, :] = own[4 * cols : 5 * cols, :]
     to, to_poles = 0, cols
     for odd, first, second, base, line in sides:
         value = jnp.where(odd, first[...], second[...])
         sm[to_poles : to_poles + base, :] = value[0:base, :]
         to_poles += base
         for c in range(4):
-            su[c, to : to + line, :] = value[base + c * line : base + (c + 1) * line, :]
+            su[c][to : to + line, :] = value[base + c * line : base + (c + 1) * line, :]
         to += line
 
     def place(rows):
@@ -327,18 +334,6 @@
     halo.update({(hx - 1, y + 1): sy + y for y in range(sy)})
     halo.update({(x, 0): 2 * sy + x for x in range(hx)})
     halo.update({(x, hy - 1): 2 * sy + hx + x for x in range(hx)})
-    build_sources(sz, place, su, feats, lhs, len(halo))
-    get_rhs.wait()
-    for x in range(sx):
-        for y in range(sy):
-            i = x * sy + y
-            cells = [(x + dx, y + dy) for dx in range(3) for dy in range(3)]
-            sources = [halo[cell] for cell in cells if cell in halo]
-            value = near_own[i : i + 1, :]
-            if sources:
-                value = value + near_sums(sz, lhs, rhs[i * LANES : (i + 1) * LANES, :], sources)
-            near[i : i + 1, :] = value
-
     for pair in range(sz // 2):
         his, los = [], []
         for zi in range(2):
@@ -358,11 +353,18 @@
                     :, i * LANES : (i + 1) * LANES
                 ]
 
-    get_table.wait()
     period = 16
     lane16 = lax.broadcasted_iota(jnp.int32, (cols, LANES), 1)
     check = [jnp.zeros((cols, LANES), F32) for _ in range(sz)]
-    for t in range(period * Q // LANES):
+    groups = list(range(0, halo_slots.shape[1], 8))
+    turns = list(range(len(halo)))
+    spans = period * Q // LANES
+    for t in range(spans):
+        if groups:
+            fill_features(sz, place, su, feats, groups.pop(0))
+        else:
+            for _ in range(-(-len(turns) // (spans - t))):
+                turn_features(feats, lhs, turns.pop(0))
         members = [s for s in range(period) if s * Q < (t + 1) * LANES and (s + 1) * Q > t * LANES]
         rows = len(members) * cols
         left = []
@@ -404,6 +406,8 @@
                 part = jnp.where((lane16 >= offset) & (lane16 < offset + Q), part, 0.0)
                 check[z] = check[z] + pltpu.roll(part, (-offset) % LANES, 1)
 
+    assert not groups and not turns
+
     rows = []
     for pz in range(sz // 2):
         for x in range(sx // 2):
@@ -431,22 +435,38 @@
     row = lax.broadcasted_iota(jnp.int32, (2 * sz * cols, sz * CAP), 0) % (sz * cols)
     lane = lax.broadcasted_iota(jnp.int32, (2 * sz * cols, sz * CAP), 1)
     owner = row - (lane // CAP) * cols
-    for x in range(sx):
-        for y in range(sy):
-            one_hot = jnp.where(owner == x * sy + y, 1.0, 0.0).astype(BF16)
-            spread_out = dot(weights, one_hot)
-            sums = []
-            for half in range(2):
-                lanes = slice(half * LANES, (half + 1) * LANES)
-                d2 = jnp.zeros((64, LANES), F32)
-                for c in range(3):
-                    gap = pos[c, x, y : y + 1, lanes] - points[c]
-                    d2 = d2 + gap * gap
-                part = spread_out[:, lanes] * lax.rsqrt(d2)
-                sums.append(jnp.sum(part, axis=0, keepdims=True))
-            i = x * sy + y
-            value = near[i : i + 1, :] + jnp.concatenate(sums, axis=1)
-            potential[x, y : y + 1, :] = column_weights(value, counts, x, y, sz)
+
+    def far(i):
+        one_hot = jnp.where(owner == i, 1.0, 0.0).astype(BF16)
+        spread_out = dot(weights, one_hot)
+        for half in range(2):
+            lanes = slice(half * LANES, (half + 1) * LANES)
+            d2 = jnp.zeros((64, LANES), F32)
+            for c in range(3):
+                gap = own[c * cols + i : c * cols + i + 1, lanes] - points[c]
+                d2 = d2 + gap * gap
+            part = spread_out[:, lanes] * lax.rsqrt(d2)
+            at = slice(i * 8, (i + 1) * 8)
+            near[at, lanes] = near[at, lanes] + jnp.sum(part.reshape(8, 8, LANES), axis=0)
+
+    near[...] = near_own[...]
+    left = list(range(cols))
+    for cell, src in halo.items():
+        targets = [
+            x * sy + y
+            for x in range(sx)
+            for y in range(sy)
+            if 0 <= cell[0] - x <= 2 and 0 <= cell[1] - y <= 2
+        ]
+        if left:
+            far(left.pop(0))
+        near_sums(sz, lhs, rhs, near, src, targets)
+    assert not left
+    for i in range(cols):
+        x, y = i // sy, i % sy
+        value = jnp.sum(near[i * 8 : (i + 1) * 8, :], axis=0, keepdims=True)
+        live = own[3 * cols + i : 3 * cols + i + 1, :] > 0
+        potential[x, y : y + 1, :] = jnp.where(live, value, 0.0)
 
 
 def source_features_at(sz, place, arrays, lane):
@@ -527,7 +547,7 @@
 
 VMEM = pl.BlockSpec(memory_space=pltpu.VMEM)
 SMEM = pl.BlockSpec(memory_space=pltpu.SMEM)
-ANY = pl.BlockSpec(memory_space=pl.ANY)
+HBM = pl.BlockSpec(memory_space=pltpu.HBM)
 
 
 def round_up(n, m):
@@ -536,107 +556,109 @@
 
 def pack_row(dims, pos, mass, counts, poles):
     sx, sy, sz = dims
-    rows = round_up((REACH + 4) * sy, 8)
-    shape = jax.ShapeDtypeStruct((rows, sz * CAP), F32)
+    shape = jax.ShapeDtypeStruct((round_up((REACH + 4) * sy, 8), sz * CAP), F32)
     return pl.pallas_call(
         functools.partial(pack_row_kernel, dims),
-        out_shape=(shape, shape),
-        in_specs=[VMEM, VMEM, SMEM, VMEM],
-        out_specs=(VMEM, VMEM),
+        out_shape=(shape, shape, jax.ShapeDtypeStruct((5 * sx * sy, sz * CAP), F32)),
+        in_specs=[HBM] * 4,
+        out_specs=(VMEM,) * 3,
+        scratch_shapes=[
+            pltpu.VMEM(pos.shape, F32),
+            pltpu.VMEM(mass.shape, F32),
+            pltpu.SMEM(counts.shape, jnp.int32),
+            pltpu.VMEM(poles.shape, F32),
+            pltpu.SemaphoreType.DMA((4,)),
+        ],
         name="pack_row",
     )(pos, mass, counts, poles)
 
 
-def prepare(ops):
+def prepare(ops, token):
     rows, width = ops.shape
     tiles = -(-width // LANES)
+    tail = jnp.pad(ops[:, (tiles - 1) * LANES :], ((0, 0), (0, tiles * LANES - width)))
     return pl.pallas_call(
         prepare_kernel,
-        grid=(1,),
         out_shape=jax.ShapeDtypeStruct((SPAN * 64, 2 * tiles * LANES), BF16),
-        in_specs=[ANY, pl.BlockSpec((rows, LANES), lambda _: (0, tiles - 1))],
-        out_specs=ANY,
+        in_specs=[HBM, VMEM, VMEM],
+        out_specs=VMEM,
         scratch_shapes=[
             pltpu.VMEM((tiles, rows, LANES), F32),
-            pltpu.VMEM((SPAN * 64, 2 * tiles * LANES), BF16),
-            pltpu.SemaphoreType.DMA((tiles,)),
             pltpu.SemaphoreType.DMA((tiles,)),
         ],
-        compiler_params=pltpu.CompilerParams(vmem_limit_bytes=20 << 20),
+        compiler_params=pltpu.CompilerParams(vmem_limit_bytes=12 << 20),
         cost_estimate=pl.CostEstimate(flops=1 << 24, bytes_accessed=10 << 20, transcendentals=0),
         name="prepare",
-    )(ops, ops)
-
-
-def pack_col(dims, pos, mass, counts, poles, got_a, got_b):
+    )(ops, tail, token)
+
+
+def pack_col(dims, own, got_a, got_b, token):
     sx, sy, sz = dims
     rows = round_up(REACH * (sx + 2 * REACH) + 4 * (sx + 2), 8)
     shape = jax.ShapeDtypeStruct((rows, sz * CAP), F32)
     return pl.pallas_call(
         functools.partial(pack_col_kernel, dims),
-        out_shape=(shape, shape),
-        in_specs=[VMEM, VMEM, SMEM, VMEM, VMEM, VMEM],
-        out_specs=(VMEM, VMEM),
+        out_shape=(shape, shape, jax.ShapeDtypeStruct(token.shape, F32)),
+        in_specs=[VMEM] * 4,
+        out_specs=(VMEM,) * 3,
         scratch_shapes=[pltpu.VMEM(got_a.shape, F32), pltpu.VMEM(got_a.shape, F32)],
+        compiler_params=pltpu.CompilerParams(vmem_limit_bytes=2 << 20),
         name="pack_col",
-    )(pos, mass, counts, poles, got_a, got_b)
-
-
-def near_own(dims, pos, mass, counts, after):
+    )(own, got_a, got_b, token)
+
+
+def near_own(dims, own):
     sx, sy, sz = dims
     cols = sx * sy
     return pl.pallas_call(
         functools.partial(near_own_kernel, dims),
         out_shape=(
-            jax.ShapeDtypeStruct((cols, sz * CAP), F32),
+            jax.ShapeDtypeStruct((cols * 8, sz * CAP), F32),
             jax.ShapeDtypeStruct((cols * LANES, sz * CAP), BF16),
+            jax.ShapeDtypeStruct((8, LANES), F32),
         ),
-        in_specs=[VMEM, VMEM, SMEM, ANY],
-        out_specs=(VMEM, VMEM),
+        in_specs=[VMEM],
+        out_specs=(VMEM,) * 3,
         scratch_shapes=[
-            pltpu.VMEM((4, cols, sz * CAP), F32),
             pltpu.VMEM((2, cols * KROWS, LANES), F32),
             pltpu.VMEM((cols * sz * CAP, LANES), BF16),
             pltpu.VMEM((2, cols * KROWS, LANES), F32),
         ],
-        compiler_params=pltpu.CompilerParams(vmem_limit_bytes=20 << 20),
+        compiler_params=pltpu.CompilerParams(vmem_limit_bytes=10 << 20),
         cost_estimate=pl.CostEstimate(flops=1 << 32, bytes_accessed=1 << 20, transcendentals=1 << 22),
         name="near_own",
-    )(pos, mass, counts, after)
-
-
-def fields(dims, pos, counts, poles, a1, b1, a2, b2, near, rhs, table, parents, l2l, c2e):
+    )(own)
+
+
+def fields(dims, own, a1, b1, a2, b2, near, rhs, table, parents, l2l, c2e):
     sx, sy, sz = dims
     cols = sx * sy
     ring = 2 * sy + 2 * (sx + 2)
     pick = jnp.asarray(gather_constant(dims), BF16)
     spread = jnp.asarray(spread_constant(dims))
     points = np.full((3, 64, LANES), 10.0, np.float32)
-    points[:, :Q, :] = surface_points().T[:, :, None]
+    points[:, :Q, :] = surface_points().T[:, :, None] - 0.5
     return pl.pallas_call(
         functools.partial(fields_kernel, dims),
         out_shape=(
             jax.ShapeDtypeStruct((sx, sy, sz * CAP), F32),
             jax.ShapeDtypeStruct((sx, sy, sz * Q), F32),
         ),
-        in_specs=[VMEM, SMEM] + [VMEM] * 6 + [ANY, ANY] + [VMEM] * 6,
+        in_specs=[VMEM] * 14,
         out_specs=(VMEM, VMEM),
         scratch_shapes=[
             pltpu.VMEM((4, round_up(ring, 8), sz * CAP), F32),
             pltpu.VMEM((2, round_up(ring, 8) * KROWS, LANES), F32),
             pltpu.VMEM((ring * sz * CAP, LANES), BF16),
-            pltpu.VMEM(rhs.shape, BF16),
-            pltpu.VMEM((cols, sz * CAP), F32),
+            pltpu.VMEM((cols * 8, sz * CAP), F32),
             pltpu.VMEM((LANES, 2 * LANES), F32),
             pltpu.VMEM((LANES, 2 * LANES), BF16),
             pltpu.VMEM((sz // 2, 2 * 64 * cols, LANES), F32),
-            pltpu.VMEM(table.shape, BF16),
             pltpu.VMEM((LANES, LANES), F32),
-            pltpu.SemaphoreType.DMA((2,)),
         ],
-        compiler_params=pltpu.CompilerParams(vmem_limit_bytes=30 << 20),
+        compiler_params=pltpu.CompilerParams(vmem_limit_bytes=16 << 20),
         name="fields",
-    )(pos, counts, poles, a1, b1, a2, b2, near, rhs, table, parents, l2l, c2e, pick, spread,
+    )(own, a1, b1, a2, b2, near, rhs, table, parents, l2l, c2e, pick, spread,
       jnp.asarray(points))
 
 
@@ -652,14 +674,14 @@
 def body(positions, masses, counts, multipoles, parent_local, m2l_ops, l2l_ops, check_to_equiv):
     sx, sy, slots = masses.shape
     dims = (sx, sy, slots // CAP)
-    table = prepare(m2l_ops)
-    a1, b1 = exchange(*pack_row(dims, positions, masses, counts, multipoles), "row")
-    send = pack_col(dims, positions, masses, counts, multipoles, a1, b1)
-    a2, b2 = exchange(*send, "col")
-    near, rhs = near_own(dims, positions, masses, counts, send[0])
+    send_a, send_b, own = pack_row(dims, positions, masses, counts, multipoles)
+    a1, b1 = exchange(send_a, send_b, "row")
+    near, rhs, token = near_own(dims, own)
+    send_a, send_b, token = pack_col(dims, own, a1, b1, token)
+    a2, b2 = exchange(send_a, send_b, "col")
+    table = prepare(m2l_ops, token)
     return fields(
-        dims, positions, counts, multipoles, a1, b1, a2, b2, near, rhs, table,
-        parent_local, l2l_ops, check_to_equiv,
+        dims, own, a1, b1, a2, b2, near, rhs, table, parent_local, l2l_ops, check_to_equiv
     )
 
 

time: 36.5 us -> 24.7 us (0.68)
  Pallas kernels: 19.2 us -> 13.1 us
  local copies, waits for them, and re-layouts: 6.94 us -> 0.95 us
  waiting for transfers between devices: 0.01 us -> 0.64 us
    unnamed x38 -> x18, local copies, waits for them, and re-layouts: 6.94 us -> 0.93 us
    pallas_call x1, Pallas kernels: 8.47 us -> 6.21 us  [fields(): pl.pallas_call(functools.partial(fields_kernel, dims), out_shape=(jax.Sha...]
    pallas_call x1, Pallas kernels: 1.65 us -> 0.07 us  [pack_col(): pl.pallas_call(functools.partial(pack_col_kernel, dims), out_shape=(shape...]
    pallas_call x1, Pallas kernels: 5.16 us -> 3.62 us  [near_own(): pl.pallas_call(functools.partial(near_own_kernel, dims), out_shape=(jax.S...]
    pallas_call x1, Pallas kernels: 2.33 us -> 1.6 us  [prepare(): pl.pallas_call(prepare_kernel, out_shape=jax.ShapeDtypeStruct((SPAN * 64,...]
    ppermute x4, waiting for transfers between devices: 0.01 us -> 0.64 us  [exchange(): got.append(lax.ppermute(value, axis, pairs + [(b, a) for a, b in pairs]))]
  transfers between devices with their start and end apart: 4 -> 4, of which waited for: 0 -> 1; matrix products, arithmetic and copies ran while one was open for 0% -> 0% of each run, Pallas kernels for 21% -> 21%
where the time goes in v3:
time: 24.7 us; the launch traced here: 24.4 us
  Pallas kernels  13.1 us (53%)
  starting transfers between devices  8.92 us (36%)
  local copies, waits for them, and re-layouts  0.95 us (4%)
  between operations  0.83 us (3%)
  waiting for transfers between devices  0.64 us (3%)
    ppermute x4, starting transfers between devices, exchange(): got.append(lax.ppermute(value, axis, pairs + [(b, a) for a, b in pairs]))  8.92 us
    pallas_call x1, Pallas kernels, fields(): pl.pallas_call(functools.partial(fields_kernel, dims), out_shape=(jax.Sha...  6.21 us
    pallas_call x1, Pallas kernels, near_own(): pl.pallas_call(functools.partial(near_own_kernel, dims), out_shape=(jax.S...  3.62 us
    pallas_call x1, Pallas kernels, prepare(): pl.pallas_call(prepare_kernel, out_shape=jax.ShapeDtypeStruct((SPAN * 64,...  1.6 us
    pallas_call x1, Pallas kernels, pack_row(): pl.pallas_call(functools.partial(pack_row_kernel, dims), out_shape=(shape...  1.56 us
    unnamed x18, local copies, waits for them, and re-layouts  0.93 us
    ppermute x4, waiting for transfers between devices, exchange(): got.append(lax.ppermute(value, axis, pairs + [(b, a) for a, b in pairs]))  0.64 us
  transfers between devices with their start and end apart: 4, of which 1 were waited for; matrix products, arithmetic and copies ran while one was open for 0% of the time, Pallas kernels for 21%

profile of v3, /device:TPU:19, one launch (start us, length us, event | category | flops | bytes accessed | tf_op | source)
XLA Modules:
  0.0 24.4 jit_solution(10686547181185494635)
XLA Ops:
  0.6 1.6 %pack_row.1 = (f32[32,256]{1,0:T(8,128)}, f32[32,256]{1,0:T(8,128)}, f32[80,256]{1,0:T(8,128)}) custom-call(f32[3,4,4,256]{3,2,1,0:T(4,128)} %pos_far.1, f32[4,4,256]{2,1,0:T(4,128)} %mass_far.1, s32[4,4,4]{2,1,0:T(4,128)} %counts_far.1, f32[4,4,224]{2,1,0:T(4,128)} %poles_far.1), custom_call_target="tpu_custom_call" | custom-call | tf_op jit(solution)/shard_map/pack_row/pallas_call | solution.py:560
  2.2 0.3 %collective-permute-start = (f32[32,256]{1,0:T(8,128)}, f32[32,256]{1,0:T(8,128)S(1)}, u32[]{:S(2)}, u32[]{:S(2)}) collective-permute-start(f32[32,256]{1,0:T(8,128)} %get-tuple-element.12), channel_id=1, source_target_pairs={{0,4},{8,12},{16,20},{24,28},{4,0},{12,8},{20,16},{28,24},{1,5},{9... | collective-permute-start | bytes 98312 | tf_op jit(solution)/shard_map/ppermute | solution.py:670
  2.5 4.1 %collective-permute-start.1 = (f32[32,256]{1,0:T(8,128)}, f32[32,256]{1,0:T(8,128)S(1)}, u32[]{:S(2)}, u32[]{:S(2)}) collective-permute-start(f32[32,256]{1,0:T(8,128)} %get-tuple-element.13), channel_id=1, source_target_pairs={{4,8},{12,16},{20,24},{8,4},{16,12},{24,20},{5,9},{13,17},{21,25},... | collective-permute-start | bytes 98312 | tf_op jit(solution)/shard_map/ppermute | solution.py:670
  6.6 0.0 copy-start.2
  6.7 0.9 %copy-done.2 = f32[80,256]{1,0:T(8,128)S(1)} copy-done((f32[80,256]{1,0:T(8,128)S(1)}, f32[80,256]{1,0:T(8,128)}, u32[]{:S(2)}) %copy-start.2) | copy-done | bytes 81944
  7.5 0.0 slice-start
  7.5 3.6 %near_own.1 = (f32[128,256]{1,0:T(8,128)S(1)}, bf16[2048,256]{1,0:T(8,128)(2,1)S(1)}, f32[8,128]{1,0:T(8,128)S(1)}) custom-call(f32[80,256]{1,0:T(8,128)S(1)} %copy-done.2), custom_call_target="tpu_custom_call" | custom-call | flops 4294967296 | bytes 1048576 | tf_op jit(solution)/shard_map/near_own/pallas_call | solution.py:613
  11.2 0.0 copy-start.1
  11.2 0.0 copy-start.3
  11.2 0.0 copy-start.4
  11.2 0.0 copy-start.5
  11.2 0.0 copy-start.6
  11.2 0.0 copy-start.7
  11.2 0.0 copy-start.8
  11.3 0.0 collective-permute-done.got_a.a1
  11.3 0.0 collective-permute-done.1.got_b.b1
  11.3 0.1 pack_col.1
  11.3 1.3 %collective-permute-start.2 = (f32[56,256]{1,0:T(8,128)S(1)}, f32[56,256]{1,0:T(8,128)S(1)}, u32[]{:S(2)}, u32[]{:S(2)}) collective-permute-start(f32[56,256]{1,0:T(8,128)S(1)} %get-tuple-element.15), channel_id=1, source_target_pairs={{0,1},{2,3},{1,0},{3,2},{4,5},{6,7},{5,4},{7,6},{8,9},{10,11},{9,8... | collective-permute-start | bytes 172040 | tf_op jit(solution)/shard_map/ppermute | solution.py:670
  12.6 3.2 %collective-permute-start.3 = (f32[56,256]{1,0:T(8,128)S(1)}, f32[56,256]{1,0:T(8,128)S(1)}, u32[]{:S(2)}, u32[]{:S(2)}) collective-permute-start(f32[56,256]{1,0:T(8,128)S(1)} %get-tuple-element.16), channel_id=1, source_target_pairs={{1,2},{2,1},{5,6},{6,5},{9,10},{10,9},{13,14},{14,13},{17,18},{18,... | collective-permute-start | bytes 172040 | tf_op jit(solution)/shard_map/ppermute | solution.py:670
  15.8 0.0 slice-done
  15.9 0.0 copy-done
  15.9 1.6 %prepare.1.table = bf16[448,6400]{1,0:T(8,128)(2,1)S(1)} custom-call(f32[343,3136]{1,0:T(8,128)S(1)} %copy-done, f32[343,128]{1,0:T(8,128)S(1)} %pad.4.tail, f32[8,128]{1,0:T(8,128)S(1)} %get-tuple-element.19.token), custom_call_target="tpu_custom_call" | custom-call | flops 16777216 | bytes 10485760 | tf_op jit(solution)/shard_map/prepare/pallas_call | solution.py:580
  17.5 0.0 collective-permute-done.2.a2
  17.5 0.6 %collective-permute-done.3.b2 = f32[56,256]{1,0:T(8,128)S(1)} collective-permute-done((f32[56,256]{1,0:T(8,128)S(1)}, f32[56,256]{1,0:T(8,128)S(1)}, u32[]{:S(2)}, u32[]{:S(2)}) %collective-permute-start.3) | collective-permute-done | bytes 57376 | tf_op jit(solution)/shard_map/ppermute | solution.py:670
  18.1 0.0 copy-done.1
  18.1 0.0 copy-done.3
  18.1 0.0 copy-done.4
  18.1 0.0 copy-done.5
  18.2 0.0 copy-done.6
  18.2 0.0 copy-done.7
  18.2 0.0 copy-done.8
  18.2 6.2 %fields.1 = (f32[4,4,256]{2,1,0:T(4,128)}, f32[4,4,224]{2,1,0:T(4,128)}) custom-call(f32[80,256]{1,0:T(8,128)S(1)} %copy-done.3, f32[32,256]{1,0:T(8,128)S(1)} %collective-permute-done.got_a.a1, f32[32,256]{1,0:T(8,128)S(1)} %collective-permute-done.1.got_b.b1, f32[56,256]{1,0:T(8,128)S(1)} %collective-permute-done.2.a2, ...), custom_call_target="tpu_custom_call" | custom-call | tf_op jit(solution)/shard_map/fields/pallas_call | solution.py:641
  (2 shorter events, 0.0 us)
Async XLA Ops:
  2.2 9.1 %collective-permute-start = (f32[32,256]{1,0:T(8,128)}, f32[32,256]{1,0:T(8,128)S(1)}, u32[]{:S(2)}, u32[]{:S(2)}) collective-permute-start(f32[32,256]{1,0:T(8,128)} %get-tuple-element.12), channel_id=1, source_target_pairs={{0,4},{8,12},{16,20},{24,28},{4,0},{12,8},{20,16},{28,24},{1,5},{9... | collective-permute-start | bytes 98312 | tf_op jit(solution)/shard_map/ppermute | solution.py:670
  2.5 8.7 %collective-permute-start.1 = (f32[32,256]{1,0:T(8,128)}, f32[32,256]{1,0:T(8,128)S(1)}, u32[]{:S(2)}, u32[]{:S(2)}) collective-permute-start(f32[32,256]{1,0:T(8,128)} %get-tuple-element.13), channel_id=1, source_target_pairs={{4,8},{12,16},{20,24},{8,4},{16,12},{24,20},{5,9},{13,17},{21,25},... | collective-permute-start | bytes 98312 | tf_op jit(solution)/shard_map/ppermute | solution.py:670
  6.6 0.9 %copy-start.2 = (f32[80,256]{1,0:T(8,128)S(1)}, f32[80,256]{1,0:T(8,128)}, u32[]{:S(2)}) copy-start(f32[80,256]{1,0:T(8,128)} %get-tuple-element.11.own) | copy-start | bytes 245764
  7.5 8.3 %slice-start = ((f32[343,3136]{1,0:T(8,128)}), f32[343,64]{1,0:T(8,128)S(1)}, s32[]{:S(2)}) async-start(f32[343,3136]{1,0:T(8,128)} %ops.1), calls=%async_computation | async-start | bytes 352256 | tf_op jit(solution)/shard_map/slice | solution.py:579
  7.5 8.3 %copy-start = (f32[343,3136]{1,0:T(8,128)S(1)}, f32[343,3136]{1,0:T(8,128)}, u32[]{:S(2)}) copy-start(f32[343,3136]{1,0:T(8,128)} %ops.1) | copy-start | bytes 12907780
  11.2 7.0 %copy-start.1 = (bf16[256,2048]{1,0:T(8,128)(2,1)S(1)}, bf16[256,2048]{1,0:T(8,128)(2,1)}, u32[]{:S(2)}) copy-start(bf16[256,2048]{1,0:T(8,128)(2,1)} %constant.9.clone.pick) | copy-start | bytes 3145732
  11.2 7.0 %copy-start.3 = (f32[80,256]{1,0:T(8,128)S(1)}, f32[80,256]{1,0:T(8,128)}, u32[]{:S(2)}) copy-start(f32[80,256]{1,0:T(8,128)} %get-tuple-element.11.own) | copy-start | bytes 245764
  11.2 7.0 %copy-start.4 = (f32[8,56,56]{2,1,0:T(8,128)S(1)}, f32[8,56,56]{2,1,0:T(8,128)}, u32[]{:S(2)}) copy-start(f32[8,56,56]{2,1,0:T(8,128)} %l2l.1) | copy-start | bytes 301060
  11.2 6.9 %copy-start.5 = (f32[3,64,128]{2,1,0:T(8,128)S(1)}, f32[3,64,128]{2,1,0:T(8,128)}, u32[]{:S(2)}) copy-start(f32[3,64,128]{2,1,0:T(8,128)} %constant.11.clone.points) | copy-start | bytes 294916
  11.2 6.9 %copy-start.6 = (f32[64,64]{1,0:T(8,128)S(1)}, f32[64,64]{1,0:T(8,128)}, u32[]{:S(2)}) copy-start(f32[64,64]{1,0:T(8,128)} %constant.10.clone.spread) | copy-start | bytes 49156
  11.2 6.9 %copy-start.7 = (f32[56,56]{1,0:T(8,128)S(1)}, f32[56,56]{1,0:T(8,128)}, u32[]{:S(2)}) copy-start(f32[56,56]{1,0:T(8,128)} %c2e.1) | copy-start | bytes 37636
  11.2 6.9 %copy-start.8 = (f32[2,2,112]{2,1,0:T(2,128)S(1)}, f32[2,2,112]{2,1,0:T(2,128)}, u32[]{:S(2)}) copy-start(f32[2,2,112]{2,1,0:T(2,128)} %parents.1) | copy-start | bytes 5380
  11.3 6.1 %collective-permute-start.2 = (f32[56,256]{1,0:T(8,128)S(1)}, f32[56,256]{1,0:T(8,128)S(1)}, u32[]{:S(2)}, u32[]{:S(2)}) collective-permute-start(f32[56,256]{1,0:T(8,128)S(1)} %get-tuple-element.15), channel_id=1, source_target_pairs={{0,1},{2,3},{1,0},{3,2},{4,5},{6,7},{5,4},{7,6},{8,9},{10,11},{9,8... | collective-permute-start | bytes 172040 | tf_op jit(solution)/shard_map/ppermute | solution.py:670
  12.6 5.5 %collective-permute-start.3 = (f32[56,256]{1,0:T(8,128)S(1)}, f32[56,256]{1,0:T(8,128)S(1)}, u32[]{:S(2)}, u32[]{:S(2)}) collective-permute-start(f32[56,256]{1,0:T(8,128)S(1)} %get-tuple-element.16), channel_id=1, source_target_pairs={{1,2},{2,1},{5,6},{6,5},{9,10},{10,9},{13,14},{14,13},{17,18},{18,... | collective-permute-start | bytes 172040 | tf_op jit(solution)/shard_map/ppermute | solution.py:670

commit v4 on v3

--- a/solution.py
+++ b/solution.py
@@ -18,7 +18,7 @@
 F32, BF16 = jnp.float32, jnp.bfloat16
 REACH = 3
 SPAN = 2 * REACH + 1
-KROWS = 136
+PITCH = 136
 
 
 def surface_points():
@@ -211,14 +211,17 @@
         lanes = slice(half * LANES, (half + 1) * LANES)
         arrays = [su[c][at : at + 8, lanes] for c in range(4)]
         for k, value in source_features_at(sz, place(rows), arrays, lane):
-            feats[half, pl.ds(at * KROWS + k, 8, stride=KROWS), :] = value
+            feats[half, at * LANES + 8 * k : at * LANES + 8 * (k + 1), :] = value
+
+
+def features_of(feats, half, i):
+    return feats[half, pl.ds((i // 8) * 8 * LANES + i % 8, LANES, stride=8), :]
 
 
 def turn_features(feats, lhs, i):
     for half in range(2):
-        block = feats[half, i * KROWS : i * KROWS + LANES, :]
         at = (2 * i + half) * LANES
-        lhs[at : at + LANES, :] = block.T.astype(BF16)
+        lhs[at : at + LANES, :] = features_of(feats, half, i).T.astype(BF16)
 
 
 def near_sums(sz, lhs, rhs, total, src, targets):
@@ -269,12 +272,11 @@
             lane = lax.broadcasted_iota(jnp.int32, (8, LANES), 1) + half * LANES
             arrays = [su[c][at : at + 8, lanes] for c in range(3)]
             for k, value in target_features_at(dims, arrays, rows, lane):
-                rfeats[half, pl.ds(at * KROWS + k, 8, stride=KROWS), :] = value
+                rfeats[half, at * LANES + 8 * k : at * LANES + 8 * (k + 1), :] = value
     for i in range(cols):
         for half in range(2):
-            rhs[i * LANES : (i + 1) * LANES, half * LANES : (half + 1) * LANES] = rfeats[
-                half, i * KROWS : i * KROWS + LANES, :
-            ].astype(BF16)
+            lanes = slice(half * LANES, (half + 1) * LANES)
+            rhs[i * LANES : (i + 1) * LANES, lanes] = features_of(rfeats, half, i).astype(BF16)
     near[...] = jnp.zeros_like(near)
     for x in range(sx):
         for y in range(sy):
@@ -286,12 +288,46 @@
             near_sums(sz, lhs, rhs, near, x * sy + y, targets)
 
 
+def targets_of(dims, cell):
+    sx, sy, _ = dims
+    return [
+        x * sy + y
+        for x in range(sx)
+        for y in range(sy)
+        if 0 <= cell[0] - x <= 2 and 0 <= cell[1] - y <= 2
+    ]
+
+
+def near_row_kernel(dims, got_a, got_b, near_own, rhs, token, near, slots, feats, lhs):
+    sx, sy, sz = dims
+    base = REACH * sy
+    odd = is_odd("row")
+    su = [slots.at[c] for c in range(4)]
+    slots[...] = jnp.zeros_like(slots)
+    for side, (first, second) in enumerate(((got_a, got_b), (got_b, got_a))):
+        for c in range(4):
+            rows = slice(base + c * sy, base + (c + 1) * sy)
+            su[c][side * sy : (side + 1) * sy, :] = jnp.where(odd, first[rows, :], second[rows, :])
+
+    def place(rows):
+        return jnp.where(rows < sy, 0, sx + 1), rows % sy + 1
+
+    for at in range(0, slots.shape[1], 8):
+        fill_features(sz, place, su, feats, at)
+    for i in range(2 * sy):
+        turn_features(feats, lhs, i)
+    near[...] = near_own[...]
+    for i in range(2 * sy):
+        cell = ((sx + 1) * (i // sy), i % sy + 1)
+        near_sums(sz, lhs, rhs, near, i, targets_of(dims, cell))
+
+
 def fields_kernel(
     dims,
     own, a1, b1, a2, b2, near_own, rhs, table, parents, l2l, c2e, pick,
     spread, points,
     potential, local_out,
-    halo_slots, feats, lhs, near, sm, picked, lm, dens,
+    halo_slots, feats, lhs, near, sm, picked, lm, dens, inherited,
 ):
     sx, sy, sz = dims
     hx, hy = sx + 2, sy + 2
@@ -300,40 +336,36 @@
     odd_row, odd_col = is_odd("row"), is_odd("col")
     base1 = REACH * sy
     base2 = REACH * (sx + 2 * REACH)
-    sides = []
-    for odd, got_a, got_b, base, line in (
-        (odd_row, a1, b1, base1, sy), (odd_col, a2, b2, base2, hx)
-    ):
-        for first, second in ((got_a, got_b), (got_b, got_a)):
-            sides.append((odd, first, second, base, line))
-
     su = [halo_slots.at[c] for c in range(4)]
     halo_slots[...] = jnp.zeros_like(halo_slots)
     sm[...] = jnp.zeros_like(sm)
     sm[0:cols, :] = own[4 * cols : 5 * cols, :]
-    to, to_poles = 0, cols
-    for odd, first, second, base, line in sides:
-        value = jnp.where(odd, first[...], second[...])
-        sm[to_poles : to_poles + base, :] = value[0:base, :]
-        to_poles += base
+    at = cols
+    for first, second in ((a1, b1), (b1, a1)):
+        sm[at : at + base1, :] = jnp.where(odd_row, first[0:base1, :], second[0:base1, :])
+        at += base1
+    for side, (first, second) in enumerate(((a2, b2), (b2, a2))):
+        value = jnp.where(odd_col, first[...], second[...])
+        sm[at : at + base2, :] = value[0:base2, :]
+        at += base2
         for c in range(4):
-            su[c][to : to + line, :] = value[base + c * line : base + (c + 1) * line, :]
-        to += line
+            rows = slice(base2 + c * hx, base2 + (c + 1) * hx)
+            su[c][side * hx : (side + 1) * hx, :] = value[rows, :]
 
     def place(rows):
-        x, y = rows - 2 * sy - hx, jnp.full_like(rows, hy - 1)
-        x = jnp.where(rows < 2 * sy + hx, rows - 2 * sy, x)
-        y = jnp.where(rows < 2 * sy + hx, 0, y)
-        x = jnp.where(rows < 2 * sy, hx - 1, x)
-        y = jnp.where(rows < 2 * sy, rows - sy + 1, y)
-        x = jnp.where(rows < sy, 0, x)
-        y = jnp.where(rows < sy, rows + 1, y)
-        return x, y
-
-    halo = {(0, y + 1): y for y in range(sy)}
-    halo.update({(hx - 1, y + 1): sy + y for y in range(sy)})
-    halo.update({(x, 0): 2 * sy + x for x in range(hx)})
-    halo.update({(x, hy - 1): 2 * sy + hx + x for x in range(hx)})
+        second = rows >= hx
+        return jnp.where(second, rows - hx, rows), jnp.where(second, hy - 1, 0)
+
+    halo = {(x, (hy - 1) * side): side * hx + x for side in range(2) for x in range(hx)}
+
+    rows = []
+    for pz in range(sz // 2):
+        for x in range(sx // 2):
+            rows.append(parents[x, :, pz * Q : (pz + 1) * Q])
+    above = jnp.concatenate(rows, axis=0)
+    below = jnp.concatenate([dot_exact(above, l2l[o]) for o in range(8)], axis=0)
+    inherited[...] = dot_exact(spread[...], below)
+
     for pair in range(sz // 2):
         his, los = [], []
         for zi in range(2):
@@ -349,9 +381,8 @@
         for xy in range(0, cols, 2):
             block = dot(picked[...], pick[:, xy * LANES : (xy + 2) * LANES])
             for i in range(2):
-                lm[pair, pl.ds(xy + i, 2 * 64, stride=cols), :] = block[
-                    :, i * LANES : (i + 1) * LANES
-                ]
+                at = (xy + i) * PITCH
+                lm[pair, at : at + LANES, :] = block[:, i * LANES : (i + 1) * LANES]
 
     period = 16
     lane16 = lax.broadcasted_iota(jnp.int32, (cols, LANES), 1)
@@ -371,18 +402,19 @@
         for j in range(-(-Q // period)):
             if j * (period * Q // LANES) + t >= tiles:
                 continue
-            start = (j * period + members[0]) * cols
+            vectors = [j * period + s for s in members]
             left.append(
                 jnp.concatenate(
                     [
                         jnp.concatenate(
                             [
-                                lm[p, h * 64 * cols + start : h * 64 * cols + start + rows, :]
+                                lm[p, pl.ds(h * 64 + q, cols, stride=PITCH), :]
                                 for p in range(sz // 2)
                             ],
                             axis=1,
                         )
                         for h in range(2)
+                        for q in vectors
                     ],
                     axis=0,
                 ).astype(BF16)
@@ -408,15 +440,10 @@
 
     assert not groups and not turns
 
-    rows = []
-    for pz in range(sz // 2):
-        for x in range(sx // 2):
-            rows.append(parents[x, :, pz * Q : (pz + 1) * Q])
-    above = jnp.concatenate(rows, axis=0)
-    below = jnp.concatenate([dot_exact(above, l2l[o]) for o in range(8)], axis=0)
-    field = jnp.concatenate([part[:, 0:Q] for part in check], axis=0)
-    field = field + dot_exact(spread[...], below)
-    local = dot_exact(field, c2e[...])
+    field = jnp.concatenate([part[:, 0:Q] for part in check], axis=0) + inherited[...]
+    field_hi, field_lo = split2(field)
+    map_hi, map_lo = split2(c2e[...])
+    local = dot(field_hi, map_hi) + (dot(field_hi, map_lo) + dot(field_lo, map_hi))
     dens[...] = jnp.zeros_like(dens)
     dens[0 : sz * cols, 0:Q] = local
     flat = None
@@ -452,15 +479,10 @@
     near[...] = near_own[...]
     left = list(range(cols))
     for cell, src in halo.items():
-        targets = [
-            x * sy + y
-            for x in range(sx)
-            for y in range(sy)
-            if 0 <= cell[0] - x <= 2 and 0 <= cell[1] - y <= 2
-        ]
-        if left:
-            far(left.pop(0))
-        near_sums(sz, lhs, rhs, near, src, targets)
+        for _ in range(2):
+            if left:
+                far(left.pop(0))
+        near_sums(sz, lhs, rhs, near, src, targets_of(dims, cell))
     assert not left
     for i in range(cols):
         x, y = i // sy, i % sy
@@ -569,8 +591,9 @@
             pltpu.VMEM(poles.shape, F32),
             pltpu.SemaphoreType.DMA((4,)),
         ],
+        compiler_params=pltpu.CompilerParams(vmem_limit_bytes=2 << 20),
         name="pack_row",
-    )(pos, mass, counts, poles)
+    )(*(pltpu.with_memory_space_constraint(a, pltpu.HBM) for a in (pos, mass, counts, poles)))
 
 
 def prepare(ops, token):
@@ -620,9 +643,9 @@
         in_specs=[VMEM],
         out_specs=(VMEM,) * 3,
         scratch_shapes=[
-            pltpu.VMEM((2, cols * KROWS, LANES), F32),
+            pltpu.VMEM((2, cols * LANES, LANES), F32),
             pltpu.VMEM((cols * sz * CAP, LANES), BF16),
-            pltpu.VMEM((2, cols * KROWS, LANES), F32),
+            pltpu.VMEM((2, cols * LANES, LANES), F32),
         ],
         compiler_params=pltpu.CompilerParams(vmem_limit_bytes=10 << 20),
         cost_estimate=pl.CostEstimate(flops=1 << 32, bytes_accessed=1 << 20, transcendentals=1 << 22),
@@ -630,10 +653,29 @@
     )(own)
 
 
+def near_row(dims, got_a, got_b, near, rhs, token):
+    sx, sy, sz = dims
+    slots = round_up(2 * sy, 8)
+    return pl.pallas_call(
+        functools.partial(near_row_kernel, dims),
+        out_shape=jax.ShapeDtypeStruct(near.shape, F32),
+        in_specs=[VMEM] * 5,
+        out_specs=VMEM,
+        scratch_shapes=[
+            pltpu.VMEM((4, slots, sz * CAP), F32),
+            pltpu.VMEM((2, slots * LANES, LANES), F32),
+            pltpu.VMEM((slots * sz * CAP, LANES), BF16),
+        ],
+        compiler_params=pltpu.CompilerParams(vmem_limit_bytes=6 << 20),
+        cost_estimate=pl.CostEstimate(flops=1 << 30, bytes_accessed=1 << 20, transcendentals=1 << 20),
+        name="near_row",
+    )(got_a, got_b, near, rhs, token)
+
+
 def fields(dims, own, a1, b1, a2, b2, near, rhs, table, parents, l2l, c2e):
     sx, sy, sz = dims
     cols = sx * sy
-    ring = 2 * sy + 2 * (sx + 2)
+    ring = 2 * (sx + 2)
     pick = jnp.asarray(gather_constant(dims), BF16)
     spread = jnp.asarray(spread_constant(dims))
     points = np.full((3, 64, LANES), 10.0, np.float32)
@@ -648,13 +690,14 @@
         out_specs=(VMEM, VMEM),
         scratch_shapes=[
             pltpu.VMEM((4, round_up(ring, 8), sz * CAP), F32),
-            pltpu.VMEM((2, round_up(ring, 8) * KROWS, LANES), F32),
+            pltpu.VMEM((2, round_up(ring, 8) * LANES, LANES), F32),
             pltpu.VMEM((ring * sz * CAP, LANES), BF16),
             pltpu.VMEM((cols * 8, sz * CAP), F32),
             pltpu.VMEM((LANES, 2 * LANES), F32),
             pltpu.VMEM((LANES, 2 * LANES), BF16),
-            pltpu.VMEM((sz // 2, 2 * 64 * cols, LANES), F32),
+            pltpu.VMEM((sz // 2, cols * PITCH, LANES), F32),
             pltpu.VMEM((LANES, LANES), F32),
+            pltpu.VMEM((sz * cols, Q), F32),
         ],
         compiler_params=pltpu.CompilerParams(vmem_limit_bytes=16 << 20),
         name="fields",
@@ -680,6 +723,7 @@
     send_a, send_b, token = pack_col(dims, own, a1, b1, token)
     a2, b2 = exchange(send_a, send_b, "col")
     table = prepare(m2l_ops, token)
+    near = near_row(dims, a1, b1, near, rhs, token)
     return fields(
         dims, own, a1, b1, a2, b2, near, rhs, table, parent_local, l2l_ops, check_to_equiv
     )

time: 24.7 us -> 22.2 us (0.90)
  Pallas kernels: 13.1 us -> 12.2 us
  local copies, waits for them, and re-layouts: 0.95 us -> 0.07 us
  waiting for transfers between devices: 0.64 us -> 0.01 us
    pallas_call x1, Pallas kernels: 6.21 us -> 5.29 us  [fields(): pl.pallas_call(functools.partial(fields_kernel, dims), out_shape=(jax.Sha...]
    pallas_call x0 -> x1, Pallas kernels: none -> 0.9 us  [near_row(): pl.pallas_call(functools.partial(near_row_kernel, dims), out_shape=jax.Sh...]
    unnamed x18 -> x14, local copies, waits for them, and re-layouts: 0.93 us -> 0.04 us
    pallas_call x1, Pallas kernels: 1.56 us -> 0.9 us  [pack_row(): pl.pallas_call(functools.partial(pack_row_kernel, dims), out_shape=(shape...]
    ppermute x4, waiting for transfers between devices: 0.64 us -> 0.01 us  [exchange(): got.append(lax.ppermute(value, axis, pairs + [(b, a) for a, b in pairs]))]
  transfers between devices with their start and end apart: 4 -> 4, of which waited for: 1 -> 0; matrix products, arithmetic and copies ran while one was open for 0% -> 0% of each run, Pallas kernels for 21% -> 27%
where the time goes in v4:
time: 22.2 us; the launch traced here: 21.9 us
  Pallas kernels  12.2 us (55%)
  starting transfers between devices  8.79 us (40%)
  between operations  0.85 us (4%)
    ppermute x4, starting transfers between devices, exchange(): got.append(lax.ppermute(value, axis, pairs + [(b, a) for a, b in pairs]))  8.79 us
    pallas_call x1, Pallas kernels, fields(): pl.pallas_call(functools.partial(fields_kernel, dims), out_shape=(jax.Sha...  5.29 us
    pallas_call x1, Pallas kernels, near_own(): pl.pallas_call(functools.partial(near_own_kernel, dims), out_shape=(jax.S...  3.41 us
    pallas_call x1, Pallas kernels, prepare(): pl.pallas_call(prepare_kernel, out_shape=jax.ShapeDtypeStruct((SPAN * 64,...  1.6 us
    pallas_call x1, Pallas kernels, near_row(): pl.pallas_call(functools.partial(near_row_kernel, dims), out_shape=jax.Sh...  0.9 us
    pallas_call x1, Pallas kernels, pack_row(): pl.pallas_call(functools.partial(pack_row_kernel, dims), out_shape=(shape...  0.9 us
  transfers between devices with their start and end apart: 4, of which 0 were waited for; matrix products, arithmetic and copies ran while one was open for 0% of the time, Pallas kernels for 27%

profile of v4, /device:TPU:19, one launch (start us, length us, event | category | flops | bytes accessed | tf_op | source)
XLA Modules:
  0.0 21.9 jit_solution(14927453078239459038)
XLA Ops:
  0.6 0.9 %pack_row.1 = (f32[32,256]{1,0:T(8,128)S(1)}, f32[32,256]{1,0:T(8,128)S(1)}, f32[80,256]{1,0:T(8,128)S(1)}) custom-call(f32[3,4,4,256]{3,2,1,0:T(4,128)} %pos_far.1, f32[4,4,256]{2,1,0:T(4,128)} %mass_far.1, s32[4,4,4]{2,1,0:T(4,128)} %counts_far.1, f32[4,4,224]{2,1,0:T(4,128)} %poles_far.1), custom_call_target="tpu_custom_call" | custom-call | tf_op jit(solution)/shard_map/pack_row/pallas_call | solution.py:582
  1.5 0.3 %collective-permute-start = (f32[32,256]{1,0:T(8,128)S(1)}, f32[32,256]{1,0:T(8,128)S(1)}, u32[]{:S(2)}, u32[]{:S(2)}) collective-permute-start(f32[32,256]{1,0:T(8,128)S(1)} %get-tuple-element.12), channel_id=1, source_target_pairs={{0,4},{8,12},{16,20},{24,28},{4,0},{12,8},{20,16},{28,24},{1,5},{9... | collective-permute-start | bytes 98312 | tf_op jit(solution)/shard_map/ppermute | solution.py:713
  1.9 4.1 %collective-permute-start.1 = (f32[32,256]{1,0:T(8,128)S(1)}, f32[32,256]{1,0:T(8,128)S(1)}, u32[]{:S(2)}, u32[]{:S(2)}) collective-permute-start(f32[32,256]{1,0:T(8,128)S(1)} %get-tuple-element.13), channel_id=1, source_target_pairs={{4,8},{12,16},{20,24},{8,4},{16,12},{24,20},{5,9},{13,17},{21,25},... | collective-permute-start | bytes 98312 | tf_op jit(solution)/shard_map/ppermute | solution.py:713
  6.0 0.0 slice-start
  6.0 0.0 copy-start
  6.0 3.4 %near_own.1 = (f32[128,256]{1,0:T(8,128)S(1)}, bf16[2048,256]{1,0:T(8,128)(2,1)S(1)}, f32[8,128]{1,0:T(8,128)S(1)}) custom-call(f32[80,256]{1,0:T(8,128)S(1)} %get-tuple-element.11.own), custom_call_target="tpu_custom_call" | custom-call | flops 4294967296 | bytes 1048576 | tf_op jit(solution)/shard_map/near_own/pallas_call | solution.py:636
  9.4 0.0 slice-done
  9.5 0.0 collective-permute-done.got_a.a1
  9.5 0.0 collective-permute-done.1.got_b.b1
  9.5 0.1 pack_col.1
  9.6 1.3 %collective-permute-start.2 = (f32[56,256]{1,0:T(8,128)S(1)}, f32[56,256]{1,0:T(8,128)S(1)}, u32[]{:S(2)}, u32[]{:S(2)}) collective-permute-start(f32[56,256]{1,0:T(8,128)S(1)} %get-tuple-element.15), channel_id=1, source_target_pairs={{0,1},{2,3},{1,0},{3,2},{4,5},{6,7},{5,4},{7,6},{8,9},{10,11},{9,8... | collective-permute-start | bytes 172040 | tf_op jit(solution)/shard_map/ppermute | solution.py:713
  10.9 3.0 %collective-permute-start.3 = (f32[56,256]{1,0:T(8,128)S(1)}, f32[56,256]{1,0:T(8,128)S(1)}, u32[]{:S(2)}, u32[]{:S(2)}) collective-permute-start(f32[56,256]{1,0:T(8,128)S(1)} %get-tuple-element.16), channel_id=1, source_target_pairs={{1,2},{2,1},{5,6},{6,5},{9,10},{10,9},{13,14},{14,13},{17,18},{18,... | collective-permute-start | bytes 172040 | tf_op jit(solution)/shard_map/ppermute | solution.py:713
  13.9 0.0 copy-done
  13.9 0.0 copy-start.1
  13.9 0.0 copy-start.2
  14.0 0.0 copy-start.3
  14.0 0.0 copy-start.4
  14.0 0.0 copy-start.5
  14.0 0.0 copy-start.6
  14.0 1.6 %prepare.1.table = bf16[448,6400]{1,0:T(8,128)(2,1)S(1)} custom-call(f32[343,3136]{1,0:T(8,128)S(1)} %copy-done, f32[343,128]{1,0:T(8,128)S(1)} %pad.4.tail, f32[8,128]{1,0:T(8,128)S(1)} %get-tuple-element.19.token), custom_call_target="tpu_custom_call" | custom-call | flops 16777216 | bytes 10485760 | tf_op jit(solution)/shard_map/prepare/pallas_call | solution.py:603
  15.6 0.9 %near_row.1.near_own = f32[128,256]{1,0:T(8,128)S(1)} custom-call(f32[32,256]{1,0:T(8,128)S(1)} %collective-permute-done.got_a.a1, f32[32,256]{1,0:T(8,128)S(1)} %collective-permute-done.1.got_b.b1, f32[128,256]{1,0:T(8,128)S(1)} %get-tuple-element.17.near_own, bf16[2048,256]{1,0:T(8,128)(2,1)S(1)} %get-tuple-element.18.rhs, ...), custom_call_target="tpu_custom_call" | custom-call | flops 1073741824 | bytes 1048576 | tf_op jit(solution)/shard_map/near_row/pallas_call | solution.py:659
  16.5 0.0 collective-permute-done.2.a2
  16.5 0.0 collective-permute-done.3.b2
  16.5 0.0 copy-done.1
  16.6 0.0 copy-done.2
  16.6 0.0 copy-done.3
  16.6 0.0 copy-done.4
  16.6 0.0 copy-done.5
  16.6 0.0 copy-done.6
  16.6 5.3 %fields.1 = (f32[4,4,256]{2,1,0:T(4,128)}, f32[4,4,224]{2,1,0:T(4,128)}) custom-call(f32[80,256]{1,0:T(8,128)S(1)} %get-tuple-element.11.own, f32[32,256]{1,0:T(8,128)S(1)} %collective-permute-done.got_a.a1, f32[32,256]{1,0:T(8,128)S(1)} %collective-permute-done.1.got_b.b1, f32[56,256]{1,0:T(8,128)S(1)} %collective-permute-done.2.a2, ...), custom_call_target="tpu_custom_call" | custom-call | tf_op jit(solution)/shard_map/fields/pallas_call | solution.py:683
  (1 shorter events, 0.0 us)
Async XLA Ops:
  1.5 7.9 %collective-permute-start = (f32[32,256]{1,0:T(8,128)S(1)}, f32[32,256]{1,0:T(8,128)S(1)}, u32[]{:S(2)}, u32[]{:S(2)}) collective-permute-start(f32[32,256]{1,0:T(8,128)S(1)} %get-tuple-element.12), channel_id=1, source_target_pairs={{0,4},{8,12},{16,20},{24,28},{4,0},{12,8},{20,16},{28,24},{1,5},{9... | collective-permute-start | bytes 98312 | tf_op jit(solution)/shard_map/ppermute | solution.py:713
  1.9 7.6 %collective-permute-start.1 = (f32[32,256]{1,0:T(8,128)S(1)}, f32[32,256]{1,0:T(8,128)S(1)}, u32[]{:S(2)}, u32[]{:S(2)}) collective-permute-start(f32[32,256]{1,0:T(8,128)S(1)} %get-tuple-element.13), channel_id=1, source_target_pairs={{4,8},{12,16},{20,24},{8,4},{16,12},{24,20},{5,9},{13,17},{21,25},... | collective-permute-start | bytes 98312 | tf_op jit(solution)/shard_map/ppermute | solution.py:713
  6.0 3.4 %slice-start = ((f32[343,3136]{1,0:T(8,128)}), f32[343,64]{1,0:T(8,128)S(1)}, s32[]{:S(2)}) async-start(f32[343,3136]{1,0:T(8,128)} %ops.1), calls=%async_computation | async-start | bytes 352256 | tf_op jit(solution)/shard_map/slice | solution.py:602
  6.0 7.9 %copy-start = (f32[343,3136]{1,0:T(8,128)S(1)}, f32[343,3136]{1,0:T(8,128)}, u32[]{:S(2)}) copy-start(f32[343,3136]{1,0:T(8,128)} %ops.1) | copy-start | bytes 12907780
  9.6 7.0 %collective-permute-start.2 = (f32[56,256]{1,0:T(8,128)S(1)}, f32[56,256]{1,0:T(8,128)S(1)}, u32[]{:S(2)}, u32[]{:S(2)}) collective-permute-start(f32[56,256]{1,0:T(8,128)S(1)} %get-tuple-element.15), channel_id=1, source_target_pairs={{0,1},{2,3},{1,0},{3,2},{4,5},{6,7},{5,4},{7,6},{8,9},{10,11},{9,8... | collective-permute-start | bytes 172040 | tf_op jit(solution)/shard_map/ppermute | solution.py:713
  10.9 5.7 %collective-permute-start.3 = (f32[56,256]{1,0:T(8,128)S(1)}, f32[56,256]{1,0:T(8,128)S(1)}, u32[]{:S(2)}, u32[]{:S(2)}) collective-permute-start(f32[56,256]{1,0:T(8,128)S(1)} %get-tuple-element.16), channel_id=1, source_target_pairs={{1,2},{2,1},{5,6},{6,5},{9,10},{10,9},{13,14},{14,13},{17,18},{18,... | collective-permute-start | bytes 172040 | tf_op jit(solution)/shard_map/ppermute | solution.py:713
  13.9 2.6 %copy-start.1 = (bf16[256,2048]{1,0:T(8,128)(2,1)S(1)}, bf16[256,2048]{1,0:T(8,128)(2,1)}, u32[]{:S(2)}) copy-start(bf16[256,2048]{1,0:T(8,128)(2,1)} %constant.9.clone.pick) | copy-start | bytes 3145732
  13.9 2.6 %copy-start.2 = (f32[8,56,56]{2,1,0:T(8,128)S(1)}, f32[8,56,56]{2,1,0:T(8,128)}, u32[]{:S(2)}) copy-start(f32[8,56,56]{2,1,0:T(8,128)} %l2l.1) | copy-start | bytes 301060
  14.0 2.6 %copy-start.3 = (f32[3,64,128]{2,1,0:T(8,128)S(1)}, f32[3,64,128]{2,1,0:T(8,128)}, u32[]{:S(2)}) copy-start(f32[3,64,128]{2,1,0:T(8,128)} %constant.11.clone.points) | copy-start | bytes 294916
  14.0 2.6 %copy-start.4 = (f32[64,64]{1,0:T(8,128)S(1)}, f32[64,64]{1,0:T(8,128)}, u32[]{:S(2)}) copy-start(f32[64,64]{1,0:T(8,128)} %constant.10.clone.spread) | copy-start | bytes 49156
  14.0 2.6 %copy-start.5 = (f32[56,56]{1,0:T(8,128)S(1)}, f32[56,56]{1,0:T(8,128)}, u32[]{:S(2)}) copy-start(f32[56,56]{1,0:T(8,128)} %c2e.1) | copy-start | bytes 37636
  14.0 2.6 %copy-start.6 = (f32[2,2,112]{2,1,0:T(2,128)S(1)}, f32[2,2,112]{2,1,0:T(2,128)}, u32[]{:S(2)}) copy-start(f32[2,2,112]{2,1,0:T(2,128)} %parents.1) | copy-start | bytes 5380

commit v5 on v4

--- a/solution.py
+++ b/solution.py
@@ -49,8 +49,10 @@
     return jnp.dot(a, b, preferred_element_type=F32)
 
 
-def dot_exact(a, b):
-    return jnp.dot(a, b, preferred_element_type=F32, precision=lax.Precision.HIGHEST)
+def dot3(a, b):
+    a_hi, a_lo = split2(a)
+    b_hi, b_lo = split2(b)
+    return dot(a_hi, b_hi) + (dot(a_hi, b_lo) + dot(a_lo, b_hi))
 
 
 def column_weights(masses, counts, x, y, sz):
@@ -140,6 +142,30 @@
                 store(at, 1, own, c * cols + (x - 1) * sy)
 
 
+def surface_features(sz):
+    points = np.full((64, 3), 10.0, np.float32)
+    points[:Q] = surface_points() - np.float32(0.5)
+
+    def pieces(x):
+        out = []
+        for _ in range(3):
+            out.append(np.asarray(x, BF16).astype(np.float32))
+            x = x - out[-1]
+        return out
+
+    left = np.zeros((64, LANES), np.float32)
+    for c in range(3):
+        parts = pieces(-2.0 * points[:, c])
+        for n, piece in enumerate((0, 0, 0, 1, 1, 2)):
+            left[:, 6 * c + n] = parts[piece]
+    at = 18 + 3 * (3 + 3 + sz)
+    for n, piece in enumerate(pieces((points * points).sum(1))):
+        left[:, at + n] = piece
+    at += 3 + 6 * (3 + 3 + sz)
+    left[:, at : at + 3] = 1.0
+    return np.asarray(left, BF16)
+
+
 def gather_constant(dims):
     sx, sy, _ = dims
     cells = [(x + REACH, y + REACH) for x in range(sx) for y in range(sy)]
@@ -173,22 +199,11 @@
     return pick
 
 
-def prepare_kernel(ops, tail, token, table, raw, sems):
-    width = ops.shape[1]
+def prepare_kernel(raw, table):
     tiles = raw.shape[0]
-    whole = tiles - 1
-
-    def fetch(j):
-        return pltpu.make_async_copy(ops.at[:, pl.ds(j * LANES, LANES)], raw.at[j], sems.at[j])
-
-    for j in range(whole):
-        fetch(j).start()
-    raw[tiles - 1] = tail[...]
     ab = lax.broadcasted_iota(jnp.int32, (64, LANES), 0)
     closeby = (jnp.abs(ab // SPAN - REACH) <= 1) & (jnp.abs(ab % SPAN - REACH) <= 1)
     for j in range(tiles):
-        if j < whole:
-            fetch(j).wait()
         for c in range(SPAN):
             block = raw[j, pl.ds(c, SPAN * SPAN, stride=SPAN), :]
             block = jnp.concatenate(
@@ -196,9 +211,6 @@
             )
             if abs(c - REACH) <= 1:
                 block = jnp.where(closeby, 0.0, block)
-            if (j + 1) * LANES > width:
-                lane = lax.broadcasted_iota(jnp.int32, (64, LANES), 1)
-                block = jnp.where(lane < width - j * LANES, block, 0.0)
             hi, lo = split2(block)
             table[c * 64 : (c + 1) * 64, 2 * j * LANES : (2 * j + 1) * LANES] = hi
             table[c * 64 : (c + 1) * 64, (2 * j + 1) * LANES : (2 * j + 2) * LANES] = lo
@@ -224,7 +236,8 @@
         lhs[at : at + LANES, :] = features_of(feats, half, i).T.astype(BF16)
 
 
-def near_sums(sz, lhs, rhs, total, src, targets):
+def near_sums(dims, lhs, rhs, total, src, targets):
+    sz = dims[2]
     halves = [[h for h in range(2) if any(abs(z - t) <= 1 for t in (2 * h, 2 * h + 1))] for z in range(sz)]
 
     def add(target, half, d2):
@@ -255,7 +268,9 @@
                 add(target, half, d2[:, n * LANES : (n + 1) * LANES])
 
 
-def near_own_kernel(dims, own, near, rhs, token, feats, lhs, rfeats):
+def near_own_kernel(
+    dims, own, near, rhs, token, feats, lhs, rfeats
+):
     sx, sy, sz = dims
     cols = sx * sy
     token[...] = own[0:8, 0:LANES]
@@ -278,14 +293,9 @@
             lanes = slice(half * LANES, (half + 1) * LANES)
             rhs[i * LANES : (i + 1) * LANES, lanes] = features_of(rfeats, half, i).astype(BF16)
     near[...] = jnp.zeros_like(near)
-    for x in range(sx):
-        for y in range(sy):
-            targets = [
-                a * sy + b
-                for a in range(max(x - 1, 0), min(x + 2, sx))
-                for b in range(max(y - 1, 0), min(y + 2, sy))
-            ]
-            near_sums(sz, lhs, rhs, near, x * sy + y, targets)
+    for i in range(cols):
+        cell = (i // sy + 1, i % sy + 1)
+        near_sums(dims, lhs, rhs, near, i, targets_of(dims, cell))
 
 
 def targets_of(dims, cell):
@@ -298,7 +308,10 @@
     ]
 
 
-def near_row_kernel(dims, got_a, got_b, near_own, rhs, token, near, slots, feats, lhs):
+def near_row_kernel(
+    dims, got_a, got_b, near_own, rhs, parents, l2l, spread, surface, ops, token,
+    near, inherited, inverse, raw, slots, feats, lhs,
+):
     sx, sy, sz = dims
     base = REACH * sy
     odd = is_odd("row")
@@ -316,18 +329,38 @@
         fill_features(sz, place, su, feats, at)
     for i in range(2 * sy):
         turn_features(feats, lhs, i)
+    rows = []
+    for pz in range(sz // 2):
+        for x in range(sx // 2):
+            rows.append(parents[x, :, pz * Q : (pz + 1) * Q])
+    above = jnp.concatenate(rows, axis=0)
+    below = jnp.concatenate([dot3(above, l2l[o]) for o in range(8)], axis=0)
+    below_hi, below_lo = split2(below)
+    inherited[...] = dot(spread[...], below_hi) + dot(spread[...], below_lo)
     near[...] = near_own[...]
+    width = ops.shape[1]
+    left = list(range(raw.shape[0]))
     for i in range(2 * sy):
         cell = ((sx + 1) * (i // sy), i % sy + 1)
-        near_sums(sz, lhs, rhs, near, i, targets_of(dims, cell))
+        near_sums(dims, lhs, rhs, near, i, targets_of(dims, cell))
+        for n in range(i * sx // 2, (i + 1) * sx // 2):
+            d2 = dot(surface[...], rhs[n * LANES : (n + 1) * LANES, :])
+            hi, lo = split2(lax.rsqrt(d2))
+            inverse[n * LANES : n * LANES + 64, :] = hi
+            inverse[n * LANES + 64 : (n + 1) * LANES, :] = lo
+        for _ in range(-(-len(left) // (2 * sy - i))):
+            j = left.pop(0)
+            lanes = min(LANES, width - j * LANES)
+            raw[j, :, 0:lanes] = ops[:, j * LANES : j * LANES + lanes]
+            if lanes < LANES:
+                raw[j, :, lanes:LANES] = jnp.zeros((ops.shape[0], LANES - lanes), F32)
 
 
 def fields_kernel(
     dims,
-    own, a1, b1, a2, b2, near_own, rhs, table, parents, l2l, c2e, pick,
-    spread, points,
+    own, a1, b1, a2, b2, near_own, rhs, table, inverse, inherited, c2e, pick,
     potential, local_out,
-    halo_slots, feats, lhs, near, sm, picked, lm, dens, inherited,
+    halo_slots, feats, lhs, near, sm, picked, lm, dens,
 ):
     sx, sy, sz = dims
     hx, hy = sx + 2, sy + 2
@@ -357,14 +390,6 @@
         return jnp.where(second, rows - hx, rows), jnp.where(second, hy - 1, 0)
 
     halo = {(x, (hy - 1) * side): side * hx + x for side in range(2) for x in range(hx)}
-
-    rows = []
-    for pz in range(sz // 2):
-        for x in range(sx // 2):
-            rows.append(parents[x, :, pz * Q : (pz + 1) * Q])
-    above = jnp.concatenate(rows, axis=0)
-    below = jnp.concatenate([dot_exact(above, l2l[o]) for o in range(8)], axis=0)
-    inherited[...] = dot_exact(spread[...], below)
 
     for pair in range(sz // 2):
         his, los = [], []
@@ -441,9 +466,7 @@
     assert not groups and not turns
 
     field = jnp.concatenate([part[:, 0:Q] for part in check], axis=0) + inherited[...]
-    field_hi, field_lo = split2(field)
-    map_hi, map_lo = split2(c2e[...])
-    local = dot(field_hi, map_hi) + (dot(field_hi, map_lo) + dot(field_lo, map_hi))
+    local = dot3(field, c2e[...])
     dens[...] = jnp.zeros_like(dens)
     dens[0 : sz * cols, 0:Q] = local
     flat = None
@@ -456,25 +479,18 @@
     for x in range(sx):
         local_out[x] = flat[x * sy : (x + 1) * sy, 0 : sz * Q]
 
-    turned = dens[...].T[0:64, :]
-    hi, lo = split2(turned[:, 0 : sz * cols])
-    weights = jnp.concatenate([hi.astype(F32), lo.astype(F32)], axis=1).astype(BF16)
-    row = lax.broadcasted_iota(jnp.int32, (2 * sz * cols, sz * CAP), 0) % (sz * cols)
-    lane = lax.broadcasted_iota(jnp.int32, (2 * sz * cols, sz * CAP), 1)
-    owner = row - (lane // CAP) * cols
+    hi, lo = split2(dens[0 : sz * cols, 0:64])
+    none = jnp.zeros_like(hi)
+    dens[0 : sz * cols, :] = jnp.concatenate([hi, hi], axis=1).astype(F32)
+    dens[sz * cols : 2 * sz * cols, :] = jnp.concatenate([lo, none], axis=1).astype(F32)
+    row = lax.broadcasted_iota(jnp.int32, (2 * sz, sz * CAP), 0) % sz
+    mine = row == lax.broadcasted_iota(jnp.int32, (2 * sz, sz * CAP), 1) // CAP
 
     def far(i):
-        one_hot = jnp.where(owner == i, 1.0, 0.0).astype(BF16)
-        spread_out = dot(weights, one_hot)
-        for half in range(2):
-            lanes = slice(half * LANES, (half + 1) * LANES)
-            d2 = jnp.zeros((64, LANES), F32)
-            for c in range(3):
-                gap = own[c * cols + i : c * cols + i + 1, lanes] - points[c]
-                d2 = d2 + gap * gap
-            part = spread_out[:, lanes] * lax.rsqrt(d2)
-            at = slice(i * 8, (i + 1) * 8)
-            near[at, lanes] = near[at, lanes] + jnp.sum(part.reshape(8, 8, LANES), axis=0)
+        pieces = dens[pl.ds(i, 2 * sz, stride=cols), :].astype(BF16)
+        value = dot(pieces, inverse[i * LANES : (i + 1) * LANES, :])
+        at = slice(i * 8, i * 8 + 2 * sz)
+        near[at, :] = near[at, :] + jnp.where(mine, value, 0.0)
 
     near[...] = near_own[...]
     left = list(range(cols))
@@ -482,7 +498,7 @@
         for _ in range(2):
             if left:
                 far(left.pop(0))
-        near_sums(sz, lhs, rhs, near, src, targets_of(dims, cell))
+        near_sums(dims, lhs, rhs, near, src, targets_of(dims, cell))
     assert not left
     for i in range(cols):
         x, y = i // sy, i % sy
@@ -562,6 +578,9 @@
             for piece in (0, 1, 2, 0, 1, 0):
                 yield k, parts[piece]
                 k += 1
+    for piece in split3(arrays[0] * arrays[0] + arrays[1] * arrays[1] + arrays[2] * arrays[2]):
+        yield k, piece
+        k += 1
     while k < LANES:
         yield k, jnp.zeros(shape, F32)
         k += 1
@@ -581,7 +600,11 @@
     shape = jax.ShapeDtypeStruct((round_up((REACH + 4) * sy, 8), sz * CAP), F32)
     return pl.pallas_call(
         functools.partial(pack_row_kernel, dims),
-        out_shape=(shape, shape, jax.ShapeDtypeStruct((5 * sx * sy, sz * CAP), F32)),
+        out_shape=(
+            shape,
+            shape,
+            jax.ShapeDtypeStruct((5 * sx * sy, sz * CAP), F32),
+        ),
         in_specs=[HBM] * 4,
         out_specs=(VMEM,) * 3,
         scratch_shapes=[
@@ -596,23 +619,17 @@
     )(*(pltpu.with_memory_space_constraint(a, pltpu.HBM) for a in (pos, mass, counts, poles)))
 
 
-def prepare(ops, token):
-    rows, width = ops.shape
-    tiles = -(-width // LANES)
-    tail = jnp.pad(ops[:, (tiles - 1) * LANES :], ((0, 0), (0, tiles * LANES - width)))
+def prepare(raw):
+    tiles = raw.shape[0]
     return pl.pallas_call(
         prepare_kernel,
         out_shape=jax.ShapeDtypeStruct((SPAN * 64, 2 * tiles * LANES), BF16),
-        in_specs=[HBM, VMEM, VMEM],
+        in_specs=[VMEM],
         out_specs=VMEM,
-        scratch_shapes=[
-            pltpu.VMEM((tiles, rows, LANES), F32),
-            pltpu.SemaphoreType.DMA((tiles,)),
-        ],
-        compiler_params=pltpu.CompilerParams(vmem_limit_bytes=12 << 20),
+        compiler_params=pltpu.CompilerParams(vmem_limit_bytes=4 << 20),
         cost_estimate=pl.CostEstimate(flops=1 << 24, bytes_accessed=10 << 20, transcendentals=0),
         name="prepare",
-    )(ops, tail, token)
+    )(raw)
 
 
 def pack_col(dims, own, got_a, got_b, token):
@@ -633,11 +650,12 @@
 def near_own(dims, own):
     sx, sy, sz = dims
     cols = sx * sy
+    operand = jax.ShapeDtypeStruct((cols * LANES, sz * CAP), BF16)
     return pl.pallas_call(
         functools.partial(near_own_kernel, dims),
         out_shape=(
             jax.ShapeDtypeStruct((cols * 8, sz * CAP), F32),
-            jax.ShapeDtypeStruct((cols * LANES, sz * CAP), BF16),
+            operand,
             jax.ShapeDtypeStruct((8, LANES), F32),
         ),
         in_specs=[VMEM],
@@ -647,20 +665,29 @@
             pltpu.VMEM((cols * sz * CAP, LANES), BF16),
             pltpu.VMEM((2, cols * LANES, LANES), F32),
         ],
-        compiler_params=pltpu.CompilerParams(vmem_limit_bytes=10 << 20),
+        compiler_params=pltpu.CompilerParams(vmem_limit_bytes=9 << 20),
         cost_estimate=pl.CostEstimate(flops=1 << 32, bytes_accessed=1 << 20, transcendentals=1 << 22),
         name="near_own",
     )(own)
 
 
-def near_row(dims, got_a, got_b, near, rhs, token):
-    sx, sy, sz = dims
+def near_row(dims, got_a, got_b, near, rhs, parents, l2l, ops, token):
+    sx, sy, sz = dims
+    cols = sx * sy
     slots = round_up(2 * sy, 8)
+    rows, width = ops.shape
+    surface = jnp.asarray(surface_features(sz))
+    spread = jnp.asarray(spread_constant(dims), BF16)
     return pl.pallas_call(
         functools.partial(near_row_kernel, dims),
-        out_shape=jax.ShapeDtypeStruct(near.shape, F32),
-        in_specs=[VMEM] * 5,
-        out_specs=VMEM,
+        out_shape=(
+            jax.ShapeDtypeStruct((cols * 8, sz * CAP), F32),
+            jax.ShapeDtypeStruct((sz * cols, Q), F32),
+            jax.ShapeDtypeStruct(rhs.shape, BF16),
+            jax.ShapeDtypeStruct((-(-width // LANES), rows, LANES), F32),
+        ),
+        in_specs=[VMEM] * 10,
+        out_specs=(VMEM,) * 4,
         scratch_shapes=[
             pltpu.VMEM((4, slots, sz * CAP), F32),
             pltpu.VMEM((2, slots * LANES, LANES), F32),
@@ -669,40 +696,35 @@
         compiler_params=pltpu.CompilerParams(vmem_limit_bytes=6 << 20),
         cost_estimate=pl.CostEstimate(flops=1 << 30, bytes_accessed=1 << 20, transcendentals=1 << 20),
         name="near_row",
-    )(got_a, got_b, near, rhs, token)
-
-
-def fields(dims, own, a1, b1, a2, b2, near, rhs, table, parents, l2l, c2e):
+    )(got_a, got_b, near, rhs, parents, l2l, spread, surface, ops, token)
+
+
+def fields(dims, own, a1, b1, a2, b2, near, rhs, table, inverse, inherited, c2e):
     sx, sy, sz = dims
     cols = sx * sy
     ring = 2 * (sx + 2)
     pick = jnp.asarray(gather_constant(dims), BF16)
-    spread = jnp.asarray(spread_constant(dims))
-    points = np.full((3, 64, LANES), 10.0, np.float32)
-    points[:, :Q, :] = surface_points().T[:, :, None] - 0.5
     return pl.pallas_call(
         functools.partial(fields_kernel, dims),
         out_shape=(
             jax.ShapeDtypeStruct((sx, sy, sz * CAP), F32),
             jax.ShapeDtypeStruct((sx, sy, sz * Q), F32),
         ),
-        in_specs=[VMEM] * 14,
+        in_specs=[VMEM] * 12,
         out_specs=(VMEM, VMEM),
         scratch_shapes=[
             pltpu.VMEM((4, round_up(ring, 8), sz * CAP), F32),
             pltpu.VMEM((2, round_up(ring, 8) * LANES, LANES), F32),
             pltpu.VMEM((ring * sz * CAP, LANES), BF16),
-            pltpu.VMEM((cols * 8, sz * CAP), F32),
+            pltpu.VMEM(near.shape, F32),
             pltpu.VMEM((LANES, 2 * LANES), F32),
             pltpu.VMEM((LANES, 2 * LANES), BF16),
             pltpu.VMEM((sz // 2, cols * PITCH, LANES), F32),
             pltpu.VMEM((LANES, LANES), F32),
-            pltpu.VMEM((sz * cols, Q), F32),
         ],
         compiler_params=pltpu.CompilerParams(vmem_limit_bytes=16 << 20),
         name="fields",
-    )(own, a1, b1, a2, b2, near, rhs, table, parents, l2l, c2e, pick, spread,
-      jnp.asarray(points))
+    )(own, a1, b1, a2, b2, near, rhs, table, inverse, inherited, c2e, pick)
 
 
 def exchange(send_a, send_b, axis):
@@ -722,10 +744,12 @@
     near, rhs, token = near_own(dims, own)
     send_a, send_b, token = pack_col(dims, own, a1, b1, token)
     a2, b2 = exchange(send_a, send_b, "col")
-    table = prepare(m2l_ops, token)
-    near = near_row(dims, a1, b1, near, rhs, token)
+    near, inherited, inverse, raw = near_row(
+        dims, a1, b1, near, rhs, parent_local, l2l_ops, m2l_ops, token
+    )
+    table = prepare(raw)
     return fields(
-        dims, own, a1, b1, a2, b2, near, rhs, table, parent_local, l2l_ops, check_to_equiv
+        dims, own, a1, b1, a2, b2, near, rhs, table, inverse, inherited, check_to_equiv
     )
 
 

time: 22.2 us -> 21.8 us (0.982)
  Pallas kernels: 12.2 us -> 11.6 us
    pallas_call x1, Pallas kernels: 1.6 us -> 0.97 us  [prepare(): pl.pallas_call(prepare_kernel, out_shape=jax.ShapeDtypeStruct((SPAN * 64,...]
    pallas_call x1, Pallas kernels: 0.9 us -> 1.37 us  [near_row(): pl.pallas_call(functools.partial(near_row_kernel, dims), out_shape=(jax.S...]
    pallas_call x1, Pallas kernels: 5.29 us -> 4.83 us  [fields(): pl.pallas_call(functools.partial(fields_kernel, dims), out_shape=(jax.Sha...]
where the time goes in v5:
time: 21.8 us; the launch traced here: 21.5 us
  Pallas kernels  11.6 us (53%)
  starting transfers between devices  8.82 us (40%)
  between operations  0.81 us (4%)
  local copies, waits for them, and re-layouts  0.25 us (1%)
    ppermute x4, starting transfers between devices, exchange(): got.append(lax.ppermute(value, axis, pairs + [(b, a) for a, b in pairs]))  8.82 us
    pallas_call x1, Pallas kernels, fields(): pl.pallas_call(functools.partial(fields_kernel, dims), out_shape=(jax.Sha...  4.83 us
    pallas_call x1, Pallas kernels, near_own(): pl.pallas_call(functools.partial(near_own_kernel, dims), out_shape=(jax.S...  3.44 us
    pallas_call x1, Pallas kernels, near_row(): pl.pallas_call(functools.partial(near_row_kernel, dims), out_shape=(jax.S...  1.37 us
    pallas_call x1, Pallas kernels, prepare(): pl.pallas_call(prepare_kernel, out_shape=jax.ShapeDtypeStruct((SPAN * 64,...  0.97 us
    pallas_call x1, Pallas kernels, pack_row(): pl.pallas_call(functools.partial(pack_row_kernel, dims), out_shape=(shape...  0.9 us
  transfers between devices with their start and end apart: 4, of which 0 were waited for; matrix products, arithmetic and copies ran while one was open for 0% of the time, Pallas kernels for 27%

profile of v5, /device:TPU:19, one launch (start us, length us, event | category | flops | bytes accessed | tf_op | source)
XLA Modules:
  0.0 21.5 jit_solution(10979227199520341769)
XLA Ops:
  0.6 0.9 %pack_row.1 = (f32[32,256]{1,0:T(8,128)S(1)}, f32[32,256]{1,0:T(8,128)S(1)}, f32[80,256]{1,0:T(8,128)S(1)}) custom-call(f32[3,4,4,256]{3,2,1,0:T(4,128)} %pos_far.1, f32[4,4,256]{2,1,0:T(4,128)} %mass_far.1, s32[4,4,4]{2,1,0:T(4,128)} %counts_far.1, f32[4,4,224]{2,1,0:T(4,128)} %poles_far.1), custom_call_target="tpu_custom_call" | custom-call | tf_op jit(solution)/shard_map/pack_row/pallas_call | solution.py:601
  1.5 0.3 %collective-permute-start = (f32[32,256]{1,0:T(8,128)S(1)}, f32[32,256]{1,0:T(8,128)S(1)}, u32[]{:S(2)}, u32[]{:S(2)}) collective-permute-start(f32[32,256]{1,0:T(8,128)S(1)} %get-tuple-element.16), channel_id=1, source_target_pairs={{0,4},{8,12},{16,20},{24,28},{4,0},{12,8},{20,16},{28,24},{1,5},{9... | collective-permute-start | bytes 98312 | tf_op jit(solution)/shard_map/ppermute | solution.py:735
  1.9 4.1 %collective-permute-start.1 = (f32[32,256]{1,0:T(8,128)S(1)}, f32[32,256]{1,0:T(8,128)S(1)}, u32[]{:S(2)}, u32[]{:S(2)}) collective-permute-start(f32[32,256]{1,0:T(8,128)S(1)} %get-tuple-element.17), channel_id=1, source_target_pairs={{4,8},{12,16},{20,24},{8,4},{16,12},{24,20},{5,9},{13,17},{21,25},... | collective-permute-start | bytes 98312 | tf_op jit(solution)/shard_map/ppermute | solution.py:735
  6.0 0.0 copy-start
  6.0 0.0 copy-start.2
  6.0 0.0 copy-start.4
  6.0 0.0 copy-start.5
  6.0 0.0 copy-start.6
  6.0 3.4 %near_own.1 = (f32[128,256]{1,0:T(8,128)S(1)}, bf16[2048,256]{1,0:T(8,128)(2,1)S(1)}, f32[8,128]{1,0:T(8,128)S(1)}) custom-call(f32[80,256]{1,0:T(8,128)S(1)} %get-tuple-element.15.own), custom_call_target="tpu_custom_call" | custom-call | flops 4294967296 | bytes 1048576 | tf_op jit(solution)/shard_map/near_own/pallas_call | solution.py:654
  9.5 0.0 collective-permute-done.got_a.a1
  9.5 0.0 collective-permute-done.1.got_b.b1
  9.5 0.1 pack_col.1
  9.6 1.3 %collective-permute-start.2 = (f32[56,256]{1,0:T(8,128)S(1)}, f32[56,256]{1,0:T(8,128)S(1)}, u32[]{:S(2)}, u32[]{:S(2)}) collective-permute-start(f32[56,256]{1,0:T(8,128)S(1)} %get-tuple-element.19), channel_id=1, source_target_pairs={{0,1},{2,3},{1,0},{3,2},{4,5},{6,7},{5,4},{7,6},{8,9},{10,11},{9,8... | collective-permute-start | bytes 172040 | tf_op jit(solution)/shard_map/ppermute | solution.py:735
  10.9 3.0 %collective-permute-start.3 = (f32[56,256]{1,0:T(8,128)S(1)}, f32[56,256]{1,0:T(8,128)S(1)}, u32[]{:S(2)}, u32[]{:S(2)}) collective-permute-start(f32[56,256]{1,0:T(8,128)S(1)} %get-tuple-element.20), channel_id=1, source_target_pairs={{1,2},{2,1},{5,6},{6,5},{9,10},{10,9},{13,14},{14,13},{17,18},{18,... | collective-permute-start | bytes 172040 | tf_op jit(solution)/shard_map/ppermute | solution.py:735
  14.0 0.0 copy-done
  14.0 0.0 copy-done.2
  14.0 0.0 copy-done.4
  14.0 0.0 copy-done.5
  14.0 0.0 copy-done.6
  14.0 1.4 %near_row.1 = (f32[128,256]{1,0:T(8,128)S(1)}, f32[64,56]{1,0:T(8,128)S(1)}, bf16[2048,256]{1,0:T(8,128)(2,1)S(1)}, f32[25,343,128]{2,1,0:T(8,128)S(1)}) custom-call(f32[32,256]{1,0:T(8,128)S(1)} %collective-permute-done.got_a.a1, f32[32,256]{1,0:T(8,128)S(1)} %collective-permute-done.1.got_b.b1, f32[128,256]{1,0:T(8,128)S(1)} %get-tuple-element.21.near_own, ...), custom_call_target="tpu_custom_call" | custom-call | flops 1073741824 | bytes 1048576 | tf_op jit(solution)/shard_map/near_row/pallas_call | solution.py:681
  15.4 0.0 copy-start.1
  15.4 0.0 copy-start.3
  15.4 1.0 %prepare.1.table = bf16[448,6400]{1,0:T(8,128)(2,1)S(1)} custom-call(f32[25,343,128]{2,1,0:T(8,128)S(1)} %get-tuple-element.25.raw), custom_call_target="tpu_custom_call" | custom-call | flops 16777216 | bytes 10485760 | tf_op jit(solution)/shard_map/prepare/pallas_call | solution.py:624
  16.4 0.0 collective-permute-done.2.a2
  16.4 0.0 collective-permute-done.3.b2
  16.4 0.2 copy-done.1
  16.6 0.0 copy-done.3
  16.6 4.8 %fields.1 = (f32[4,4,256]{2,1,0:T(4,128)}, f32[4,4,224]{2,1,0:T(4,128)}) custom-call(f32[80,256]{1,0:T(8,128)S(1)} %get-tuple-element.15.own, f32[32,256]{1,0:T(8,128)S(1)} %collective-permute-done.got_a.a1, f32[32,256]{1,0:T(8,128)S(1)} %collective-permute-done.1.got_b.b1, f32[56,256]{1,0:T(8,128)S(1)} %collective-permute-done.2.a2, ...), custom_call_target="tpu_custom_call" | custom-call | tf_op jit(solution)/shard_map/fields/pallas_call | solution.py:707
Async XLA Ops:
  1.5 8.0 %collective-permute-start = (f32[32,256]{1,0:T(8,128)S(1)}, f32[32,256]{1,0:T(8,128)S(1)}, u32[]{:S(2)}, u32[]{:S(2)}) collective-permute-start(f32[32,256]{1,0:T(8,128)S(1)} %get-tuple-element.16), channel_id=1, source_target_pairs={{0,4},{8,12},{16,20},{24,28},{4,0},{12,8},{20,16},{28,24},{1,5},{9... | collective-permute-start | bytes 98312 | tf_op jit(solution)/shard_map/ppermute | solution.py:735
  1.9 7.7 %collective-permute-start.1 = (f32[32,256]{1,0:T(8,128)S(1)}, f32[32,256]{1,0:T(8,128)S(1)}, u32[]{:S(2)}, u32[]{:S(2)}) collective-permute-start(f32[32,256]{1,0:T(8,128)S(1)} %get-tuple-element.17), channel_id=1, source_target_pairs={{4,8},{12,16},{20,24},{8,4},{16,12},{24,20},{5,9},{13,17},{21,25},... | collective-permute-start | bytes 98312 | tf_op jit(solution)/shard_map/ppermute | solution.py:735
  6.0 8.0 %copy-start = (f32[343,3136]{1,0:T(8,128)S(1)}, f32[343,3136]{1,0:T(8,128)}, u32[]{:S(2)}) copy-start(f32[343,3136]{1,0:T(8,128)} %ops.1) | copy-start | bytes 12907780
  6.0 8.0 %copy-start.2 = (f32[8,56,56]{2,1,0:T(8,128)S(1)}, f32[8,56,56]{2,1,0:T(8,128)}, u32[]{:S(2)}) copy-start(f32[8,56,56]{2,1,0:T(8,128)} %l2l.1) | copy-start | bytes 301060
  6.0 8.0 %copy-start.4 = (bf16[64,64]{1,0:T(8,128)(2,1)S(1)}, bf16[64,64]{1,0:T(8,128)(2,1)}, u32[]{:S(2)}) copy-start(bf16[64,64]{1,0:T(8,128)(2,1)} %constant.7.clone.spread) | copy-start | bytes 24580
  6.0 8.0 %copy-start.5 = (bf16[64,128]{1,0:T(8,128)(2,1)S(1)}, bf16[64,128]{1,0:T(8,128)(2,1)}, u32[]{:S(2)}) copy-start(bf16[64,128]{1,0:T(8,128)(2,1)} %constant.6.clone.surface) | copy-start | bytes 49156
  6.0 8.0 %copy-start.6 = (f32[2,2,112]{2,1,0:T(2,128)S(1)}, f32[2,2,112]{2,1,0:T(2,128)}, u32[]{:S(2)}) copy-start(f32[2,2,112]{2,1,0:T(2,128)} %parents.1) | copy-start | bytes 5380
  9.6 6.8 %collective-permute-start.2 = (f32[56,256]{1,0:T(8,128)S(1)}, f32[56,256]{1,0:T(8,128)S(1)}, u32[]{:S(2)}, u32[]{:S(2)}) collective-permute-start(f32[56,256]{1,0:T(8,128)S(1)} %get-tuple-element.19), channel_id=1, source_target_pairs={{0,1},{2,3},{1,0},{3,2},{4,5},{6,7},{5,4},{7,6},{8,9},{10,11},{9,8... | collective-permute-start | bytes 172040 | tf_op jit(solution)/shard_map/ppermute | solution.py:735
  10.9 5.5 %collective-permute-start.3 = (f32[56,256]{1,0:T(8,128)S(1)}, f32[56,256]{1,0:T(8,128)S(1)}, u32[]{:S(2)}, u32[]{:S(2)}) collective-permute-start(f32[56,256]{1,0:T(8,128)S(1)} %get-tuple-element.20), channel_id=1, source_target_pairs={{1,2},{2,1},{5,6},{6,5},{9,10},{10,9},{13,14},{14,13},{17,18},{18,... | collective-permute-start | bytes 172040 | tf_op jit(solution)/shard_map/ppermute | solution.py:735
  15.4 1.2 %copy-start.1 = (bf16[256,2048]{1,0:T(8,128)(2,1)S(1)}, bf16[256,2048]{1,0:T(8,128)(2,1)}, u32[]{:S(2)}) copy-start(bf16[256,2048]{1,0:T(8,128)(2,1)} %constant.8.clone.pick) | copy-start | bytes 3145732
  15.4 1.2 %copy-start.3 = (f32[56,56]{1,0:T(8,128)S(1)}, f32[56,56]{1,0:T(8,128)}, u32[]{:S(2)}) copy-start(f32[56,56]{1,0:T(8,128)} %c2e.1) | copy-start | bytes 37636

commit v6 on v5

--- a/solution.py
+++ b/solution.py
@@ -391,6 +391,11 @@
 
     halo = {(x, (hy - 1) * side): side * hx + x for side in range(2) for x in range(hx)}
 
+    for at in range(0, halo_slots.shape[1], 8):
+        fill_features(sz, place, su, feats, at)
+    for i in range(len(halo)):
+        turn_features(feats, lhs, i)
+
     for pair in range(sz // 2):
         his, los = [], []
         for zi in range(2):
@@ -412,15 +417,10 @@
     period = 16
     lane16 = lax.broadcasted_iota(jnp.int32, (cols, LANES), 1)
     check = [jnp.zeros((cols, LANES), F32) for _ in range(sz)]
-    groups = list(range(0, halo_slots.shape[1], 8))
-    turns = list(range(len(halo)))
+    near[...] = near_own[...]
+    sources = list(halo.items())
     spans = period * Q // LANES
     for t in range(spans):
-        if groups:
-            fill_features(sz, place, su, feats, groups.pop(0))
-        else:
-            for _ in range(-(-len(turns) // (spans - t))):
-                turn_features(feats, lhs, turns.pop(0))
         members = [s for s in range(period) if s * Q < (t + 1) * LANES and (s + 1) * Q > t * LANES]
         rows = len(members) * cols
         left = []
@@ -462,8 +462,10 @@
                 part = both[i * cols : (i + 1) * cols, :]
                 part = jnp.where((lane16 >= offset) & (lane16 < offset + Q), part, 0.0)
                 check[z] = check[z] + pltpu.roll(part, (-offset) % LANES, 1)
-
-    assert not groups and not turns
+        for _ in range(-(-len(sources) // (spans - t))):
+            cell, src = sources.pop(0)
+            near_sums(dims, lhs, rhs, near, src, targets_of(dims, cell))
+    assert not sources
 
     field = jnp.concatenate([part[:, 0:Q] for part in check], axis=0) + inherited[...]
     local = dot3(field, c2e[...])
@@ -492,14 +494,8 @@
         at = slice(i * 8, i * 8 + 2 * sz)
         near[at, :] = near[at, :] + jnp.where(mine, value, 0.0)
 
-    near[...] = near_own[...]
-    left = list(range(cols))
-    for cell, src in halo.items():
-        for _ in range(2):
-            if left:
-                far(left.pop(0))
-        near_sums(dims, lhs, rhs, near, src, targets_of(dims, cell))
-    assert not left
+    for i in range(cols):
+        far(i)
     for i in range(cols):
         x, y = i // sy, i % sy
         value = jnp.sum(near[i * 8 : (i + 1) * 8, :], axis=0, keepdims=True)
@@ -627,7 +623,7 @@
         in_specs=[VMEM],
         out_specs=VMEM,
         compiler_params=pltpu.CompilerParams(vmem_limit_bytes=4 << 20),
-        cost_estimate=pl.CostEstimate(flops=1 << 24, bytes_accessed=10 << 20, transcendentals=0),
+        cost_estimate=pl.CostEstimate(flops=1 << 24, bytes_accessed=1 << 20, transcendentals=0),
         name="prepare",
     )(raw)
 
@@ -694,7 +690,7 @@
             pltpu.VMEM((slots * sz * CAP, LANES), BF16),
         ],
         compiler_params=pltpu.CompilerParams(vmem_limit_bytes=6 << 20),
-        cost_estimate=pl.CostEstimate(flops=1 << 30, bytes_accessed=1 << 20, transcendentals=1 << 20),
+        cost_estimate=pl.CostEstimate(flops=1 << 26, bytes_accessed=1 << 20, transcendentals=0),
         name="near_row",
     )(got_a, got_b, near, rhs, parents, l2l, spread, surface, ops, token)
 

time: 21.8 us -> 21.6 us (level)
  no operation moved by 1% of the time
where the time goes in v6:
time: 21.6 us; the launch traced here: 21.3 us
  Pallas kernels  11.4 us (53%)
  starting transfers between devices  8.82 us (41%)
  between operations  0.81 us (4%)
  local copies, waits for them, and re-layouts  0.25 us (1%)
    ppermute x4, starting transfers between devices, exchange(): got.append(lax.ppermute(value, axis, pairs + [(b, a) for a, b in pairs]))  8.82 us
    pallas_call x1, Pallas kernels, fields(): pl.pallas_call(functools.partial(fields_kernel, dims), out_shape=(jax.Sha...  4.65 us
    pallas_call x1, Pallas kernels, near_own(): pl.pallas_call(functools.partial(near_own_kernel, dims), out_shape=(jax.S...  3.44 us
    pallas_call x1, Pallas kernels, near_row(): pl.pallas_call(functools.partial(near_row_kernel, dims), out_shape=(jax.S...  1.37 us
    pallas_call x1, Pallas kernels, prepare(): pl.pallas_call(prepare_kernel, out_shape=jax.ShapeDtypeStruct((SPAN * 64,...  0.97 us
    pallas_call x1, Pallas kernels, pack_row(): pl.pallas_call(functools.partial(pack_row_kernel, dims), out_shape=(shape...  0.9 us
  transfers between devices with their start and end apart: 4, of which 0 were waited for; matrix products, arithmetic and copies ran while one was open for 0% of the time, Pallas kernels for 27%

profile of v6, /device:TPU:19, one launch (start us, length us, event | category | flops | bytes accessed | tf_op | source)
XLA Modules:
  0.0 21.3 jit_solution(1573044867989307970)
XLA Ops:
  0.6 0.9 %pack_row.1 = (f32[32,256]{1,0:T(8,128)S(1)}, f32[32,256]{1,0:T(8,128)S(1)}, f32[80,256]{1,0:T(8,128)S(1)}) custom-call(f32[3,4,4,256]{3,2,1,0:T(4,128)} %pos_far.1, f32[4,4,256]{2,1,0:T(4,128)} %mass_far.1, s32[4,4,4]{2,1,0:T(4,128)} %counts_far.1, f32[4,4,224]{2,1,0:T(4,128)} %poles_far.1), custom_call_target="tpu_custom_call" | custom-call | tf_op jit(solution)/shard_map/pack_row/pallas_call | solution.py:597
  1.5 0.3 %collective-permute-start = (f32[32,256]{1,0:T(8,128)S(1)}, f32[32,256]{1,0:T(8,128)S(1)}, u32[]{:S(2)}, u32[]{:S(2)}) collective-permute-start(f32[32,256]{1,0:T(8,128)S(1)} %get-tuple-element.16), channel_id=1, source_target_pairs={{0,4},{8,12},{16,20},{24,28},{4,0},{12,8},{20,16},{28,24},{1,5},{9... | collective-permute-start | bytes 98312 | tf_op jit(solution)/shard_map/ppermute | solution.py:731
  1.9 4.1 %collective-permute-start.1 = (f32[32,256]{1,0:T(8,128)S(1)}, f32[32,256]{1,0:T(8,128)S(1)}, u32[]{:S(2)}, u32[]{:S(2)}) collective-permute-start(f32[32,256]{1,0:T(8,128)S(1)} %get-tuple-element.17), channel_id=1, source_target_pairs={{4,8},{12,16},{20,24},{8,4},{16,12},{24,20},{5,9},{13,17},{21,25},... | collective-permute-start | bytes 98312 | tf_op jit(solution)/shard_map/ppermute | solution.py:731
  6.0 0.0 copy-start
  6.0 0.0 copy-start.2
  6.0 0.0 copy-start.4
  6.0 0.0 copy-start.5
  6.0 0.0 copy-start.6
  6.0 3.4 %near_own.1 = (f32[128,256]{1,0:T(8,128)S(1)}, bf16[2048,256]{1,0:T(8,128)(2,1)S(1)}, f32[8,128]{1,0:T(8,128)S(1)}) custom-call(f32[80,256]{1,0:T(8,128)S(1)} %get-tuple-element.15.own), custom_call_target="tpu_custom_call" | custom-call | flops 4294967296 | bytes 1048576 | tf_op jit(solution)/shard_map/near_own/pallas_call | solution.py:650
  9.5 0.0 collective-permute-done.got_a.a1
  9.5 0.0 collective-permute-done.1.got_b.b1
  9.5 0.1 pack_col.1
  9.6 1.3 %collective-permute-start.2 = (f32[56,256]{1,0:T(8,128)S(1)}, f32[56,256]{1,0:T(8,128)S(1)}, u32[]{:S(2)}, u32[]{:S(2)}) collective-permute-start(f32[56,256]{1,0:T(8,128)S(1)} %get-tuple-element.19), channel_id=1, source_target_pairs={{0,1},{2,3},{1,0},{3,2},{4,5},{6,7},{5,4},{7,6},{8,9},{10,11},{9,8... | collective-permute-start | bytes 172040 | tf_op jit(solution)/shard_map/ppermute | solution.py:731
  10.9 3.0 %collective-permute-start.3 = (f32[56,256]{1,0:T(8,128)S(1)}, f32[56,256]{1,0:T(8,128)S(1)}, u32[]{:S(2)}, u32[]{:S(2)}) collective-permute-start(f32[56,256]{1,0:T(8,128)S(1)} %get-tuple-element.20), channel_id=1, source_target_pairs={{1,2},{2,1},{5,6},{6,5},{9,10},{10,9},{13,14},{14,13},{17,18},{18,... | collective-permute-start | bytes 172040 | tf_op jit(solution)/shard_map/ppermute | solution.py:731
  14.0 0.0 copy-done
  14.0 0.0 copy-done.2
  14.0 0.0 copy-done.4
  14.0 0.0 copy-done.5
  14.0 0.0 copy-done.6
  14.0 1.4 %near_row.1 = (f32[128,256]{1,0:T(8,128)S(1)}, f32[64,56]{1,0:T(8,128)S(1)}, bf16[2048,256]{1,0:T(8,128)(2,1)S(1)}, f32[25,343,128]{2,1,0:T(8,128)S(1)}) custom-call(f32[32,256]{1,0:T(8,128)S(1)} %collective-permute-done.got_a.a1, f32[32,256]{1,0:T(8,128)S(1)} %collective-permute-done.1.got_b.b1, f32[128,256]{1,0:T(8,128)S(1)} %get-tuple-element.21.near_own, ...), custom_call_target="tpu_custom_call" | custom-call | flops 67108864 | bytes 1048576 | tf_op jit(solution)/shard_map/near_row/pallas_call | solution.py:677
  15.4 0.0 copy-start.1
  15.4 0.0 copy-start.3
  15.4 1.0 %prepare.1.table = bf16[448,6400]{1,0:T(8,128)(2,1)S(1)} custom-call(f32[25,343,128]{2,1,0:T(8,128)S(1)} %get-tuple-element.25.raw), custom_call_target="tpu_custom_call" | custom-call | flops 16777216 | bytes 1048576 | tf_op jit(solution)/shard_map/prepare/pallas_call | solution.py:620
  16.4 0.0 collective-permute-done.2.a2
  16.4 0.0 collective-permute-done.3.b2
  16.4 0.2 copy-done.1
  16.6 0.0 copy-done.3
  16.6 4.6 %fields.1 = (f32[4,4,256]{2,1,0:T(4,128)}, f32[4,4,224]{2,1,0:T(4,128)}) custom-call(f32[80,256]{1,0:T(8,128)S(1)} %get-tuple-element.15.own, f32[32,256]{1,0:T(8,128)S(1)} %collective-permute-done.got_a.a1, f32[32,256]{1,0:T(8,128)S(1)} %collective-permute-done.1.got_b.b1, f32[56,256]{1,0:T(8,128)S(1)} %collective-permute-done.2.a2, ...), custom_call_target="tpu_custom_call" | custom-call | tf_op jit(solution)/shard_map/fields/pallas_call | solution.py:703
Async XLA Ops:
  1.5 8.0 %collective-permute-start = (f32[32,256]{1,0:T(8,128)S(1)}, f32[32,256]{1,0:T(8,128)S(1)}, u32[]{:S(2)}, u32[]{:S(2)}) collective-permute-start(f32[32,256]{1,0:T(8,128)S(1)} %get-tuple-element.16), channel_id=1, source_target_pairs={{0,4},{8,12},{16,20},{24,28},{4,0},{12,8},{20,16},{28,24},{1,5},{9... | collective-permute-start | bytes 98312 | tf_op jit(solution)/shard_map/ppermute | solution.py:731
  1.9 7.7 %collective-permute-start.1 = (f32[32,256]{1,0:T(8,128)S(1)}, f32[32,256]{1,0:T(8,128)S(1)}, u32[]{:S(2)}, u32[]{:S(2)}) collective-permute-start(f32[32,256]{1,0:T(8,128)S(1)} %get-tuple-element.17), channel_id=1, source_target_pairs={{4,8},{12,16},{20,24},{8,4},{16,12},{24,20},{5,9},{13,17},{21,25},... | collective-permute-start | bytes 98312 | tf_op jit(solution)/shard_map/ppermute | solution.py:731
  6.0 8.0 %copy-start = (f32[343,3136]{1,0:T(8,128)S(1)}, f32[343,3136]{1,0:T(8,128)}, u32[]{:S(2)}) copy-start(f32[343,3136]{1,0:T(8,128)} %ops.1) | copy-start | bytes 12907780
  6.0 8.0 %copy-start.2 = (f32[8,56,56]{2,1,0:T(8,128)S(1)}, f32[8,56,56]{2,1,0:T(8,128)}, u32[]{:S(2)}) copy-start(f32[8,56,56]{2,1,0:T(8,128)} %l2l.1) | copy-start | bytes 301060
  6.0 8.0 %copy-start.4 = (bf16[64,64]{1,0:T(8,128)(2,1)S(1)}, bf16[64,64]{1,0:T(8,128)(2,1)}, u32[]{:S(2)}) copy-start(bf16[64,64]{1,0:T(8,128)(2,1)} %constant.7.clone.spread) | copy-start | bytes 24580
  6.0 8.0 %copy-start.5 = (bf16[64,128]{1,0:T(8,128)(2,1)S(1)}, bf16[64,128]{1,0:T(8,128)(2,1)}, u32[]{:S(2)}) copy-start(bf16[64,128]{1,0:T(8,128)(2,1)} %constant.6.clone.surface) | copy-start | bytes 49156
  6.0 8.0 %copy-start.6 = (f32[2,2,112]{2,1,0:T(2,128)S(1)}, f32[2,2,112]{2,1,0:T(2,128)}, u32[]{:S(2)}) copy-start(f32[2,2,112]{2,1,0:T(2,128)} %parents.1) | copy-start | bytes 5380
  9.6 6.8 %collective-permute-start.2 = (f32[56,256]{1,0:T(8,128)S(1)}, f32[56,256]{1,0:T(8,128)S(1)}, u32[]{:S(2)}, u32[]{:S(2)}) collective-permute-start(f32[56,256]{1,0:T(8,128)S(1)} %get-tuple-element.19), channel_id=1, source_target_pairs={{0,1},{2,3},{1,0},{3,2},{4,5},{6,7},{5,4},{7,6},{8,9},{10,11},{9,8... | collective-permute-start | bytes 172040 | tf_op jit(solution)/shard_map/ppermute | solution.py:731
  10.9 5.5 %collective-permute-start.3 = (f32[56,256]{1,0:T(8,128)S(1)}, f32[56,256]{1,0:T(8,128)S(1)}, u32[]{:S(2)}, u32[]{:S(2)}) collective-permute-start(f32[56,256]{1,0:T(8,128)S(1)} %get-tuple-element.20), channel_id=1, source_target_pairs={{1,2},{2,1},{5,6},{6,5},{9,10},{10,9},{13,14},{14,13},{17,18},{18,... | collective-permute-start | bytes 172040 | tf_op jit(solution)/shard_map/ppermute | solution.py:731
  15.4 1.2 %copy-start.1 = (bf16[256,2048]{1,0:T(8,128)(2,1)S(1)}, bf16[256,2048]{1,0:T(8,128)(2,1)}, u32[]{:S(2)}) copy-start(bf16[256,2048]{1,0:T(8,128)(2,1)} %constant.8.clone.pick) | copy-start | bytes 3145732
  15.4 1.2 %copy-start.3 = (f32[56,56]{1,0:T(8,128)S(1)}, f32[56,56]{1,0:T(8,128)}, u32[]{:S(2)}) copy-start(f32[56,56]{1,0:T(8,128)} %c2e.1) | copy-start | bytes 37636

commit v7 on v6

--- a/solution.py
+++ b/solution.py
@@ -199,7 +199,7 @@
     return pick
 
 
-def prepare_kernel(raw, table):
+def prepare_kernel(raw, pick, table):
     tiles = raw.shape[0]
     ab = lax.broadcasted_iota(jnp.int32, (64, LANES), 0)
     closeby = (jnp.abs(ab // SPAN - REACH) <= 1) & (jnp.abs(ab % SPAN - REACH) <= 1)
@@ -615,17 +615,17 @@
     )(*(pltpu.with_memory_space_constraint(a, pltpu.HBM) for a in (pos, mass, counts, poles)))
 
 
-def prepare(raw):
+def prepare(raw, pick):
     tiles = raw.shape[0]
     return pl.pallas_call(
         prepare_kernel,
         out_shape=jax.ShapeDtypeStruct((SPAN * 64, 2 * tiles * LANES), BF16),
-        in_specs=[VMEM],
+        in_specs=[VMEM, VMEM],
         out_specs=VMEM,
         compiler_params=pltpu.CompilerParams(vmem_limit_bytes=4 << 20),
         cost_estimate=pl.CostEstimate(flops=1 << 24, bytes_accessed=1 << 20, transcendentals=0),
         name="prepare",
-    )(raw)
+    )(raw, pick)
 
 
 def pack_col(dims, own, got_a, got_b, token):
@@ -695,11 +695,10 @@
     )(got_a, got_b, near, rhs, parents, l2l, spread, surface, ops, token)
 
 
-def fields(dims, own, a1, b1, a2, b2, near, rhs, table, inverse, inherited, c2e):
+def fields(dims, own, a1, b1, a2, b2, near, rhs, table, inverse, inherited, c2e, pick):
     sx, sy, sz = dims
     cols = sx * sy
     ring = 2 * (sx + 2)
-    pick = jnp.asarray(gather_constant(dims), BF16)
     return pl.pallas_call(
         functools.partial(fields_kernel, dims),
         out_shape=(
@@ -743,9 +742,11 @@
     near, inherited, inverse, raw = near_row(
         dims, a1, b1, near, rhs, parent_local, l2l_ops, m2l_ops, token
     )
-    table = prepare(raw)
+    pick = jnp.asarray(gather_constant(dims), BF16)
+    table = prepare(raw, pick)
     return fields(
-        dims, own, a1, b1, a2, b2, near, rhs, table, inverse, inherited, check_to_equiv
+        dims, own, a1, b1, a2, b2, near, rhs, table, inverse, inherited, check_to_equiv,
+        pick,
     )
 
 

time: 21.6 us -> 21.5 us (level)
  no operation moved by 1% of the time
where the time goes in v7:
time: 21.5 us; the launch traced here: 21.2 us
  Pallas kernels  11.4 us (53%)
  starting transfers between devices  8.92 us (41%)
  between operations  0.83 us (4%)
    ppermute x4, starting transfers between devices, exchange(): got.append(lax.ppermute(value, axis, pairs + [(b, a) for a, b in pairs]))  8.92 us
    pallas_call x1, Pallas kernels, fields(): pl.pallas_call(functools.partial(fields_kernel, dims), out_shape=(jax.Sha...  4.66 us
    pallas_call x1, Pallas kernels, near_own(): pl.pallas_call(functools.partial(near_own_kernel, dims), out_shape=(jax.S...  3.42 us
    pallas_call x1, Pallas kernels, near_row(): pl.pallas_call(functools.partial(near_row_kernel, dims), out_shape=(jax.S...  1.36 us
    pallas_call x1, Pallas kernels, prepare(): pl.pallas_call(prepare_kernel, out_shape=jax.ShapeDtypeStruct((SPAN * 64,...  0.97 us
    pallas_call x1, Pallas kernels, pack_row(): pl.pallas_call(functools.partial(pack_row_kernel, dims), out_shape=(shape...  0.9 us
  transfers between devices with their start and end apart: 4, of which 0 were waited for; matrix products, arithmetic and copies ran while one was open for 0% of the time, Pallas kernels for 27%

profile of v7, /device:TPU:19, one launch (start us, length us, event | category | flops | bytes accessed | tf_op | source)
XLA Modules:
  0.0 21.2 jit_solution(17705061640830560641)
XLA Ops:
  0.6 0.9 %pack_row.1 = (f32[32,256]{1,0:T(8,128)S(1)}, f32[32,256]{1,0:T(8,128)S(1)}, f32[80,256]{1,0:T(8,128)S(1)}) custom-call(f32[3,4,4,256]{3,2,1,0:T(4,128)} %pos_far.1, f32[4,4,256]{2,1,0:T(4,128)} %mass_far.1, s32[4,4,4]{2,1,0:T(4,128)} %counts_far.1, f32[4,4,224]{2,1,0:T(4,128)} %poles_far.1), custom_call_target="tpu_custom_call" | custom-call | tf_op jit(solution)/shard_map/pack_row/pallas_call | solution.py:597
  1.5 0.3 %collective-permute-start = (f32[32,256]{1,0:T(8,128)S(1)}, f32[32,256]{1,0:T(8,128)S(1)}, u32[]{:S(2)}, u32[]{:S(2)}) collective-permute-start(f32[32,256]{1,0:T(8,128)S(1)} %get-tuple-element.16), channel_id=1, source_target_pairs={{0,4},{8,12},{16,20},{24,28},{4,0},{12,8},{20,16},{28,24},{1,5},{9... | collective-permute-start | bytes 98312 | tf_op jit(solution)/shard_map/ppermute | solution.py:730
  1.9 4.1 %collective-permute-start.1 = (f32[32,256]{1,0:T(8,128)S(1)}, f32[32,256]{1,0:T(8,128)S(1)}, u32[]{:S(2)}, u32[]{:S(2)}) collective-permute-start(f32[32,256]{1,0:T(8,128)S(1)} %get-tuple-element.17), channel_id=1, source_target_pairs={{4,8},{12,16},{20,24},{8,4},{16,12},{24,20},{5,9},{13,17},{21,25},... | collective-permute-start | bytes 98312 | tf_op jit(solution)/shard_map/ppermute | solution.py:730
  6.0 0.0 copy-start
  6.0 0.0 copy-start.2
  6.0 0.0 copy-start.4
  6.0 0.0 copy-start.5
  6.0 0.0 copy-start.6
  6.0 3.4 %near_own.1 = (f32[128,256]{1,0:T(8,128)S(1)}, bf16[2048,256]{1,0:T(8,128)(2,1)S(1)}, f32[8,128]{1,0:T(8,128)S(1)}) custom-call(f32[80,256]{1,0:T(8,128)S(1)} %get-tuple-element.15.own), custom_call_target="tpu_custom_call" | custom-call | flops 4294967296 | bytes 1048576 | tf_op jit(solution)/shard_map/near_own/pallas_call | solution.py:650
  9.5 0.0 copy-start.1
  9.5 0.0 collective-permute-done.got_a.a1
  9.5 0.0 collective-permute-done.1.got_b.b1
  9.5 0.1 pack_col.1
  9.6 1.3 %collective-permute-start.2 = (f32[56,256]{1,0:T(8,128)S(1)}, f32[56,256]{1,0:T(8,128)S(1)}, u32[]{:S(2)}, u32[]{:S(2)}) collective-permute-start(f32[56,256]{1,0:T(8,128)S(1)} %get-tuple-element.19), channel_id=1, source_target_pairs={{0,1},{2,3},{1,0},{3,2},{4,5},{6,7},{5,4},{7,6},{8,9},{10,11},{9,8... | collective-permute-start | bytes 172040 | tf_op jit(solution)/shard_map/ppermute | solution.py:730
  10.9 3.2 %collective-permute-start.3 = (f32[56,256]{1,0:T(8,128)S(1)}, f32[56,256]{1,0:T(8,128)S(1)}, u32[]{:S(2)}, u32[]{:S(2)}) collective-permute-start(f32[56,256]{1,0:T(8,128)S(1)} %get-tuple-element.20), channel_id=1, source_target_pairs={{1,2},{2,1},{5,6},{6,5},{9,10},{10,9},{13,14},{14,13},{17,18},{18,... | collective-permute-start | bytes 172040 | tf_op jit(solution)/shard_map/ppermute | solution.py:730
  14.1 0.0 copy-done
  14.1 0.0 copy-done.2
  14.1 0.0 copy-done.4
  14.1 0.0 copy-done.5
  14.1 0.0 copy-done.6
  14.1 1.4 %near_row.1 = (f32[128,256]{1,0:T(8,128)S(1)}, f32[64,56]{1,0:T(8,128)S(1)}, bf16[2048,256]{1,0:T(8,128)(2,1)S(1)}, f32[25,343,128]{2,1,0:T(8,128)S(1)}) custom-call(f32[32,256]{1,0:T(8,128)S(1)} %collective-permute-done.got_a.a1, f32[32,256]{1,0:T(8,128)S(1)} %collective-permute-done.1.got_b.b1, f32[128,256]{1,0:T(8,128)S(1)} %get-tuple-element.21.near_own, ...), custom_call_target="tpu_custom_call" | custom-call | flops 67108864 | bytes 1048576 | tf_op jit(solution)/shard_map/near_row/pallas_call | solution.py:677
  15.5 0.0 copy-done.1
  15.5 0.0 copy-start.3
  15.5 1.0 %prepare.1.table = bf16[448,6400]{1,0:T(8,128)(2,1)S(1)} custom-call(f32[25,343,128]{2,1,0:T(8,128)S(1)} %get-tuple-element.25.raw, bf16[256,2048]{1,0:T(8,128)(2,1)S(1)} %copy-done.1), custom_call_target="tpu_custom_call" | custom-call | flops 16777216 | bytes 1048576 | tf_op jit(solution)/shard_map/prepare/pallas_call | solution.py:620
  16.5 0.0 collective-permute-done.2.a2
  16.5 0.0 collective-permute-done.3.b2
  16.5 0.0 copy-done.3
  16.5 4.7 %fields.1 = (f32[4,4,256]{2,1,0:T(4,128)}, f32[4,4,224]{2,1,0:T(4,128)}) custom-call(f32[80,256]{1,0:T(8,128)S(1)} %get-tuple-element.15.own, f32[32,256]{1,0:T(8,128)S(1)} %collective-permute-done.got_a.a1, f32[32,256]{1,0:T(8,128)S(1)} %collective-permute-done.1.got_b.b1, f32[56,256]{1,0:T(8,128)S(1)} %collective-permute-done.2.a2, ...), custom_call_target="tpu_custom_call" | custom-call | tf_op jit(solution)/shard_map/fields/pallas_call | solution.py:702
Async XLA Ops:
  1.5 8.0 %collective-permute-start = (f32[32,256]{1,0:T(8,128)S(1)}, f32[32,256]{1,0:T(8,128)S(1)}, u32[]{:S(2)}, u32[]{:S(2)}) collective-permute-start(f32[32,256]{1,0:T(8,128)S(1)} %get-tuple-element.16), channel_id=1, source_target_pairs={{0,4},{8,12},{16,20},{24,28},{4,0},{12,8},{20,16},{28,24},{1,5},{9... | collective-permute-start | bytes 98312 | tf_op jit(solution)/shard_map/ppermute | solution.py:730
  1.9 7.6 %collective-permute-start.1 = (f32[32,256]{1,0:T(8,128)S(1)}, f32[32,256]{1,0:T(8,128)S(1)}, u32[]{:S(2)}, u32[]{:S(2)}) collective-permute-start(f32[32,256]{1,0:T(8,128)S(1)} %get-tuple-element.17), channel_id=1, source_target_pairs={{4,8},{12,16},{20,24},{8,4},{16,12},{24,20},{5,9},{13,17},{21,25},... | collective-permute-start | bytes 98312 | tf_op jit(solution)/shard_map/ppermute | solution.py:730
  6.0 8.1 %copy-start = (f32[343,3136]{1,0:T(8,128)S(1)}, f32[343,3136]{1,0:T(8,128)}, u32[]{:S(2)}) copy-start(f32[343,3136]{1,0:T(8,128)} %ops.1) | copy-start | bytes 12907780
  6.0 8.1 %copy-start.2 = (f32[8,56,56]{2,1,0:T(8,128)S(1)}, f32[8,56,56]{2,1,0:T(8,128)}, u32[]{:S(2)}) copy-start(f32[8,56,56]{2,1,0:T(8,128)} %l2l.1) | copy-start | bytes 301060
  6.0 8.1 %copy-start.4 = (bf16[64,64]{1,0:T(8,128)(2,1)S(1)}, bf16[64,64]{1,0:T(8,128)(2,1)}, u32[]{:S(2)}) copy-start(bf16[64,64]{1,0:T(8,128)(2,1)} %constant.7.clone.spread) | copy-start | bytes 24580
  6.0 8.1 %copy-start.5 = (bf16[64,128]{1,0:T(8,128)(2,1)S(1)}, bf16[64,128]{1,0:T(8,128)(2,1)}, u32[]{:S(2)}) copy-start(bf16[64,128]{1,0:T(8,128)(2,1)} %constant.6.clone.surface) | copy-start | bytes 49156
  6.0 8.1 %copy-start.6 = (f32[2,2,112]{2,1,0:T(2,128)S(1)}, f32[2,2,112]{2,1,0:T(2,128)}, u32[]{:S(2)}) copy-start(f32[2,2,112]{2,1,0:T(2,128)} %parents.1) | copy-start | bytes 5380
  9.5 6.0 %copy-start.1 = (bf16[256,2048]{1,0:T(8,128)(2,1)S(1)}, bf16[256,2048]{1,0:T(8,128)(2,1)}, u32[]{:S(2)}) copy-start(bf16[256,2048]{1,0:T(8,128)(2,1)} %constant.8.clone.pick) | copy-start | bytes 3145732
  9.6 6.9 %collective-permute-start.2 = (f32[56,256]{1,0:T(8,128)S(1)}, f32[56,256]{1,0:T(8,128)S(1)}, u32[]{:S(2)}, u32[]{:S(2)}) collective-permute-start(f32[56,256]{1,0:T(8,128)S(1)} %get-tuple-element.19), channel_id=1, source_target_pairs={{0,1},{2,3},{1,0},{3,2},{4,5},{6,7},{5,4},{7,6},{8,9},{10,11},{9,8... | collective-permute-start | bytes 172040 | tf_op jit(solution)/shard_map/ppermute | solution.py:730
  10.9 5.6 %collective-permute-start.3 = (f32[56,256]{1,0:T(8,128)S(1)}, f32[56,256]{1,0:T(8,128)S(1)}, u32[]{:S(2)}, u32[]{:S(2)}) collective-permute-start(f32[56,256]{1,0:T(8,128)S(1)} %get-tuple-element.20), channel_id=1, source_target_pairs={{1,2},{2,1},{5,6},{6,5},{9,10},{10,9},{13,14},{14,13},{17,18},{18,... | collective-permute-start | bytes 172040 | tf_op jit(solution)/shard_map/ppermute | solution.py:730
  15.5 1.0 %copy-start.3 = (f32[56,56]{1,0:T(8,128)S(1)}, f32[56,56]{1,0:T(8,128)}, u32[]{:S(2)}) copy-start(f32[56,56]{1,0:T(8,128)} %c2e.1) | copy-start | bytes 37636
